TPU v7x, 32 devices: a whole 2x2x4 slice. The times are simulated.
32 devices in a mesh: dp: 8 (over y, x, core), tensor: 4 (over z).
Axes of the slice: x: 2, y: 2, z: 4, core: 2. Of those that a mesh axis runs over, the one named last changes fastest.
Arguments:
- tokens: bfloat16 [8192, 2048], P(('dp', 'tensor')), may hold values from -6 to 6
- lengths: int32 [8], P('dp'), may hold values from 513 to 1024, as said below
- routes: int32 [8192, 4], P('dp'), may hold values from 0 to 7, all different within a row; in each aligned block of 1024 rows (0 to 1023, 1024 to 2047, ...) at most 768 rows name the same one
- cotangent: bfloat16 [8192, 2048], P(('dp', 'tensor')), may hold values from -6 to 6
- norm_one: bfloat16 [2048], replicated, may hold values from 0.5 to 1.5
- qkv_weight: bfloat16 [2048, 3, 2048], P(None, None, 'tensor'), may hold values from -0.125 to 0.125
- qkv_bias: bfloat16 [3, 2048], P(None, 'tensor'), may hold values from -0.59765625 to 0.59765625
- out_weight: bfloat16 [2048, 2048], P('tensor'), may hold values from -1.5 to 1.5
- norm_two: bfloat16 [2048], replicated, may hold values from 0.5 to 1.5
- router_weight: bfloat16 [2048, 8], replicated, may hold values from -0.0625 to 0.0625
- expert_in: bfloat16 [8, 2048, 2, 1408], P(None, None, None, 'tensor'), may hold values from -0.125 to 0.125
- expert_out: bfloat16 [8, 1408, 2048], P(None, 'tensor'), may hold values from -0.625 to 0.625
- shared_in: bfloat16 [2048, 2, 5632], P(None, None, 'tensor'), may hold values from -0.125 to 0.125
- shared_out: bfloat16 [5632, 2048], P('tensor'), may hold values from -0.15625 to 0.15625
- shared_gate: bfloat16 [2048], replicated, may hold values from -0.125 to 0.125
Outputs:
- output: bfloat16 [8192, 2048], P(('dp', 'tensor'))
- input_grad: float32 [8192, 2048], P(('dp', 'tensor'))
- norm_one_grad: float32 [2048], replicated
- qkv_weight_grad: float32 [2048, 3, 2048], P('dp', None, 'tensor')
- qkv_bias_grad: float32 [3, 2048], P(None, 'tensor')
- out_weight_grad: float32 [2048, 2048], P('tensor', 'dp')
- norm_two_grad: float32 [2048], replicated
- router_grad: float32 [2048, 8], replicated
- expert_in_grad: float32 [8, 2048, 2, 1408], P(None, 'dp', None, 'tensor')
- expert_out_grad: float32 [8, 1408, 2048], P(None, 'tensor', 'dp')
- shared_in_grad: float32 [2048, 2, 5632], P('dp', None, 'tensor')
- shared_out_grad: float32 [5632, 2048], P('tensor', 'dp')
- shared_gate_grad: float32 [2048], replicated
Inputs may be any that keep to these rules, and one draw needn't show every extreme that they name: Row r holds one sequence in its first lengths[r] slots; the other slots are padding. In every draw some row is full. `routes`: the 4 experts of a slot are all different. Within each packed row (aligned blocks of 1024 slots) no expert is named more than 768 times; in some row some expert is named exactly 768 times.
All inputs are finite; a program needn't handle non-finite values.
Results may differ from a plain program's by a relative error of at most 0.018.
The roundings to bfloat16 on the way count: a program that leaves them out, or rounds other values in their place, can miss the bound.
Values may be sent and summed in bfloat16 or wider, within the bound.
A program may use at most 384 MiB of HBM per device.

v0:
```python
import jax
import jax.numpy as jnp
from jax import lax
from jax.sharding import PartitionSpec as P

HEAD_DIM = 128


epsilon = 1e-06
theta_base = 1000000.0
precise = lax.Precision.HIGHEST


def rotary_tables(row_count, head_width):
    half_index = jnp.arange(head_width // 2).astype(jnp.float32)
    frequency = theta_base ** (-2.0 * half_index / head_width)
    angles = jnp.arange(row_count).astype(jnp.float32)[:, None] * frequency[None, :]
    angles = jnp.concatenate([angles, angles], axis=-1)
    return (jnp.cos(angles)[:, None, :], jnp.sin(angles)[:, None, :])


def rotary(values, cos_table, sine_table):
    half_width = values.shape[-1] // 2
    turned = jnp.concatenate([-values[..., half_width:], values[..., :half_width]], axis=-1)
    return values * cos_table + turned * sine_table


def rotary_back(grads_in, cos_table, sine_table):
    half_width = grads_in.shape[-1] // 2
    scaled = grads_in * sine_table
    return grads_in * cos_table + jnp.concatenate(
        [scaled[..., half_width:], -scaled[..., :half_width]], axis=-1
    )


def swiglu_back(gate_up, d_inner):
    gate_part = gate_up[:, 0]
    up_part = gate_up[:, 1]
    gate_sig = jax.nn.sigmoid(gate_part)
    d_gate = d_inner * up_part * gate_sig * (1.0 + gate_part * (1.0 - gate_sig))
    d_up = d_inner * gate_part * gate_sig
    return jnp.stack([d_gate, d_up], axis=1)


def norm_back(d_normed, unit_rows, inverse, gain_vector):
    d_unit = d_normed * gain_vector
    return inverse * (d_unit - unit_rows * jnp.mean(d_unit * unit_rows, axis=-1, keepdims=True))


def expert_forward(row_data, in_weight, down_weight):
    in_flat = in_weight.reshape(in_weight.shape[0], -1)
    gate_up = jnp.dot(row_data, in_flat, preferred_element_type=jnp.float32).reshape(
        row_data.shape[0], 2, -1
    )
    inner_act = (jax.nn.silu(gate_up[:, 0]) * gate_up[:, 1]).astype(jnp.bfloat16)
    result = jnp.dot(inner_act, down_weight, preferred_element_type=jnp.float32)
    return (gate_up, inner_act, result)


def expert_backward(row_data, d_rows, scale_rows, gate_up, inner_act, in_weight, down_weight):
    d_result = (scale_rows[:, None] * d_rows).astype(jnp.bfloat16)
    down_grad = jnp.einsum("nf,nd->fd", inner_act, d_result, preferred_element_type=jnp.float32)
    d_inner = jnp.einsum("nd,fd->nf", d_result, down_weight, preferred_element_type=jnp.float32)
    projected = jnp.einsum("nd,fd->nf", d_rows, down_weight, preferred_element_type=jnp.float32)
    d_scale = jnp.sum(projected * inner_act.astype(jnp.float32), axis=-1)
    d_gate_up = swiglu_back(gate_up, d_inner).reshape(row_data.shape[0], -1).astype(jnp.bfloat16)
    in_flat = in_weight.reshape(in_weight.shape[0], -1)
    in_grad = jnp.einsum("nd,nc->dc", row_data, d_gate_up, preferred_element_type=jnp.float32)
    d_rows_in = jnp.einsum("nc,dc->nd", d_gate_up, in_flat, preferred_element_type=jnp.float32)
    return (in_grad.reshape(in_weight.shape), down_grad, d_scale, d_rows_in)


def on_device(
    tokens,
    lengths,
    routes,
    cotangent,
    norm_one,
    qkv_weight,
    qkv_bias,
    out_weight,
    norm_two,
    router_weight,
    expert_in,
    expert_out,
    shared_in,
    shared_out,
    shared_gate,
):
    own_rows = tokens.shape[0]
    slot_count = routes.shape[0]
    model_width = tokens.shape[1]
    qkv_cols = qkv_weight.shape[2]
    local_heads = qkv_cols // HEAD_DIM
    experts_total = router_weight.shape[1]
    length = lengths[0]
    tensor_index = lax.axis_index("tensor")
    first_row = tensor_index * own_rows
    slot_index = jnp.arange(slot_count)
    live_own = (first_row + jnp.arange(own_rows) < length).astype(jnp.float32)[:, None]
    block_rows = min(512, slot_count)
    scale = HEAD_DIM ** (-0.5)
    tokens_f = tokens.astype(jnp.float32)
    gain_one = norm_one.astype(jnp.float32)
    gain_two = norm_two.astype(jnp.float32)
    inv_one = lax.rsqrt(jnp.mean(tokens_f * tokens_f, axis=-1, keepdims=True) + epsilon)
    unit_one = tokens_f * inv_one
    normed_one = lax.all_gather(
        (unit_one * gain_one).astype(jnp.bfloat16), "tensor", axis=0, tiled=True
    )
    qkv_flat_weight = qkv_weight.reshape(model_width, 3 * qkv_cols)
    qkv_all = jnp.dot(normed_one, qkv_flat_weight, preferred_element_type=jnp.float32)
    qkv_all = qkv_all.reshape(slot_count, 3, qkv_cols) + qkv_bias.astype(jnp.float32)
    cos_table, sine_table = rotary_tables(slot_count, HEAD_DIM)
    query_heads = rotary(
        qkv_all[:, 0].reshape(slot_count, local_heads, HEAD_DIM), cos_table, sine_table
    ).astype(jnp.bfloat16)
    key_heads = rotary(
        qkv_all[:, 1].reshape(slot_count, local_heads, HEAD_DIM), cos_table, sine_table
    ).astype(jnp.bfloat16)
    value_heads = qkv_all[:, 2].reshape(slot_count, local_heads, HEAD_DIM).astype(jnp.bfloat16)

    def block_scores(block_start, block_end):
        raw_scores = (
            jnp.einsum(
                "qhd,khd->hqk",
                query_heads[block_start:block_end],
                key_heads[:block_end],
                preferred_element_type=jnp.float32,
            )
            * scale
        )
        allowed = (slot_index[None, :block_end] <= slot_index[block_start:block_end, None]) & (
            slot_index[None, :block_end] < length
        )
        return jnp.where(allowed[None], raw_scores, -1000000000.0)

    mixed_parts = []
    lse_parts = []
    for block_start in range(0, slot_count, block_rows):
        block_end = block_start + block_rows
        raw_scores = block_scores(block_start, block_end)
        row_peak = jnp.max(raw_scores, axis=-1, keepdims=True)
        exp_terms = jnp.exp(raw_scores - row_peak)
        summed = jnp.sum(exp_terms, axis=-1, keepdims=True)
        probs_low = (exp_terms / summed).astype(jnp.bfloat16)
        mixed_parts.append(
            jnp.einsum(
                "hqk,khd->qhd",
                probs_low,
                value_heads[:block_end],
                preferred_element_type=jnp.float32,
            )
        )
        lse_parts.append(row_peak + jnp.log(summed))
    mixed = jnp.concatenate(mixed_parts, axis=0).reshape(slot_count, qkv_cols).astype(jnp.bfloat16)
    branch_one = lax.psum_scatter(
        jnp.dot(mixed, out_weight, preferred_element_type=jnp.float32),
        "tensor",
        scatter_dimension=0,
        tiled=True,
    )
    hidden = tokens_f + live_own * branch_one
    inv_two = lax.rsqrt(jnp.mean(hidden * hidden, axis=-1, keepdims=True) + epsilon)
    unit_two = hidden * inv_two
    normed_two = lax.all_gather(
        (unit_two * gain_two).astype(jnp.bfloat16), "tensor", axis=0, tiled=True
    )
    router_probs = jax.nn.softmax(
        jnp.dot(normed_two, router_weight, preferred_element_type=jnp.float32), axis=-1
    )
    picked = jnp.sum(
        (routes[:, :, None] == jnp.arange(experts_total)[None, None, :]).astype(jnp.float32), axis=1
    )
    weights = router_probs * picked
    combined = jnp.zeros((slot_count, model_width), jnp.float32)
    kept_rows = []
    for expert in range(experts_total):
        gate_up, inner_act, result = expert_forward(
            normed_two, expert_in[expert], expert_out[expert]
        )
        combined = combined + weights[:, expert : expert + 1] * result
        kept_rows.append((gate_up, inner_act))
    shared_up, shared_act, shared_result = expert_forward(normed_two, shared_in, shared_out)
    gate_value = jax.nn.sigmoid(
        jnp.dot(normed_two, shared_gate, preferred_element_type=jnp.float32)
    )
    combined = combined + gate_value[:, None] * shared_result
    branch_two = lax.psum_scatter(
        combined.astype(jnp.bfloat16), "tensor", scatter_dimension=0, tiled=True
    ).astype(jnp.float32)
    output = (hidden + live_own * branch_two).astype(jnp.bfloat16)
    grad_out = cotangent.astype(jnp.float32) * live_own
    d_two = lax.all_gather((live_own * grad_out).astype(jnp.bfloat16), "tensor", axis=0, tiled=True)
    shared_in_grad, shared_out_grad, d_shared_scale, d_normed = expert_backward(
        normed_two, d_two, gate_value, shared_up, shared_act, shared_in, shared_out
    )
    d_gate_logit = d_shared_scale * gate_value * (1.0 - gate_value)
    in_grads = []
    out_grads = []
    d_columns = []
    for expert in range(experts_total):
        gate_up, inner_act = kept_rows[expert]
        in_grad, down_grad, d_scale, d_rows_in = expert_backward(
            normed_two,
            d_two,
            weights[:, expert],
            gate_up,
            inner_act,
            expert_in[expert],
            expert_out[expert],
        )
        d_normed = d_normed + d_rows_in
        d_columns.append(d_scale)
        in_grads.append(in_grad)
        out_grads.append(down_grad)
    expert_in_grad = jnp.stack(in_grads, axis=0)
    expert_out_grad = jnp.stack(out_grads, axis=0)
    d_probs = jnp.stack(d_columns, axis=1) * picked
    d_logits = router_probs * (d_probs - jnp.sum(router_probs * d_probs, axis=-1, keepdims=True))
    d_normed = d_normed + jnp.einsum(
        "se,de->sd", d_logits, router_weight.astype(jnp.float32), precision=precise
    )
    d_normed = d_normed + d_gate_logit[:, None] * shared_gate.astype(jnp.float32)[None, :]
    small_cols = jnp.concatenate([d_logits, d_gate_logit[:, None]], axis=1)
    col_sums = jnp.einsum(
        "sc,sd->cd", small_cols, normed_two.astype(jnp.float32), precision=precise
    )
    router_part = col_sums[:experts_total].T
    gate_part = col_sums[experts_total]
    grad_two = lax.psum_scatter(d_normed, "tensor", scatter_dimension=0, tiled=True)
    norm_two_part = jnp.sum(grad_two * unit_two, axis=0)
    grad_hidden = grad_out + norm_back(grad_two, unit_two, inv_two, gain_two)
    d_one = lax.all_gather(
        (live_own * grad_hidden).astype(jnp.bfloat16), "tensor", axis=0, tiled=True
    )
    out_weight_grad = jnp.einsum("sc,sd->cd", mixed, d_one, preferred_element_type=jnp.float32)
    d_mixed = jnp.einsum("sd,cd->sc", d_one, out_weight, preferred_element_type=jnp.float32)
    d_mixed = d_mixed.astype(jnp.bfloat16).reshape(slot_count, local_heads, HEAD_DIM)
    d_query_parts = []
    d_key = jnp.zeros((slot_count, local_heads, HEAD_DIM), jnp.float32)
    d_value = jnp.zeros((slot_count, local_heads, HEAD_DIM), jnp.float32)
    for block_number, block_start in enumerate(range(0, slot_count, block_rows)):
        block_end = block_start + block_rows
        raw_scores = block_scores(block_start, block_end)
        probs_full = jnp.exp(raw_scores - lse_parts[block_number])
        probs_low = probs_full.astype(jnp.bfloat16)
        d_grad_block = d_mixed[block_start:block_end]
        d_probs_att = jnp.einsum(
            "qhd,khd->hqk",
            d_grad_block,
            value_heads[:block_end],
            preferred_element_type=jnp.float32,
        )
        delta_sum = jnp.sum(probs_full * d_probs_att, axis=-1, keepdims=True)
        d_scores = (probs_full * (d_probs_att - delta_sum)).astype(jnp.bfloat16)
        d_query_parts.append(
            jnp.einsum(
                "hqk,khd->qhd", d_scores, key_heads[:block_end], preferred_element_type=jnp.float32
            )
            * scale
        )
        d_key = d_key.at[:block_end].add(
            jnp.einsum(
                "hqk,qhd->khd",
                d_scores,
                query_heads[block_start:block_end],
                preferred_element_type=jnp.float32,
            )
            * scale
        )
        d_value = d_value.at[:block_end].add(
            jnp.einsum("hqk,qhd->khd", probs_low, d_grad_block, preferred_element_type=jnp.float32)
        )
    d_query = jnp.concatenate(d_query_parts, axis=0)
    d_qkv = jnp.stack(
        [
            rotary_back(d_query, cos_table, sine_table).reshape(slot_count, qkv_cols),
            rotary_back(d_key, cos_table, sine_table).reshape(slot_count, qkv_cols),
            d_value.reshape(slot_count, qkv_cols),
        ],
        axis=1,
    ).astype(jnp.bfloat16)
    d_qkv_flat = d_qkv.reshape(slot_count, 3 * qkv_cols)
    qkv_weight_grad = jnp.einsum(
        "sd,sc->dc", normed_one, d_qkv_flat, preferred_element_type=jnp.float32
    )
    qkv_weight_grad = qkv_weight_grad.reshape(model_width, 3, qkv_cols)
    bias_part = jnp.sum(d_qkv.astype(jnp.float32), axis=0)
    grad_one = jnp.einsum(
        "sc,dc->sd", d_qkv_flat, qkv_flat_weight, preferred_element_type=jnp.float32
    )
    grad_one = lax.psum_scatter(
        grad_one.astype(jnp.bfloat16), "tensor", scatter_dimension=0, tiled=True
    ).astype(jnp.float32)
    norm_one_part = jnp.sum(grad_one * unit_one, axis=0)
    input_grad = grad_hidden + norm_back(grad_one, unit_one, inv_one, gain_one)
    column_start = tensor_index * qkv_cols
    zero_index = jnp.zeros((), jnp.int32)
    bias_full = lax.dynamic_update_slice(
        jnp.zeros((3, qkv_cols * lax.axis_size("tensor")), jnp.float32),
        bias_part,
        (zero_index, column_start),
    )
    norm_one_grad, norm_two_grad, router_grad, shared_gate_grad, bias_sum = lax.psum(
        (norm_one_part, norm_two_part, router_part, gate_part, bias_full), ("dp", "tensor")
    )
    qkv_bias_grad = lax.dynamic_slice(bias_sum, (zero_index, column_start), (3, qkv_cols))
    qkv_sum, out_sum, expert_in_sum, expert_out_sum, shared_in_sum, shared_out_sum = (
        lax.psum_scatter(
            qkv_weight_grad.astype(jnp.bfloat16), "dp", scatter_dimension=0, tiled=True
        ).astype(jnp.float32),
        lax.psum_scatter(
            out_weight_grad.astype(jnp.bfloat16), "dp", scatter_dimension=1, tiled=True
        ).astype(jnp.float32),
        lax.psum_scatter(
            expert_in_grad.astype(jnp.bfloat16), "dp", scatter_dimension=1, tiled=True
        ).astype(jnp.float32),
        lax.psum_scatter(
            expert_out_grad.astype(jnp.bfloat16), "dp", scatter_dimension=2, tiled=True
        ).astype(jnp.float32),
        lax.psum_scatter(
            shared_in_grad.astype(jnp.bfloat16), "dp", scatter_dimension=0, tiled=True
        ).astype(jnp.float32),
        lax.psum_scatter(
            shared_out_grad.astype(jnp.bfloat16), "dp", scatter_dimension=1, tiled=True
        ).astype(jnp.float32),
    )
    return (
        output,
        input_grad,
        norm_one_grad,
        qkv_sum,
        qkv_bias_grad,
        out_sum,
        norm_two_grad,
        router_grad,
        expert_in_sum,
        expert_out_sum,
        shared_in_sum,
        shared_out_sum,
        shared_gate_grad,
    )


def solution(mesh):
    in_specs = (
        P(("dp", "tensor"), None),
        P("dp"),
        P("dp", None),
        P(("dp", "tensor"), None),
        P(),
        P(None, None, "tensor"),
        P(None, "tensor"),
        P("tensor", None),
        P(),
        P(),
        P(None, None, None, "tensor"),
        P(None, "tensor", None),
        P(None, None, "tensor"),
        P("tensor", None),
        P(),
    )
    out_specs = (
        P(("dp", "tensor"), None),
        P(("dp", "tensor"), None),
        P(),
        P("dp", None, "tensor"),
        P(None, "tensor"),
        P("tensor", "dp"),
        P(),
        P(),
        P(None, "dp", None, "tensor"),
        P(None, "tensor", "dp"),
        P("dp", None, "tensor"),
        P("tensor", "dp"),
        P(),
    )
    return jax.shard_map(
        on_device, mesh=mesh, in_specs=in_specs, out_specs=out_specs, check_vma=False
    )
```

profile of v0, /device:TPU:0, one launch (start us, length us, event | category | flops | bytes accessed | tf_op | source)
XLA Modules:
  0.0 1672.7 jit_solution(9152987854078074397)
XLA Ops:
  26.3 70.0 %all-gather.5.cloned.1.call-done = bf16[1024,2048]{1,0:T(8,128)(2,1)} async-done(((bf16[256,2048]{1,0:T(8,128)(2,1)}), bf16[1024,2048]{1,0:T(8,128)(2,1)}) %all-gather.5.cloned.1.call-update) | async-done | bytes 4194320 | tf_op jit(solution)/shard_map/all_gather | solution.py:108
  140.6 142.5 %reduce-scatter.11.cloned.1.call-done = f32[256,2048]{1,0:T(8,128)} async-done(((f32[1024,2048]{1,0:T(8,128)}), f32[256,2048]{1,0:T(8,128)}) %reduce-scatter.11.cloned.1.call-update) | async-done | bytes 2097168 | tf_op jit(solution)/shard_map/reduce_scatter | solution.py:157
  290.4 11.4 copy.161
  301.8 15.1 copy.107
  317.5 16.4 fusion.447
  334.0 36.8 %all-gather.7.cloned.1.call-done = bf16[1024,2048]{1,0:T(8,128)(2,1)} async-done(((bf16[256,2048]{1,0:T(8,128)(2,1)}), bf16[1024,2048]{1,0:T(8,128)(2,1)}) %all-gather.7.cloned.1.call-update) | async-done | bytes 4194320 | tf_op jit(solution)/shard_map/all_gather | solution.py:166
  417.7 34.4 %all-gather.9.cloned.1.call-done = bf16[1024,2048]{1,0:T(8,128)(2,1)} async-done(((bf16[256,2048]{1,0:T(8,128)(2,1)}), bf16[1024,2048]{1,0:T(8,128)(2,1)}) %all-gather.9.cloned.1.call-update) | async-done | bytes 4194320 | tf_op jit(solution)/shard_map/all_gather | solution.py:194
  472.4 17.7 %fusion.46 = f32[1024,2,1408]{2,0,1:T(8,128)S(1)} fusion(bf16[2,1408,2048]{2,1,0:T(8,128)(2,1)} %bitcast.918, bf16[1024,2048]{1,0:T(8,128)(2,1)} %all-gather.7.cloned.1.call-done), kind=kOutput, calls=%fused_computation.74 | convolution fusion | flops 11811160064 | bytes 27262976 | tf_op jit(solution)/shard_map/dot_general | solution.py:52
  596.4 12.7 multiply_bitcast_fusion.1
  609.1 38.0 %fusion.19 = f32[1024,2048]{1,0:T(8,128)} fusion(f32[1024,2048]{1,0:T(8,128)} %fusion.501, f32[1024,2048]{1,0:T(8,128)} %fusion.500, f32[1024,2048]{1,0:T(8,128)} %fusion.499, f32[1024,2048]{1,0:T(8,128)} %fusion.498, f32[1024,2048]{1,0:T(8,128)} %fusion.497, f32[1024,2048]{1,0:T(8,128)} %fusion.496, f32[1024,2048]{1,0:T(8,128)} %fusion.495, ...), kind=kOutput, calls=%fused_computation.32 | convolution fusion | flops 11837112320 | bytes 101199872 | tf_op jit(solution)/shard_map/nc,dc->nd/dot_general | solution.py:69
  698.1 29.5 %add_convert_fusion = bf16[1024,2048]{1,0:T(8,128)(2,1)} fusion(f32[1024,2048]{1,0:T(8,128)} %fusion.319, f32[1024,2048]{1,0:T(8,128)} %fusion.323, f32[1024,2048]{1,0:T(8,128)} %fusion.327, f32[1024,2048]{1,0:T(8,128)} %fusion.331, f32[1024,2048]{1,0:T(8,128)} %fusion.335, f32[1024,2048]{1,0:T(8,128)} %fusion.339, f32[1024,2048]{1,0:T(8,128)} %fusion.343, ...), kind=kOutput, calls=%fused_computation.36 | convolution fusion | flops 5943328768 | bytes 79990784 | tf_op jit(solution)/shard_map/dot_general | solution.py:56
  727.7 62.7 %reduce-scatter.15.cloned.1.call-done = f32[256,2048]{1,0:T(8,128)} async-done(((f32[1024,2048]{1,0:T(8,128)}), f32[256,2048]{1,0:T(8,128)}) %reduce-scatter.15.cloned.1.call-update) | async-done | bytes 2097168 | tf_op jit(solution)/shard_map/reduce_scatter | solution.py:231
  793.7 76.8 %reduce-scatter.13.cloned.1.call-done = bf16[256,2048]{1,0:T(8,128)(2,1)} async-done(((bf16[1024,2048]{1,0:T(8,128)(2,1)}), bf16[256,2048]{1,0:T(8,128)(2,1)}) %reduce-scatter.13.cloned.1.call-update) | async-done | bytes 1048592 | tf_op jit(solution)/shard_map/reduce_scatter | solution.py:189
  876.4 10.7 convolution_convert_fusion.1
  929.1 19.2 %convolution_convert_fusion = bf16[2048,2,1408]{2,0,1:T(8,128)(2,1)} fusion(bf16[1024,2,1408]{0,2,1:T(8,128)(2,1)} %copy.137, bf16[1024,2048]{1,0:T(8,128)(2,1)} %all-gather.7.cloned.1.call-done), kind=kOutput, calls=%fused_computation.12 | convolution fusion | flops 11816927232 | bytes 21495808 | tf_op jit(solution)/shard_map/nd,nc->dc/dot_general | solution.py:68
  1029.0 12.0 bitcast_convert_fusion
  1045.8 11.5 convolution_convert_fusion.2
  1112.7 86.9 %reduce-scatter.27.cloned.1.call-done = bf16[256,2,1408]{2,0,1:T(8,128)(2,1)} async-done(((bf16[2048,2,1408]{2,0,1:T(8,128)(2,1)}), bf16[256,2,1408]{2,0,1:T(8,128)(2,1)}) %reduce-scatter.27.cloned.1.call-update) | async-done | bytes 1441808 | tf_op jit(solution)/shard_map/reduce_scatter | solution.py:322
  1204.1 40.1 %reduce-scatter.21.cloned.1.call-done = bf16[512,256]{1,0:T(8,128)(2,1)} async-done(((bf16[512,2048]{1,0:T(8,128)(2,1)}), bf16[512,256]{1,0:T(8,128)(2,1)}) %reduce-scatter.21.cloned.1.call-update) | async-done | bytes 262160 | tf_op jit(solution)/shard_map/reduce_scatter | solution.py:313
  1246.0 77.8 %reduce-scatter.17.cloned.1.call-done = bf16[256,2048]{1,0:T(8,128)(2,1)} async-done(((bf16[1024,2048]{1,0:T(8,128)(2,1)}), bf16[256,2048]{1,0:T(8,128)(2,1)}) %reduce-scatter.17.cloned.1.call-update) | async-done | bytes 1048592 | tf_op jit(solution)/shard_map/reduce_scatter | solution.py:293
  1326.0 42.2 %all-reduce.2 = (f32[2048]{0:T(1024)}, f32[3,2048]{1,0:T(4,128)S(1)}, f32[2048]{0:T(1024)}, f32[2048]{0:T(1024)}) all-reduce(f32[2048]{0:T(1024)S(1)} %get-tuple-element.118, f32[3,2048]{1,0:T(4,128)S(1)} %constant_dynamic-update-slice_fusion, f32[2048]{0:T(1024)S(1)} %copy-done.152, ...), channel_id=1, replica_groups=mesh['dp'=8,'tensor'=4] {'dp','tensor'}, use_global_device_ids=true, to_apply=%region_28.29 | all-reduce | flops 12288 | bytes 98304 | tf_op jit(solution)/shard_map/psum | solution.py:305
  1372.6 17.6 %reduce-scatter.19.cloned.1.call-done = bf16[256,3,512]{2,0,1:T(8,128)(2,1)} async-done(((bf16[2048,3,512]{2,0,1:T(8,128)(2,1)}), bf16[256,3,512]{2,0,1:T(8,128)(2,1)}) %reduce-scatter.19.cloned.1.call-update) | async-done | bytes 786448 | tf_op jit(solution)/shard_map/reduce_scatter | solution.py:310
  1392.6 147.4 %reduce-scatter.23.cloned.1.call-done = bf16[8,256,2,352]{1,3,2,0:T(8,128)(2,1)} async-done(((bf16[8,2048,2,352]{1,3,2,0:T(8,128)(2,1)}), bf16[8,256,2,352]{1,3,2,0:T(8,128)(2,1)}) %reduce-scatter.23.cloned.1.call-update) | async-done | bytes 2883600 | tf_op jit(solution)/shard_map/reduce_scatter | solution.py:316
  1545.0 119.5 %all-reduce.5.cloned.1.call-done = f32[2048,8]{0,1:T(8,128)} async-done(((f32[2048,8]{0,1:T(8,128)}), f32[2048,8]{0,1:T(8,128)}) %all-reduce.5.cloned.1.call-update) | async-done | bytes 65552 | tf_op jit(solution)/shard_map/psum | solution.py:305
  (604 shorter events, 506.7 us)
Async XLA Ops:
  7.2 89.1 %all-gather.5.cloned.1.call-start = ((), (), s32[]{:S(2)}) async-start(), calls=%async_computation.10 | async-start | bytes 5242880 | tf_op jit(solution)/shard_map/all_gather | solution.py:108
  12.7 270.4 %reduce-scatter.11.cloned.1.call-start = ((), (), s32[]{:S(2)}) async-start(), calls=%async_computation.11 | async-start | bytes 10485760 | tf_op jit(solution)/shard_map/reduce_scatter | solution.py:157
  139.9 143.2 %copy-start.10 = (bf16[256,2048]{1,0:T(8,128)(2,1)S(1)}, bf16[256,2048]{1,0:T(8,128)(2,1)}, u32[]{:S(2)}) copy-start(bf16[256,2048]{1,0:T(8,128)(2,1)} %param.27) | copy-start | bytes 3145732
  139.9 230.9 %all-gather.7.cloned.1.call-start = ((), (), s32[]{:S(2)}) async-start(), calls=%async_computation.12 | async-start | bytes 5242880 | tf_op jit(solution)/shard_map/all_gather | solution.py:166
  140.6 146.0 %copy-start.129 = (f32[2048]{0:T(1024)}, f32[2048]{0:T(1024)S(1)}, u32[]{:S(2)}) copy-start(f32[2048]{0:T(1024)S(1)} %convert_element_type.408) | copy-start | bytes 24580
  140.6 146.0 %copy-start.164 = (f32[256]{0:T(256)}, f32[256]{0:T(256)S(1)}, u32[]{:S(2)}) copy-start(f32[256]{0:T(256)S(1)} %compare_convert_fusion) | copy-start | bytes 3076
  289.1 163.0 %all-gather.9.cloned.1.call-start = ((), (), s32[]{:S(2)}) async-start(), calls=%async_computation.14 | async-start | bytes 5242880 | tf_op jit(solution)/shard_map/all_gather | solution.py:194
  334.0 456.4 %reduce-scatter.15.cloned.1.call-start = ((), (), s32[]{:S(2)}) async-start(), calls=%async_computation.15 | async-start | bytes 10485760 | tf_op jit(solution)/shard_map/reduce_scatter | solution.py:231
  647.1 223.4 %reduce-scatter.13.cloned.1.call-start = ((), (), s32[]{:S(2)}) async-start(), calls=%async_computation.13 | async-start | bytes 5242880 | tf_op jit(solution)/shard_map/reduce_scatter | solution.py:189
  727.6 143.0 %copy-start.28 = (bf16[256,2048]{1,0:T(8,128)(2,1)S(1)}, bf16[256,2048]{1,0:T(8,128)(2,1)}, u32[]{:S(2)}) copy-start(bf16[256,2048]{1,0:T(8,128)(2,1)} %param.30) | copy-start | bytes 3145732
  727.6 142.9 %copy-start.165 = (f32[256]{0:T(256)S(1)}, f32[256]{0:T(256)}, u32[]{:S(2)}) copy-start(f32[256]{0:T(256)} %copy-done.164) | copy-start | bytes 3076
  727.6 230.2 %all-gather.11.cloned.1.call-start = ((), (), s32[]{:S(2)}) async-start(), calls=%async_computation.16 | async-start | bytes 5242880 | tf_op jit(solution)/shard_map/all_gather | solution.py:234
  876.3 226.7 %reduce-scatter.29.cloned.1.call-start = ((), (), s32[]{:S(2)}) async-start(), calls=%async_computation.24 | async-start | bytes 6488064 | tf_op jit(solution)/shard_map/reduce_scatter | solution.py:325
  887.2 222.3 %reduce-scatter.25.cloned.1.call-start = ((), (), s32[]{:S(2)}) async-start(), calls=%async_computation.22 | async-start | bytes 12976128 | tf_op jit(solution)/shard_map/reduce_scatter | solution.py:319
  914.4 285.3 %reduce-scatter.27.cloned.1.call-start = ((), (), s32[]{:S(2)}) async-start(), calls=%async_computation.23 | async-start | bytes 12976128 | tf_op jit(solution)/shard_map/reduce_scatter | solution.py:322
  948.3 295.9 %reduce-scatter.21.cloned.1.call-start = ((), (), s32[]{:S(2)}) async-start(), calls=%async_computation.19 | async-start | bytes 2359296 | tf_op jit(solution)/shard_map/reduce_scatter | solution.py:313
  989.6 334.3 %reduce-scatter.17.cloned.1.call-start = ((), (), s32[]{:S(2)}) async-start(), calls=%async_computation.17 | async-start | bytes 5242880 | tf_op jit(solution)/shard_map/reduce_scatter | solution.py:293
  1041.0 349.1 %reduce-scatter.19.cloned.1.call-start = ((), (), s32[]{:S(2)}) async-start(), calls=%async_computation.18 | async-start | bytes 7077888 | tf_op jit(solution)/shard_map/reduce_scatter | solution.py:310
  1057.4 482.6 %reduce-scatter.23.cloned.1.call-start = ((), (), s32[]{:S(2)}) async-start(), calls=%async_computation.21 | async-start | bytes 25952256 | tf_op jit(solution)/shard_map/reduce_scatter | solution.py:316
  1097.7 566.9 %all-reduce.5.cloned.1.call-start = ((), (), s32[]{:S(2)}) async-start(), calls=%async_computation.20 | async-start | bytes 131072 | tf_op jit(solution)/shard_map/psum | solution.py:305
  1112.7 211.1 %copy-start.11 = (bf16[256,2048]{1,0:T(8,128)(2,1)S(1)}, bf16[256,2048]{1,0:T(8,128)(2,1)}, u32[]{:S(2)}) copy-start(bf16[256,2048]{1,0:T(8,128)(2,1)} %param.27) | copy-start | bytes 3145732
  1112.7 211.1 %copy-start.127 = (f32[2048]{0:T(1024)S(1)}, f32[2048]{0:T(1024)}, u32[]{:S(2)}) copy-start(f32[2048]{0:T(1024)} %copy-done.126) | copy-start | bytes 24580
  1112.7 211.1 %copy-start.157 = (f32[256]{0:T(256)S(1)}, f32[256]{0:T(256)}, u32[]{:S(2)}) copy-start(f32[256]{0:T(256)} %copy-done.156) | copy-start | bytes 3076
  1112.7 213.2 %copy-start.152 = (f32[2048]{0:T(1024)S(1)}, f32[2048]{0:T(1024)}, u32[]{:S(2)}) copy-start(f32[2048]{0:T(1024)} %get-tuple-element.116) | copy-start | bytes 24580
  (184 other events, 2080.9 us)
Sparse Core Ops, SparseCore 0:
  12.8 83.4 all-gather.4
  140.0 142.9 reduce-scatter.10
  289.3 81.4 all-gather.6
  372.8 79.2 all-gather.8
  647.3 143.0 reduce-scatter.14
  793.0 77.4 reduce-scatter.12
  876.5 81.2 all-gather.10
  961.6 57.5 reduce-scatter.28
  1022.7 86.7 reduce-scatter.24
  1112.9 86.7 reduce-scatter.26
  1203.0 41.2 reduce-scatter.20
  1247.1 76.7 reduce-scatter.16
  1327.2 62.8 reduce-scatter.18
  1394.0 145.9 reduce-scatter.22
  1546.9 117.5 all-reduce.4
where the time goes:
time: 1680 us; the launch traced here: 1670 us
  waiting for transfers between devices  920 us (55%)
  matrix products  451 us (27%)
  local copies, waits for them, and re-layouts  148 us (9%)
  other arithmetic  92.2 us (5%)
  blocking collectives  42.2 us (3%)
  between operations  17.1 us (1%)
    reduce_scatter x1, waiting for transfers between devices, on_device(): lax.psum_scatter(expert_in_grad.astype(jnp.bfloat16), 'dp', scatter_dimen...  147 us
    reduce_scatter x1, waiting for transfers between devices, on_device(): lax.psum_scatter(jnp.dot(mixed, out_weight, preferred_element_type=jnp.fl...  142 us
    psum x1, waiting for transfers between devices, on_device(): lax.psum((norm_one_part, norm_two_part, router_part, gate_part, bias_full...  120 us
    reduce_scatter x1, waiting for transfers between devices, on_device(): lax.psum_scatter(shared_in_grad.astype(jnp.bfloat16), 'dp', scatter_dimen...  86.9 us
    dot_general x9, matrix products, expert_backward(): jnp.einsum('nc,dc->nd', d_gate_up, in_flat, preferred_element_type=jnp.fl...  83.9 us
    dot_general x9, matrix products, expert_forward(): result = jnp.dot(inner_act, down_weight, preferred_element_type=jnp.float32)  79.8 us
    reduce_scatter x1, waiting for transfers between devices, on_device(): lax.psum_scatter(grad_one.astype(jnp.bfloat16), 'tensor', scatter_dimensi...  77.8 us
    reduce_scatter x1, waiting for transfers between devices, on_device(): lax.psum_scatter(combined.astype(jnp.bfloat16), 'tensor', scatter_dimensi...  76.8 us
  transfers between devices with their start and end apart: 15, of which 14 were waited for; matrix products, arithmetic and copies ran while one was open for 25% of the time, Pallas kernels for 0%

commit v1 on v0

v1 whole, which is shorter than its diff:
```python
import functools

import jax
import jax.numpy as jnp
from jax import lax
from jax.experimental import pallas as pl
from jax.experimental.pallas import tpu as pltpu
from jax.sharding import PartitionSpec as P

HEAD_DIM = 128
MESH = pl.DeviceIdType.MESH
LA, LB, LC = 1, 2, 2
MIB = 2**20


epsilon = 1e-06
theta_base = 1000000.0
NT = (((1,), (1,)), ((), ()))
TN = (((0,), (0,)), ((), ()))


def rotary_tables(row_count, head_width):
    half_index = jnp.arange(head_width // 2).astype(jnp.float32)
    frequency = theta_base ** (-2.0 * half_index / head_width)
    angles = jnp.arange(row_count).astype(jnp.float32)[:, None] * frequency[None, :]
    angles = jnp.concatenate([angles, angles], axis=-1)
    return (jnp.cos(angles)[:, None, :], jnp.sin(angles)[:, None, :])


def rotary(values, cos_table, sine_table):
    half_width = values.shape[-1] // 2
    turned = jnp.concatenate([-values[..., half_width:], values[..., :half_width]], axis=-1)
    return values * cos_table + turned * sine_table


def rotary_back(grads_in, cos_table, sine_table):
    half_width = grads_in.shape[-1] // 2
    scaled = grads_in * sine_table
    return grads_in * cos_table + jnp.concatenate(
        [scaled[..., half_width:], -scaled[..., :half_width]], axis=-1
    )


def norm_back(d_normed, unit_rows, inverse, gain_vector):
    d_unit = d_normed * gain_vector
    return inverse * (d_unit - unit_rows * jnp.mean(d_unit * unit_rows, axis=-1, keepdims=True))


def rs_body(nc, a_ref, b_ref, o_ref, own, sa, ra, kt, s1, r1, ku, s2, r2, sem_sa, sem_ra, sem_s1, sem_r1, sem_s2, sem_r2):
    i = pl.program_id(0)
    r, w = o_ref.shape
    hr = r // 2
    dp = lax.axis_index("dp")
    k = dp % 2
    x = (dp // 2) % 2
    y = dp // 4
    core_peer = y * 4 + x * 2 + (1 - k)
    x_peer = y * 4 + (1 - x) * 2 + k
    y_peer = (1 - y) * 4 + x * 2 + k

    def copy_a(c):
        return pltpu.make_async_remote_copy(
            src_ref=sa.at[c % 2], dst_ref=ra.at[c % 3], send_sem=sem_sa.at[c % 2], recv_sem=sem_ra.at[c % 3],
            device_id={"dp": core_peer}, device_id_type=MESH)

    def copy_1(c, half):
        return pltpu.make_async_remote_copy(
            src_ref=s1.at[c % 3, half], dst_ref=r1.at[c % 6, half], send_sem=sem_s1.at[c % 3, half],
            recv_sem=sem_r1.at[c % 6, half], device_id={"dp": y_peer if half else x_peer}, device_id_type=MESH)

    def copy_2(c, half):
        return pltpu.make_async_remote_copy(
            src_ref=s2.at[c % 2, half], dst_ref=r2.at[c % 6, half], send_sem=sem_s2.at[c % 2, half],
            recv_sem=sem_r2.at[c % 6, half], device_id={"dp": x_peer if half else y_peer}, device_id_type=MESH)

    @pl.when(i == 0)
    def _():
        barrier = pltpu.get_barrier_semaphore()
        for peer in (core_peer, x_peer, y_peer):
            pl.semaphore_signal(barrier, inc=1, device_id={"dp": peer}, device_id_type=MESH)
        pl.semaphore_wait(barrier, 3)

    @pl.when(jnp.logical_and(i >= LA + 3, i < nc + LA + 3))
    def _():
        copy_1(i - LA - 3, 0).wait_send()
        copy_1(i - LA - 3, 1).wait_send()

    @pl.when(jnp.logical_and(i >= LA, i < nc + LA))
    def _():
        c = i - LA
        copy_a(c).wait_recv()
        for half in range(2):
            rows = slice(half * hr, half * hr + hr)
            keep, other = (1, 2) if half else (2, 1)
            def total(role):
                return own[c % 2, role, rows, :] + ra[c % 3, role, rows, :].astype(jnp.float32)
            s1[c % 3, half, 0] = total(other).astype(jnp.bfloat16)
            s1[c % 3, half, 1] = total(3).astype(jnp.bfloat16)
            copy_1(c, half).start()
            kt[c % 3, half, 0] = total(0)
            kt[c % 3, half, 1] = total(keep)

    @pl.when(jnp.logical_and(i >= LA + LB, i < nc + LA + LB))
    def _():
        c = i - LA - LB
        @pl.when(c >= 2)
        def _():
            copy_2(c - 2, 0).wait_send()
            copy_2(c - 2, 1).wait_send()
        for half in range(2):
            copy_1(c, half).wait_recv()
            s2[c % 2, half] = (kt[c % 3, half, 1] + r1[c % 6, half, 1].astype(jnp.float32)).astype(jnp.bfloat16)
            copy_2(c, half).start()
            ku[c % 3, half] = kt[c % 3, half, 0] + r1[c % 6, half, 0].astype(jnp.float32)

    @pl.when(i >= LA + LB + LC)
    def _():
        c = i - LA - LB - LC
        for half in range(2):
            copy_2(c, half).wait_recv()
            o_ref[half * hr:half * hr + hr, :] = ku[c % 3, half] + r2[c % 6, half].astype(jnp.float32)
        @pl.when(c >= nc - 2)
        def _():
            copy_2(c, 0).wait_send()
            copy_2(c, 1).wait_send()

    @pl.when(jnp.logical_and(i >= 2, i < nc + 2))
    def _():
        copy_a(i - 2).wait_send()

    @pl.when(i < nc)
    def _():
        a = a_ref[...]
        targets = (y * 4 + x * 2, y * 4 + (1 - x) * 2, (1 - y) * 4 + x * 2, (1 - y) * 4 + (1 - x) * 2)
        for role in range(4):
            cols = pl.ds(pl.multiple_of((targets[role] + 1 - k) * w, w), w)
            sa[i % 2, role] = jnp.dot(a, b_ref[:, cols], preferred_element_type=jnp.float32).astype(jnp.bfloat16)
        copy_a(i).start()
        for role in range(4):
            cols = pl.ds(pl.multiple_of((targets[role] + k) * w, w), w)
            own[i % 2, role] = jnp.dot(a, b_ref[:, cols], preferred_element_type=jnp.float32)

def weight_grad_scatter_kernel(a, b, r, cid, name):
    R, T = a.shape
    D = b.shape[1]
    w = D // 8
    nc = R // r
    L = LA + LB + LC
    f32, bf = jnp.float32, jnp.bfloat16
    dma = pltpu.SemaphoreType.DMA
    return pl.pallas_call(
        functools.partial(rs_body, nc),
        grid=(nc + L,),
        in_specs=[pl.BlockSpec((r, T), lambda i: (jnp.minimum(i, nc - 1), 0)),
                  pl.BlockSpec((T, D), lambda i: (0, 0), pipeline_mode=pl.Buffered(1))],
        out_specs=pl.BlockSpec((r, w), lambda i: (jnp.maximum(i - L, 0), 0)),
        out_shape=jax.ShapeDtypeStruct((R, w), f32),
        scratch_shapes=[
            pltpu.VMEM((2, 4, r, w), f32), pltpu.VMEM((2, 4, r, w), bf), pltpu.VMEM((3, 4, r, w), bf),
            pltpu.VMEM((3, 2, 2, r // 2, w), f32), pltpu.VMEM((3, 2, 2, r // 2, w), bf), pltpu.VMEM((6, 2, 2, r // 2, w), bf),
            pltpu.VMEM((3, 2, r // 2, w), f32), pltpu.VMEM((2, 2, r // 2, w), bf), pltpu.VMEM((6, 2, r // 2, w), bf),
            dma((2,)), dma((3,)), dma((3, 2)), dma((6, 2)), dma((2, 2)), dma((6, 2))],
        compiler_params=pltpu.CompilerParams(vmem_limit_bytes=48 * 2**20, collective_id=cid, has_side_effects=True),
        cost_estimate=pl.CostEstimate(flops=2 * R * T * D, bytes_accessed=2 * R * T + 2 * T * D + 4 * R * w, transcendentals=0),
        name=name)(a, b)


def ffn_body(
    experts, x_ref, d_ref, routes_ref, rw_ref, wi_ref, wd_ref,
    dgu_ref, s_ref, dn_ref, bt_ref, rg_ref,
    dn_acc, bt_acc, probs_ref, w_ref, ds_ref,
):
    c = pl.program_id(0)
    chunks = pl.num_programs(0)
    h = wd_ref.shape[1]
    slots, width = x_ref.shape
    wi = wi_ref.at[0]
    wd = wd_ref.at[0]

    def picked():
        expert = lax.broadcasted_iota(jnp.int32, (experts, slots), 0)
        hit = jnp.zeros((experts, slots), jnp.float32)
        for j in range(routes_ref.shape[0]):
            hit = hit + jnp.where(routes_ref[j : j + 1, :] == expert, 1.0, 0.0)
        return hit

    @pl.when(c == 0)
    def _():
        logits = lax.dot_general(rw_ref[...], x_ref[...], NT, preferred_element_type=jnp.float32)
        raised = jnp.exp(logits[:experts] - jnp.max(logits[:experts], axis=0, keepdims=True))
        probs = raised / jnp.sum(raised, axis=0, keepdims=True)
        gate = 1.0 / (1.0 + jnp.exp(-logits[experts:]))
        probs_ref[...] = probs
        w_ref[:experts, :] = probs * picked()
        w_ref[experts:, :] = gate
        ds_ref[...] = jnp.zeros_like(ds_ref)
        dn_acc[...] = jnp.zeros_like(dn_acc)
        bt_acc[...] = jnp.zeros_like(bt_acc)

    row = pl.ds(jnp.minimum(c, experts), 1)
    x = x_ref[...]
    g = lax.dot_general(wi[:h], x, NT, preferred_element_type=jnp.float32)
    u = lax.dot_general(wi[h:], x, NT, preferred_element_type=jnp.float32)
    p = lax.dot_general(wd[...], d_ref[...], NT, preferred_element_type=jnp.float32)
    w = w_ref[row, :]
    sg = 1.0 / (1.0 + jnp.exp(-g))
    si = g * sg
    inner = (si * u).astype(jnp.bfloat16).astype(jnp.float32)
    s = (w * inner).astype(jnp.bfloat16)
    s_ref[0] = s
    ds_ref[row, :] += jnp.sum(p * inner, axis=0, keepdims=True)
    di = w * p
    dg = (di * u * sg * (1.0 + g * (1.0 - sg))).astype(jnp.bfloat16)
    du = (di * si).astype(jnp.bfloat16)
    dgu_ref[0, :h] = dg
    dgu_ref[0, h:] = du
    dgu = jnp.concatenate([dg, du], axis=0)
    block = 512
    for n in range(0, width, block):
        cols = slice(n, n + block)
        dn_acc[:, cols] += lax.dot_general(dgu, wi[:, cols], TN, preferred_element_type=jnp.float32)
        bt_acc[:, cols] += lax.dot_general(s, wd[:, cols], TN, preferred_element_type=jnp.float32)

    @pl.when(c == chunks - 1)
    def _():
        probs = probs_ref[...]
        d_probs = ds_ref[:experts, :] * picked()
        d_logits = probs * (d_probs - jnp.sum(probs * d_probs, axis=0, keepdims=True))
        gate = w_ref[experts:, :]
        d_gate = ds_ref[experts:, :] * gate * (1.0 - gate)
        small = jnp.concatenate([d_logits, d_gate], axis=0)
        high = small.astype(jnp.bfloat16)
        low = (small - high.astype(jnp.float32)).astype(jnp.bfloat16)
        rg_ref[...] = jnp.dot(high, x_ref[...], preferred_element_type=jnp.float32) + jnp.dot(
            low, x_ref[...], preferred_element_type=jnp.float32
        )
        for n in range(0, width, block):
            cols = slice(n, n + block)
            extra = lax.dot_general(high, rw_ref[:, cols], TN, preferred_element_type=jnp.float32)
            extra += lax.dot_general(low, rw_ref[:, cols], TN, preferred_element_type=jnp.float32)
            dn_ref[:, cols] = (dn_acc[:, cols] + extra).astype(dn_ref.dtype)
        bt_ref[...] = bt_acc[...].astype(bt_ref.dtype)


def ffn(x, d_two, routes_t, router_rows, wi, wd, experts):
    chunks, h2, width = wi.shape
    h = h2 // 2
    slots = x.shape[0]
    rows = router_rows.shape[0]
    bf, f32 = jnp.bfloat16, jnp.float32

    def whole(shape):
        return pl.BlockSpec(shape, lambda c: (0,) * len(shape), pipeline_mode=pl.Buffered(1))

    def chunk(shape):
        return pl.BlockSpec((1, *shape), lambda c: (c, 0, 0))

    return pl.pallas_call(
        functools.partial(ffn_body, experts),
        grid=(chunks,),
        in_specs=[
            whole((slots, width)), whole((slots, width)), whole(routes_t.shape), whole((rows, width)),
            chunk((h2, width)), chunk((h, width)),
        ],
        out_specs=[
            chunk((h2, slots)), chunk((h, slots)), whole((slots, width)), whole((slots, width)), whole((rows, width)),
        ],
        out_shape=[
            jax.ShapeDtypeStruct((chunks, h2, slots), bf), jax.ShapeDtypeStruct((chunks, h, slots), bf),
            jax.ShapeDtypeStruct((slots, width), bf), jax.ShapeDtypeStruct((slots, width), bf),
            jax.ShapeDtypeStruct((rows, width), f32),
        ],
        scratch_shapes=[
            pltpu.VMEM((slots, width), f32), pltpu.VMEM((slots, width), f32),
            pltpu.VMEM((experts, slots), f32), pltpu.VMEM((rows, slots), f32), pltpu.VMEM((rows, slots), f32),
        ],
        compiler_params=pltpu.CompilerParams(vmem_limit_bytes=62 * MIB),
        cost_estimate=pl.CostEstimate(
            flops=12 * chunks * h * slots * width, bytes_accessed=10 * chunks * h * width + 16 * slots * width,
            transcendentals=chunks * h * slots,
        ),
        name="ffn",
    )(x, d_two, routes_t, router_rows, wi, wd)


def weight_grad_scatter(a, b, r, cid, name):
    if lax.axis_size("dp") == 8:
        return weight_grad_scatter_kernel(a, b, r, cid, name)
    product = jnp.dot(a, b, preferred_element_type=jnp.float32)
    return lax.psum_scatter(
        product.astype(jnp.bfloat16), "dp", scatter_dimension=1, tiled=True
    ).astype(jnp.float32)


def gather_body(own_ref, out_ref, local_sem, send_sem, recv_sem):
    me = lax.axis_index("tensor")
    size = lax.axis_size("tensor")
    rows = own_ref.shape[0]
    barrier = pltpu.get_barrier_semaphore()
    for step in range(1, size):
        pl.semaphore_signal(
            barrier, inc=1, device_id={"tensor": lax.rem(me + step, size)}, device_id_type=MESH
        )
    pl.semaphore_wait(barrier, size - 1)
    place = pl.ds(pl.multiple_of(me * rows, rows), rows)
    local = pltpu.make_async_copy(own_ref, out_ref.at[place], local_sem)
    local.start()
    copies = []
    for step in range(1, size):
        copies.append(
            pltpu.make_async_remote_copy(
                src_ref=own_ref, dst_ref=out_ref.at[place], send_sem=send_sem.at[step], recv_sem=recv_sem.at[step],
                device_id={"tensor": lax.rem(me + step, size)}, device_id_type=MESH,
            )
        )
        copies[-1].start()
    local.wait()
    for copy in copies:
        copy.wait()


def gather_rows(own, cid):
    size = lax.axis_size("tensor")
    rows, width = own.shape
    return pl.pallas_call(
        gather_body,
        in_specs=[pl.BlockSpec(memory_space=pl.ANY)],
        out_specs=pl.BlockSpec(memory_space=pl.ANY),
        out_shape=jax.ShapeDtypeStruct((rows * size, width), own.dtype),
        scratch_shapes=[
            pltpu.SemaphoreType.DMA, pltpu.SemaphoreType.DMA((size,)), pltpu.SemaphoreType.DMA((size,)),
        ],
        compiler_params=pltpu.CompilerParams(collective_id=cid, has_side_effects=True),
        cost_estimate=pl.CostEstimate(flops=0, bytes_accessed=2 * rows * size * width * 2, transcendentals=0),
        name="gather_rows",
    )(own)


def sums_body(part_ref, dp_ref, all_ref, from_dp, from_tensor, send_dp, recv_dp, send_t, recv_t):
    size_dp = lax.axis_size("dp")
    size_t = lax.axis_size("tensor")
    me_dp = lax.axis_index("dp")
    me_t = lax.axis_index("tensor")
    barrier = pltpu.get_barrier_semaphore()
    for step in range(1, size_dp):
        pl.semaphore_signal(
            barrier, inc=1, device_id={"dp": lax.rem(me_dp + step, size_dp)}, device_id_type=MESH
        )
    for step in range(1, size_t):
        pl.semaphore_signal(
            barrier, inc=1, device_id={"tensor": lax.rem(me_t + step, size_t)}, device_id_type=MESH
        )
    pl.semaphore_wait(barrier, size_dp + size_t - 2)

    def exchange(axis, me, size, source, slots, send, recv):
        copies = []
        for step in range(1, size):
            copies.append(
                pltpu.make_async_remote_copy(
                    src_ref=source, dst_ref=slots.at[step], send_sem=send.at[step], recv_sem=recv.at[step],
                    device_id={axis: lax.rem(me + step, size)}, device_id_type=MESH,
                )
            )
            copies[-1].start()
        total = source[...]
        for step in range(1, size):
            copies[step - 1].wait_recv()
            total = total + slots[step]
        for copy in copies:
            copy.wait_send()
        return total

    dp_ref[...] = exchange("dp", me_dp, size_dp, part_ref, from_dp, send_dp, recv_dp)
    all_ref[...] = exchange("tensor", me_t, size_t, dp_ref, from_tensor, send_t, recv_t)


def small_sums(part, cid):
    size_dp, size_t = lax.axis_size("dp"), lax.axis_size("tensor")
    vmem = pl.BlockSpec(memory_space=pltpu.VMEM)
    dma = pltpu.SemaphoreType.DMA
    return pl.pallas_call(
        sums_body,
        in_specs=[vmem],
        out_specs=[vmem, vmem],
        out_shape=[jax.ShapeDtypeStruct(part.shape, part.dtype)] * 2,
        scratch_shapes=[
            pltpu.VMEM((size_dp, *part.shape), part.dtype), pltpu.VMEM((size_t, *part.shape), part.dtype),
            dma((size_dp,)), dma((size_dp,)), dma((size_t,)), dma((size_t,)),
        ],
        compiler_params=pltpu.CompilerParams(collective_id=cid, has_side_effects=True),
        name="small_sums",
    )(part)


def on_device(
    tokens,
    lengths,
    routes,
    cotangent,
    norm_one,
    qkv_weight,
    qkv_bias,
    out_weight,
    norm_two,
    router_weight,
    expert_in,
    expert_out,
    shared_in,
    shared_out,
    shared_gate,
):
    own_rows = tokens.shape[0]
    slot_count = routes.shape[0]
    model_width = tokens.shape[1]
    qkv_cols = qkv_weight.shape[2]
    local_heads = qkv_cols // HEAD_DIM
    experts_total = router_weight.shape[1]
    eff = expert_in.shape[3]
    shared_chunks = shared_out.shape[0] // eff
    length = lengths[0]
    tensor_index = lax.axis_index("tensor")
    first_row = tensor_index * own_rows
    slot_index = jnp.arange(slot_count)
    live_own = (first_row + jnp.arange(own_rows) < length).astype(jnp.float32)[:, None]
    block_rows = min(512, slot_count)
    scale = HEAD_DIM ** (-0.5)
    tokens_f = tokens.astype(jnp.float32)
    gain_one = norm_one.astype(jnp.float32)
    gain_two = norm_two.astype(jnp.float32)
    inv_one = lax.rsqrt(jnp.mean(tokens_f * tokens_f, axis=-1, keepdims=True) + epsilon)
    unit_one = tokens_f * inv_one
    normed_one = lax.all_gather(
        (unit_one * gain_one).astype(jnp.bfloat16), "tensor", axis=0, tiled=True
    )
    shared_in_t = shared_in.reshape(model_width, 2, shared_chunks, eff).transpose(2, 1, 3, 0)
    wi = jnp.concatenate(
        [
            expert_in.transpose(0, 2, 3, 1).reshape(experts_total, 2 * eff, model_width),
            shared_in_t.reshape(shared_chunks, 2 * eff, model_width),
        ],
        axis=0,
    )
    wd = jnp.concatenate([expert_out, shared_out.reshape(shared_chunks, eff, model_width)], axis=0)
    router_rows = jnp.concatenate(
        [
            router_weight.T,
            shared_gate[None],
            jnp.zeros((16 - (experts_total + 1) % 16, model_width), jnp.bfloat16),
        ],
        axis=0,
    )
    normed_one, wi, wd = lax.optimization_barrier((normed_one, wi, wd))
    qkv_flat_weight = qkv_weight.reshape(model_width, 3 * qkv_cols)
    qkv_all = jnp.dot(normed_one, qkv_flat_weight, preferred_element_type=jnp.float32)
    qkv_all = qkv_all.reshape(slot_count, 3, qkv_cols) + qkv_bias.astype(jnp.float32)
    cos_table, sine_table = rotary_tables(slot_count, HEAD_DIM)
    query_heads = rotary(
        qkv_all[:, 0].reshape(slot_count, local_heads, HEAD_DIM), cos_table, sine_table
    ).astype(jnp.bfloat16)
    key_heads = rotary(
        qkv_all[:, 1].reshape(slot_count, local_heads, HEAD_DIM), cos_table, sine_table
    ).astype(jnp.bfloat16)
    value_heads = qkv_all[:, 2].reshape(slot_count, local_heads, HEAD_DIM).astype(jnp.bfloat16)

    def block_scores(block_start, block_end):
        raw_scores = (
            jnp.einsum(
                "qhd,khd->hqk",
                query_heads[block_start:block_end],
                key_heads[:block_end],
                preferred_element_type=jnp.float32,
            )
            * scale
        )
        allowed = (slot_index[None, :block_end] <= slot_index[block_start:block_end, None]) & (
            slot_index[None, :block_end] < length
        )
        return jnp.where(allowed[None], raw_scores, -1000000000.0)

    mixed_parts = []
    lse_parts = []
    for block_start in range(0, slot_count, block_rows):
        block_end = block_start + block_rows
        raw_scores = block_scores(block_start, block_end)
        row_peak = jnp.max(raw_scores, axis=-1, keepdims=True)
        exp_terms = jnp.exp(raw_scores - row_peak)
        summed = jnp.sum(exp_terms, axis=-1, keepdims=True)
        probs_low = (exp_terms / summed).astype(jnp.bfloat16)
        mixed_parts.append(
            jnp.einsum(
                "hqk,khd->qhd",
                probs_low,
                value_heads[:block_end],
                preferred_element_type=jnp.float32,
            )
        )
        lse_parts.append(row_peak + jnp.log(summed))
    mixed = jnp.concatenate(mixed_parts, axis=0).reshape(slot_count, qkv_cols).astype(jnp.bfloat16)
    branch_partial = jnp.dot(mixed, out_weight, preferred_element_type=jnp.float32)
    branch_one = lax.psum_scatter(
        branch_partial.astype(jnp.bfloat16), "tensor", scatter_dimension=0, tiled=True
    ).astype(jnp.float32)
    grad_out = cotangent.astype(jnp.float32) * live_own
    d_two_own = (live_own * grad_out).astype(jnp.bfloat16)
    d_two_own, _ = lax.optimization_barrier((d_two_own, mixed))
    d_two = gather_rows(d_two_own, 1)
    hidden = tokens_f + live_own * branch_one
    inv_two = lax.rsqrt(jnp.mean(hidden * hidden, axis=-1, keepdims=True) + epsilon)
    unit_two = hidden * inv_two
    normed_two = lax.all_gather(
        (unit_two * gain_two).astype(jnp.bfloat16), "tensor", axis=0, tiled=True
    )
    d_gate_up, scaled_inner, d_normed, combined, router_part = ffn(
        normed_two, d_two, routes.T, router_rows, wi, wd, experts_total
    )
    chunks = experts_total + shared_chunks
    grad_two = lax.psum_scatter(
        d_normed, "tensor", scatter_dimension=0, tiled=True
    ).astype(jnp.float32)
    out_grads = weight_grad_scatter(
        scaled_inner.reshape(chunks * eff, slot_count), d_two, eff, 2, "down_grads"
    )
    norm_two_part = jnp.sum(grad_two * unit_two, axis=0)
    grad_hidden = grad_out + norm_back(grad_two, unit_two, inv_two, gain_two)
    d_one_own, out_grads = lax.optimization_barrier(
        ((live_own * grad_hidden).astype(jnp.bfloat16), out_grads)
    )
    d_one = lax.all_gather(d_one_own, "tensor", axis=0, tiled=True)
    half = chunks // 2
    d_gate_up_a, _ = lax.optimization_barrier((d_gate_up[:half], d_one_own))
    in_grads_a = weight_grad_scatter(
        d_gate_up_a.reshape(half * 2 * eff, slot_count), normed_two, eff, 3, "in_grads_a"
    )
    d_one, in_grads_a, combined = lax.optimization_barrier((d_one, in_grads_a, combined))
    branch_two = lax.psum_scatter(combined, "tensor", scatter_dimension=0, tiled=True).astype(
        jnp.float32
    )
    output = (hidden + live_own * branch_two).astype(jnp.bfloat16)
    d_mixed = jnp.einsum("sd,cd->sc", d_one, out_weight, preferred_element_type=jnp.float32)
    d_mixed = d_mixed.astype(jnp.bfloat16).reshape(slot_count, local_heads, HEAD_DIM)
    d_query_parts = []
    d_key = jnp.zeros((slot_count, local_heads, HEAD_DIM), jnp.float32)
    d_value = jnp.zeros((slot_count, local_heads, HEAD_DIM), jnp.float32)
    for block_number, block_start in enumerate(range(0, slot_count, block_rows)):
        block_end = block_start + block_rows
        raw_scores = block_scores(block_start, block_end)
        probs_full = jnp.exp(raw_scores - lse_parts[block_number])
        probs_low = probs_full.astype(jnp.bfloat16)
        d_grad_block = d_mixed[block_start:block_end]
        d_probs_att = jnp.einsum(
            "qhd,khd->hqk",
            d_grad_block,
            value_heads[:block_end],
            preferred_element_type=jnp.float32,
        )
        delta_sum = jnp.sum(probs_full * d_probs_att, axis=-1, keepdims=True)
        d_scores = (probs_full * (d_probs_att - delta_sum)).astype(jnp.bfloat16)
        d_query_parts.append(
            jnp.einsum(
                "hqk,khd->qhd", d_scores, key_heads[:block_end], preferred_element_type=jnp.float32
            )
            * scale
        )
        d_key = d_key.at[:block_end].add(
            jnp.einsum(
                "hqk,qhd->khd",
                d_scores,
                query_heads[block_start:block_end],
                preferred_element_type=jnp.float32,
            )
            * scale
        )
        d_value = d_value.at[:block_end].add(
            jnp.einsum("hqk,qhd->khd", probs_low, d_grad_block, preferred_element_type=jnp.float32)
        )
    d_query = jnp.concatenate(d_query_parts, axis=0)
    d_qkv = jnp.stack(
        [
            rotary_back(d_query, cos_table, sine_table).reshape(slot_count, qkv_cols),
            rotary_back(d_key, cos_table, sine_table).reshape(slot_count, qkv_cols),
            d_value.reshape(slot_count, qkv_cols),
        ],
        axis=1,
    ).astype(jnp.bfloat16)
    d_qkv_flat = d_qkv.reshape(slot_count, 3 * qkv_cols)
    bias_part = jnp.sum(d_qkv.astype(jnp.float32), axis=0)
    grad_one = jnp.einsum(
        "sc,dc->sd", d_qkv_flat, qkv_flat_weight, preferred_element_type=jnp.float32
    ).astype(jnp.bfloat16)
    grad_one_own = lax.psum_scatter(grad_one, "tensor", scatter_dimension=0, tiled=True)
    d_gate_up_b, _ = lax.optimization_barrier((d_gate_up[half:], grad_one))
    in_grads_b = weight_grad_scatter(
        d_gate_up_b.reshape((chunks - half) * 2 * eff, slot_count), normed_two, eff, 4, "in_grads_b"
    )
    qkv_sum = weight_grad_scatter(d_qkv_flat.T, normed_one, 3 * qkv_cols // 4, 5, "qkv_grads")
    out_sum = weight_grad_scatter(mixed.T, d_one, qkv_cols // 2, 6, "mix_grads")
    grad_one = grad_one_own.astype(jnp.float32)
    norm_one_part = jnp.sum(grad_one * unit_one, axis=0)
    input_grad = grad_hidden + norm_back(grad_one, unit_one, inv_one, gain_one)
    part = jnp.concatenate(
        [
            router_part[: experts_total + 1],
            norm_one_part[None],
            norm_two_part[None],
            jnp.pad(bias_part.reshape(1, 3 * qkv_cols), ((0, 0), (0, model_width - 3 * qkv_cols))),
        ],
        axis=0,
    )
    dp_sums, all_sums = small_sums(part, 7)
    qkv_bias_grad = dp_sums[experts_total + 3, : 3 * qkv_cols].reshape(3, qkv_cols)
    router_grad = all_sums[:experts_total].T
    shared_gate_grad = all_sums[experts_total]
    norm_one_grad = all_sums[experts_total + 1]
    norm_two_grad = all_sums[experts_total + 2]
    own_cols = out_grads.shape[1]
    in_grads = jnp.concatenate([in_grads_a, in_grads_b], axis=0).reshape(chunks, 2, eff, own_cols)
    expert_in_grad = in_grads[:experts_total].transpose(0, 3, 1, 2)
    shared_in_grad = (
        in_grads[experts_total:].transpose(3, 1, 0, 2).reshape(own_cols, 2, shared_chunks * eff)
    )
    expert_out_grad = out_grads[: experts_total * eff].reshape(experts_total, eff, own_cols)
    shared_out_grad = out_grads[experts_total * eff :]
    return (
        output,
        input_grad,
        norm_one_grad,
        qkv_sum.reshape(3, qkv_cols, own_cols).transpose(2, 0, 1),
        qkv_bias_grad,
        out_sum,
        norm_two_grad,
        router_grad,
        expert_in_grad,
        expert_out_grad,
        shared_in_grad,
        shared_out_grad,
        shared_gate_grad,
    )


def solution(mesh):
    in_specs = (
        P(("dp", "tensor"), None),
        P("dp"),
        P("dp", None),
        P(("dp", "tensor"), None),
        P(),
        P(None, None, "tensor"),
        P(None, "tensor"),
        P("tensor", None),
        P(),
        P(),
        P(None, None, None, "tensor"),
        P(None, "tensor", None),
        P(None, None, "tensor"),
        P("tensor", None),
        P(),
    )
    out_specs = (
        P(("dp", "tensor"), None),
        P(("dp", "tensor"), None),
        P(),
        P("dp", None, "tensor"),
        P(None, "tensor"),
        P("tensor", "dp"),
        P(),
        P(),
        P(None, "dp", None, "tensor"),
        P(None, "tensor", "dp"),
        P("dp", None, "tensor"),
        P("tensor", "dp"),
        P(),
    )
    return jax.shard_map(
        on_device, mesh=mesh, in_specs=in_specs, out_specs=out_specs, check_vma=False
    )
```

time: 1680 us -> 1000 us (0.60)
  waiting for transfers between devices: 920 us -> 109 us
  Pallas kernels: 0 us -> 585 us
  matrix products: 451 us -> 57.6 us
  blocking collectives: 42.2 us -> 0 us
    pallas_call x0 -> x8, Pallas kernels: none -> 585 us  [the longest x5 284 us: weight_grad_scatter_kernel(): pl.pallas_call(functools.partial(rs_body, nc), grid=(nc + L,), in_specs=[...]
    reduce_scatter x9 -> x3, waiting for transfers between devices: 593 us -> 79 us  [the longest x1 79 us: on_device(): lax.psum_scatter(branch_partial.astype(jnp.bfloat16), 'tensor', scatter_d...]
    dot_general x69 -> x0, matrix products: 394 us -> none  [the longest x9 83.9 us: expert_backward(): jnp.einsum('nc,dc->nd', d_gate_up, in_flat, preferred_element_type=jnp.fl...]
    psum x1 -> x0, waiting for transfers between devices: 120 us -> none  [on_device(): lax.psum((norm_one_part, norm_two_part, router_part, gate_part, bias_full...]
    all_gather x1, waiting for transfers between devices: 70 us -> 0.02 us  [on_device(): lax.all_gather((unit_one * gain_one).astype(jnp.bfloat16), 'tensor', axis...]
    reduce_scatter x1, waiting for transfers between devices: 62.7 us -> 5.91 us  [on_device(): lax.psum_scatter(d_normed, 'tensor', scatter_dimension=0, tiled=True)]
    concatenate x0 -> x5, other arithmetic: none -> 45.5 us  [the longest x1 24.2 us: on_device(): jnp.concatenate([expert_in.transpose(0, 2, 3, 1).reshape(experts_total, 2...]
    psum x1 -> x0, blocking collectives: 42.2 us -> none  [on_device(): lax.psum((norm_one_part, norm_two_part, router_part, gate_part, bias_full...]
  transfers between devices with their start and end apart: 15 -> 7, of which waited for: 14 -> 3; matrix products, arithmetic and copies ran while one was open for 25% -> 14% of each run, Pallas kernels for 0% -> 44%
where the time goes in v1:
time: 1000 us; the launch traced here: 995 us
  Pallas kernels  585 us (58%)
  local copies, waits for them, and re-layouts  140 us (14%)
  waiting for transfers between devices  109 us (11%)
  other arithmetic  87.6 us (9%)
  matrix products  57.6 us (6%)
  between operations  15.9 us (2%)
    pallas_call x5, Pallas kernels, weight_grad_scatter_kernel(): pl.pallas_call(functools.partial(rs_body, nc), grid=(nc + L,), in_specs=[...  284 us
    pallas_call x1, Pallas kernels, ffn(): pl.pallas_call(functools.partial(ffn_body, experts), grid=(chunks,), in_s...  143 us
    pallas_call x1, Pallas kernels, gather_rows(): pl.pallas_call(gather_body, in_specs=[pl.BlockSpec(memory_space=pl.ANY)],...  129 us
    reduce_scatter x1, waiting for transfers between devices, on_device(): lax.psum_scatter(branch_partial.astype(jnp.bfloat16), 'tensor', scatter_d...  79 us
    unnamed x128, local copies, waits for them, and re-layouts  64.9 us
    pallas_call x1, Pallas kernels, small_sums(): pl.pallas_call(sums_body, in_specs=[vmem], out_specs=[vmem, vmem], out_sh...  29.2 us
    concatenate x1, other arithmetic, on_device(): jnp.concatenate([expert_in.transpose(0, 2, 3, 1).reshape(experts_total, 2...  24.2 us
    all_gather x1, waiting for transfers between devices, on_device(): lax.all_gather((unit_two * gain_two).astype(jnp.bfloat16), 'tensor', axis...  22.8 us
  transfers between devices with their start and end apart: 7, of which 3 were waited for; matrix products, arithmetic and copies ran while one was open for 14% of the time, Pallas kernels for 44%

profile of v1, /device:TPU:0, one launch (start us, length us, event | category | flops | bytes accessed | tf_op | source)
XLA Modules:
  0.0 995.4 jit_solution(3576047836529483032)
XLA Ops:
  12.6 28.8 %copy.55 = bf16[2048,2,1408]{0,2,1:T(8,128)(2,1)} copy(bf16[2048,2,1408]{2,1,0:T(2,128)(2,1)} %param.39) | data formatting | bytes 23068672 | tf_op args[12]
  41.4 10.1 %copy.56 = bf16[4,2,352,2048]{3,2,1,0:T(8,128)(2,1)} copy(bf16[4,2,352,2048]{3,2,0,1:T(8,128)(2,1)} %bitcast.118) | data formatting | bytes 23068672 | tf_op jit(solution)/shard_map/transpose | solution.py:435
  51.5 8.9 copy.57
  65.0 14.3 %pad_maximum_fusion.1.wd_ref = bf16[12,352,2048]{2,1,0:T(8,128)(2,1)} fusion(bf16[4,352,2048]{2,1,0:T(8,128)(2,1)} %bitcast.130, bf16[8,352,2048]{2,1,0:T(8,128)(2,1)} %param.38), kind=kLoop, calls=%fused_computation.1 | loop fusion | flops 8650752 | bytes 34603008 | tf_op jit(solution)/shard_map/concatenate | solution.py:443
  79.3 24.2 %pad_maximum_fusion.wi_ref = bf16[12,704,2048]{2,1,0:T(8,128)(2,1)} fusion(bf16[4,704,2048]{2,1,0:T(8,128)(2,1)} %bitcast.119, bf16[8,704,2048]{2,1,0:T(8,128)(2,1)} %bitcast.120), kind=kLoop, calls=%fused_computation | loop fusion | flops 17301504 | bytes 69206016 | tf_op jit(solution)/shard_map/concatenate | solution.py:436
  103.5 10.1 %fusion.68 = (bf16[1024,3,512]{0,2,1:T(8,128)(2,1)S(1)}, f32[1024,3,512]{0,2,1:T(8,128)S(1)}) fusion(f32[3,512]{1,0:T(4,128)S(1)} %convert_element_type.124, bf16[2048,3,512]{0,2,1:T(8,128)(2,1)} %copy.57, bf16[1024,2048]{1,0:T(8,128)(2,1)} %all-gather.4.cloned.1.call-done.b_ref), kind=kOutput, calls=%fused_computation.128 | convolution fusion | flops 6445596672 | bytes 19929088 | tf_op jit(solution)/shard_map/dot_general | solution.py:454
  145.8 79.0 %reduce-scatter.5.cloned.1.call-done = bf16[256,2048]{1,0:T(8,128)(2,1)} async-done(((bf16[1024,2048]{1,0:T(8,128)(2,1)}), bf16[256,2048]{1,0:T(8,128)(2,1)}) %reduce-scatter.5.cloned.1.call-update) | async-done | bytes 1048592 | tf_op jit(solution)/shard_map/reduce_scatter | solution.py:500
  229.5 128.8 %gather_rows.1.d_ref.b_ref = bf16[1024,2048]{1,0:T(8,128)(2,1)} custom-call(bf16[256,2048]{1,0:T(8,128)(2,1)} %get-tuple-element.96.own_ref), custom_call_target="tpu_custom_call" | custom-call | bytes 8388608 | tf_op jit(solution)/shard_map/gather_rows/pallas_call | solution.py:325
  358.4 22.8 %all-gather.6.cloned.1.call-done.x_ref.b_ref = bf16[1024,2048]{1,0:T(8,128)(2,1)} async-done(((bf16[256,2048]{1,0:T(8,128)(2,1)}), bf16[1024,2048]{1,0:T(8,128)(2,1)}) %all-gather.6.cloned.1.call-update) | async-done | bytes 4194320 | tf_op jit(solution)/shard_map/all_gather | solution.py:510
  381.1 143.0 %ffn.1 = (bf16[12,704,1024]{2,1,0:T(8,128)(2,1)}, bf16[12,352,1024]{2,1,0:T(8,128)(2,1)}, bf16[1024,2048]{1,0:T(8,128)(2,1)}, bf16[1024,2048]{1,0:T(8,128)(2,1)}, f32[16,2048]{1,0:T(8,128)}) custom-call(bf16[1024,2048]{1,0:T(8,128)(2,1)} %all-gather.6.cloned.1.call-done.x_ref.b_ref, bf16[1024,2048]{1,0:T(8,128)(2,1)} %gather_rows.1.d_ref.b_ref, ...), custom_call_target="tpu_custom_call" | custom-call | flops 106300440576 | bytes 120061952 | tf_op jit(solution)/shard_map/ffn/pallas_call | solution.py:258
  526.4 78.8 %down_grads.1 = f32[4224,256]{1,0:T(8,128)} custom-call(bf16[4224,1024]{1,0:T(8,128)(2,1)} %bitcast.155, bf16[1024,2048]{1,0:T(8,128)(2,1)S(1)} %copy-done), custom_call_target="tpu_custom_call" | custom-call | flops 17716740096 | bytes 17170432 | tf_op jit(solution)/shard_map/down_grads/pallas_call | solution.py:151
  605.2 5.9 reduce-scatter.7.cloned.1.call-done
  619.9 13.3 %fusion.62 = (bf16[6,704,1024]{2,1,0:T(8,128)(2,1)}, bf16[6,704,1024]{2,1,0:T(8,128)(2,1)}) fusion(bf16[12,704,1024]{2,1,0:T(8,128)(2,1)} %get-tuple-element.102), kind=kLoop, calls=%fused_computation.122 | loop fusion | bytes 34603008 | tf_op jit(solution)/shard_map/slice | solution.py:591
  633.3 78.7 %in_grads_a.1 = f32[4224,256]{1,0:T(8,128)} custom-call(bf16[4224,1024]{1,0:T(8,128)(2,1)} %bitcast.124, bf16[1024,2048]{1,0:T(8,128)(2,1)S(1)} %copy-done.6), custom_call_target="tpu_custom_call" | custom-call | flops 17716740096 | bytes 17170432 | tf_op jit(solution)/shard_map/in_grads_a/pallas_call | solution.py:151
  712.0 4.7 convolution_convert_fusion.1
  735.2 6.1 maximum_multiply_fusion.3
  759.8 6.0 bitcast_add_fusion
  773.3 11.2 %bitcast_convert_fusion = bf16[1024,2048]{1,0:T(8,128)(2,1)} fusion(bf16[1024,3,512]{2,0,1:T(8,128)(2,1)S(1)} %get-tuple-element.131, bf16[2048,3,512]{2,0,1:T(8,128)(2,1)} %param.32), kind=kOutput, calls=%fused_computation.2 | convolution fusion | flops 6444548096 | bytes 13631488 | tf_op jit(solution)/shard_map/sc,dc->sd/dot_general | solution.py:587
  797.0 77.9 %in_grads_b.1 = f32[4224,256]{1,0:T(8,128)} custom-call(bf16[4224,1024]{1,0:T(8,128)(2,1)} %bitcast.123, bf16[1024,2048]{1,0:T(8,128)(2,1)S(1)} %copy-done.7), custom_call_target="tpu_custom_call" | custom-call | flops 17716740096 | bytes 17170432 | tf_op jit(solution)/shard_map/in_grads_b/pallas_call | solution.py:151
  878.6 5.5 copy.94
  887.6 14.8 %mix_grads.1 = f32[512,256]{1,0:T(8,128)S(1)} custom-call(bf16[512,1024]{1,0:T(8,128)(2,1)S(1)} %bitcast.115, bf16[1024,2048]{1,0:T(8,128)(2,1)S(1)} %copy-done.8), custom_call_target="tpu_custom_call" | custom-call | flops 2147483648 | bytes 5767168 | tf_op jit(solution)/shard_map/mix_grads/pallas_call | solution.py:151
  902.4 34.1 %qkv_grads.1 = f32[1536,256]{1,0:T(8,128)S(1)} custom-call(bf16[1536,1024]{1,0:T(8,128)(2,1)S(1)} %bitcast.112, bf16[1024,2048]{1,0:T(8,128)(2,1)} %all-gather.4.cloned.1.call-done.b_ref), custom_call_target="tpu_custom_call" | custom-call | flops 6442450944 | bytes 8912896 | tf_op jit(solution)/shard_map/qkv_grads/pallas_call | solution.py:151
  940.7 5.7 pad_maximum_fusion.2
  949.3 29.2 %small_sums.1 = (f32[12,2048]{1,0:T(8,128)}, f32[12,2048]{1,0:T(8,128)}) custom-call(f32[12,2048]{1,0:T(8,128)} %select_maximum_fusion.part_ref), custom_call_target="tpu_custom_call" | custom-call | tf_op jit(solution)/shard_map/small_sums/pallas_call | solution.py:381
  (231 shorter events, 137.7 us)
Async XLA Ops:
  7.2 96.3 %all-gather.4.cloned.1.call-start = ((), (), s32[]{:S(2)}) async-start(), calls=%async_computation.4 | async-start | bytes 5242880 | tf_op jit(solution)/shard_map/all_gather | solution.py:432
  12.5 212.3 %reduce-scatter.5.cloned.1.call-start = ((), (), s32[]{:S(2)}) async-start(), calls=%async_computation.5 | async-start | bytes 5242880 | tf_op jit(solution)/shard_map/reduce_scatter | solution.py:500
  51.5 8.9 copy-start.54
  63.6 63.0 %copy-start.25 = (f32[1024,128]{1,0:T(8,128)}, f32[1024,128]{1,0:T(8,128)S(1)}, u32[]{:S(2)}) copy-start(f32[1024,128]{1,0:T(8,128)S(1)} %get-tuple-element.152) | copy-start | bytes 1572868
  63.6 63.0 %copy-start.30 = (f32[1024,128]{1,0:T(8,128)}, f32[1024,128]{1,0:T(8,128)S(1)}, u32[]{:S(2)}) copy-start(f32[1024,128]{1,0:T(8,128)S(1)} %get-tuple-element.153) | copy-start | bytes 1572868
  145.1 79.7 %copy-start.10 = (bf16[256,2048]{1,0:T(8,128)(2,1)S(1)}, bf16[256,2048]{1,0:T(8,128)(2,1)}, u32[]{:S(2)}) copy-start(bf16[256,2048]{1,0:T(8,128)(2,1)} %param.27) | copy-start | bytes 3145732
  145.1 81.6 %copy-start.20 = (bf16[256,2048]{1,0:T(8,128)(2,1)S(1)}, bf16[256,2048]{1,0:T(8,128)(2,1)}, u32[]{:S(2)}) copy-start(bf16[256,2048]{1,0:T(8,128)(2,1)} %param.30) | copy-start | bytes 3145732
  145.1 236.0 %all-gather.6.cloned.1.call-start = ((), (), s32[]{:S(2)}) async-start(), calls=%async_computation.6 | async-start | bytes 5242880 | tf_op jit(solution)/shard_map/all_gather | solution.py:510
  228.6 382.5 %reduce-scatter.7.cloned.1.call-start = ((), (), s32[]{:S(2)}) async-start(), calls=%async_computation.7 | async-start | bytes 5242880 | tf_op jit(solution)/shard_map/reduce_scatter | solution.py:517
  524.1 187.9 %all-gather.8.cloned.1.call-start = ((), (), s32[]{:S(2)}) async-start(), calls=%async_computation.8 | async-start | bytes 5242880 | tf_op jit(solution)/shard_map/all_gather | solution.py:528
  526.4 84.7 %copy-start.16 = (bf16[256,2048]{1,0:T(8,128)(2,1)S(1)}, bf16[256,2048]{1,0:T(8,128)(2,1)}, u32[]{:S(2)}) copy-start(bf16[256,2048]{1,0:T(8,128)(2,1)} %reduce-scatter.5.cloned.1.call-done) | copy-start | bytes 3145732
  615.6 330.8 %reduce-scatter.11.cloned.1.call-start = ((), (), s32[]{:S(2)}) async-start(), calls=%async_computation.10 | async-start | bytes 5242880 | tf_op jit(solution)/shard_map/reduce_scatter | solution.py:590
  619.9 13.3 %copy-start.6 = (bf16[1024,2048]{1,0:T(8,128)(2,1)S(1)}, bf16[1024,2048]{1,0:T(8,128)(2,1)}, u32[]{:S(2)}) copy-start(bf16[1024,2048]{1,0:T(8,128)(2,1)} %all-gather.6.cloned.1.call-done.x_ref.b_ref) | copy-start | bytes 12582916
  633.3 78.7 %copy-start.58 = (bf16[512,2048]{1,0:T(8,128)(2,1)S(1)}, bf16[512,2048]{1,0:T(8,128)(2,1)}, u32[]{:S(2)}) copy-start(bf16[512,2048]{1,0:T(8,128)(2,1)} %param.34) | copy-start | bytes 6291460
  712.0 4.8 copy-start.13
  716.8 7.7 copy-start.31
  718.9 5.7 slice-start
  784.5 198.5 %reduce-scatter.9.cloned.1.call-start = ((), (), s32[]{:S(2)}) async-start(), calls=%async_computation.9 | async-start | bytes 5242880 | tf_op jit(solution)/shard_map/reduce_scatter | solution.py:535
  902.4 34.1 %copy-start.4 = (f32[512,256]{1,0:T(8,128)}, f32[512,256]{1,0:T(8,128)S(1)}, u32[]{:S(2)}) copy-start(f32[512,256]{1,0:T(8,128)S(1)} %mix_grads.1) | copy-start | bytes 1572868
  940.7 5.7 copy-start.11
  940.7 5.7 copy-start.45
  940.7 5.7 copy-start.53
  946.4 36.6 %copy-start.17 = (bf16[256,2048]{1,0:T(8,128)(2,1)S(1)}, bf16[256,2048]{1,0:T(8,128)(2,1)}, u32[]{:S(2)}) copy-start(bf16[256,2048]{1,0:T(8,128)(2,1)} %reduce-scatter.5.cloned.1.call-done) | copy-start | bytes 3145732
  983.0 4.6 copy-start.5
  (45 other events, 90.7 us)
Sparse Core Ops, SparseCore 0:
  12.7 83.4 all-gather.3
  145.2 79.5 reduce-scatter.4
  228.8 152.3 all-gather.5
  524.2 86.7 reduce-scatter.6
  615.7 83.6 all-gather.7
  784.6 78.8 reduce-scatter.10
  865.9 77.2 reduce-scatter.8

commit v2 on v1

v2 whole, which is shorter than its diff:
```python
import functools

import jax
import jax.numpy as jnp
from jax import lax
from jax.experimental import pallas as pl
from jax.experimental.pallas import tpu as pltpu
from jax.sharding import PartitionSpec as P

HEAD_DIM = 128
MESH = pl.DeviceIdType.MESH
LA, LB, LC = 1, 2, 2
MIB = 2**20


epsilon = 1e-06
theta_base = 1000000.0
NT = (((1,), (1,)), ((), ()))
TN = (((0,), (0,)), ((), ()))


def rotary_tables(row_count, head_width):
    half_index = jnp.arange(head_width // 2).astype(jnp.float32)
    frequency = theta_base ** (-2.0 * half_index / head_width)
    angles = jnp.arange(row_count).astype(jnp.float32)[:, None] * frequency[None, :]
    sines = jnp.sin(angles)
    cosines = jnp.cos(angles)
    return (
        jnp.concatenate([cosines, cosines], axis=-1),
        jnp.concatenate([-sines, sines], axis=-1),
    )


def norm_back(d_normed, unit_rows, inverse, gain_vector):
    d_unit = d_normed * gain_vector
    return inverse * (d_unit - unit_rows * jnp.mean(d_unit * unit_rows, axis=-1, keepdims=True))


def rs_body(nc, cut, a_ref, b_ref, o_ref, o2_ref, own, sa, ra, kt, s1, r1, ku, s2, r2, sem_sa, sem_ra, sem_s1, sem_r1, sem_s2, sem_r2):
    i = pl.program_id(0)
    r, w = o_ref.shape
    hr = r // 2
    dp = lax.axis_index("dp")
    k = dp % 2
    x = (dp // 2) % 2
    y = dp // 4
    core_peer = y * 4 + x * 2 + (1 - k)
    x_peer = y * 4 + (1 - x) * 2 + k
    y_peer = (1 - y) * 4 + x * 2 + k

    def copy_a(c):
        return pltpu.make_async_remote_copy(
            src_ref=sa.at[c % 2], dst_ref=ra.at[c % 3], send_sem=sem_sa.at[c % 2], recv_sem=sem_ra.at[c % 3],
            device_id={"dp": core_peer}, device_id_type=MESH)

    def copy_1(c, half):
        return pltpu.make_async_remote_copy(
            src_ref=s1.at[c % 3, half], dst_ref=r1.at[c % 6, half], send_sem=sem_s1.at[c % 3, half],
            recv_sem=sem_r1.at[c % 6, half], device_id={"dp": y_peer if half else x_peer}, device_id_type=MESH)

    def copy_2(c, half):
        return pltpu.make_async_remote_copy(
            src_ref=s2.at[c % 2, half], dst_ref=r2.at[c % 6, half], send_sem=sem_s2.at[c % 2, half],
            recv_sem=sem_r2.at[c % 6, half], device_id={"dp": x_peer if half else y_peer}, device_id_type=MESH)

    @pl.when(i == 0)
    def _():
        barrier = pltpu.get_barrier_semaphore()
        for peer in (core_peer, x_peer, y_peer):
            pl.semaphore_signal(barrier, inc=1, device_id={"dp": peer}, device_id_type=MESH)
        pl.semaphore_wait(barrier, 3)

    @pl.when(jnp.logical_and(i >= LA + 3, i < nc + LA + 3))
    def _():
        copy_1(i - LA - 3, 0).wait_send()
        copy_1(i - LA - 3, 1).wait_send()

    @pl.when(jnp.logical_and(i >= LA, i < nc + LA))
    def _():
        c = i - LA
        copy_a(c).wait_recv()
        for half in range(2):
            rows = slice(half * hr, half * hr + hr)
            keep, other = (1, 2) if half else (2, 1)
            def total(role):
                return own[c % 2, role, rows, :] + ra[c % 3, role, rows, :].astype(jnp.float32)
            s1[c % 3, half, 0] = total(other).astype(jnp.bfloat16)
            s1[c % 3, half, 1] = total(3).astype(jnp.bfloat16)
            copy_1(c, half).start()
            kt[c % 3, half, 0] = total(0)
            kt[c % 3, half, 1] = total(keep)

    @pl.when(jnp.logical_and(i >= LA + LB, i < nc + LA + LB))
    def _():
        c = i - LA - LB
        @pl.when(c >= 2)
        def _():
            copy_2(c - 2, 0).wait_send()
            copy_2(c - 2, 1).wait_send()
        for half in range(2):
            copy_1(c, half).wait_recv()
            s2[c % 2, half] = (kt[c % 3, half, 1] + r1[c % 6, half, 1].astype(jnp.float32)).astype(jnp.bfloat16)
            copy_2(c, half).start()
            ku[c % 3, half] = kt[c % 3, half, 0] + r1[c % 6, half, 0].astype(jnp.float32)

    @pl.when(i >= LA + LB + LC)
    def _():
        c = i - LA - LB - LC
        for half in range(2):
            rows = slice(half * hr, half * hr + hr)
            copy_2(c, half).wait_recv()
            result = ku[c % 3, half] + r2[c % 6, half].astype(jnp.float32)

            @pl.when(c < cut)
            def _():
                o_ref[rows, :] = result

            @pl.when(c >= cut)
            def _():
                o2_ref[rows, :] = result

        @pl.when(c >= nc - 2)
        def _():
            copy_2(c, 0).wait_send()
            copy_2(c, 1).wait_send()

    @pl.when(jnp.logical_and(i >= 2, i < nc + 2))
    def _():
        copy_a(i - 2).wait_send()

    @pl.when(i < nc)
    def _():
        a = a_ref[...]
        targets = (y * 4 + x * 2, y * 4 + (1 - x) * 2, (1 - y) * 4 + x * 2, (1 - y) * 4 + (1 - x) * 2)
        for role in range(4):
            cols = pl.ds(pl.multiple_of((targets[role] + 1 - k) * w, w), w)
            sa[i % 2, role] = jnp.dot(a, b_ref[:, cols], preferred_element_type=jnp.float32).astype(jnp.bfloat16)
        copy_a(i).start()
        for role in range(4):
            cols = pl.ds(pl.multiple_of((targets[role] + k) * w, w), w)
            own[i % 2, role] = jnp.dot(a, b_ref[:, cols], preferred_element_type=jnp.float32)

def weight_grad_scatter_kernel(a, b, r, cid, name, first, count, cut):
    T = a.shape[1]
    R = count * r
    D = b.shape[1]
    w = D // 8
    nc = count
    L = LA + LB + LC
    f32, bf = jnp.float32, jnp.bfloat16
    dma = pltpu.SemaphoreType.DMA
    return pl.pallas_call(
        functools.partial(rs_body, nc, cut),
        grid=(nc + L,),
        in_specs=[pl.BlockSpec((r, T), lambda i: (jnp.minimum(i, nc - 1) + first, 0)),
                  pl.BlockSpec((T, D), lambda i: (0, 0), pipeline_mode=pl.Buffered(1))],
        out_specs=[
            pl.BlockSpec((r, w), lambda i: (jnp.clip(i - L, 0, cut - 1), 0)),
            pl.BlockSpec((r, w), lambda i: (jnp.clip(i - L - cut, 0, max(nc - cut, 1) - 1), 0)),
        ],
        out_shape=[
            jax.ShapeDtypeStruct((cut * r, w), f32),
            jax.ShapeDtypeStruct((max(nc - cut, 1) * r, w), f32),
        ],
        scratch_shapes=[
            pltpu.VMEM((2, 4, r, w), f32), pltpu.VMEM((2, 4, r, w), bf), pltpu.VMEM((3, 4, r, w), bf),
            pltpu.VMEM((3, 2, 2, r // 2, w), f32), pltpu.VMEM((3, 2, 2, r // 2, w), bf), pltpu.VMEM((6, 2, 2, r // 2, w), bf),
            pltpu.VMEM((3, 2, r // 2, w), f32), pltpu.VMEM((2, 2, r // 2, w), bf), pltpu.VMEM((6, 2, r // 2, w), bf),
            dma((2,)), dma((3,)), dma((3, 2)), dma((6, 2)), dma((2, 2)), dma((6, 2))],
        compiler_params=pltpu.CompilerParams(vmem_limit_bytes=48 * 2**20, collective_id=cid, has_side_effects=True),
        cost_estimate=pl.CostEstimate(flops=2 * R * T * D, bytes_accessed=2 * R * T + 2 * T * D + 4 * R * w, transcendentals=0),
        name=name)(a, b)


def ffn_body(
    experts, x_ref, d_ref, routes_ref, rw_ref, ei_ref, si_ref, eo_ref, so_ref,
    dgu_ref, s_ref, dn_ref, bt_ref, rg_ref, np_ref,
    dn_acc, bt_acc, probs_ref, w_ref, ds_ref, wi_buf, wd_buf, sem,
):
    c = pl.program_id(0)
    chunks = pl.num_programs(0)
    h = eo_ref.shape[1]
    slots, width = x_ref.shape

    def fetch(step):
        slot = step % 2

        @pl.when(step < experts)
        def _():
            pltpu.make_async_copy(ei_ref.at[step], wi_buf.at[slot], sem.at[0, slot]).start()
            pltpu.make_async_copy(eo_ref.at[step], wd_buf.at[slot], sem.at[1, slot]).start()

        @pl.when(step >= experts)
        def _():
            pltpu.make_async_copy(si_ref.at[step - experts], wi_buf.at[slot], sem.at[0, slot]).start()
            pltpu.make_async_copy(so_ref.at[step - experts], wd_buf.at[slot], sem.at[1, slot]).start()

    @pl.when(c == 0)
    def _():
        fetch(c)

    @pl.when(c + 1 < chunks)
    def _():
        fetch(c + 1)

    def picked():
        expert = lax.broadcasted_iota(jnp.int32, (experts, slots), 0)
        hit = jnp.zeros((experts, slots), jnp.float32)
        for j in range(routes_ref.shape[0]):
            hit = hit + jnp.where(routes_ref[j : j + 1, :] == expert, 1.0, 0.0)
        return hit

    @pl.when(c == 0)
    def _():
        logits = lax.dot_general(rw_ref[...], x_ref[...], NT, preferred_element_type=jnp.float32)
        raised = jnp.exp(logits[:experts] - jnp.max(logits[:experts], axis=0, keepdims=True))
        probs = raised / jnp.sum(raised, axis=0, keepdims=True)
        gate = 1.0 / (1.0 + jnp.exp(-logits[experts:]))
        probs_ref[...] = probs
        w_ref[:experts, :] = probs * picked()
        w_ref[experts:, :] = gate
        ds_ref[...] = jnp.zeros_like(ds_ref)
        dn_acc[...] = jnp.zeros_like(dn_acc)
        bt_acc[...] = jnp.zeros_like(bt_acc)

    row = pl.ds(jnp.minimum(c, experts), 1)
    slot = c % 2
    pltpu.make_async_copy(ei_ref.at[0], wi_buf.at[slot], sem.at[0, slot]).wait()
    pltpu.make_async_copy(eo_ref.at[0], wd_buf.at[slot], sem.at[1, slot]).wait()
    wi = wi_buf.at[slot]
    wd = wd_buf.at[slot]
    x = x_ref[...]
    g = lax.dot_general(wi[:h], x, NT, preferred_element_type=jnp.float32)
    u = lax.dot_general(wi[h:], x, NT, preferred_element_type=jnp.float32)
    p = lax.dot_general(wd[...], d_ref[...], NT, preferred_element_type=jnp.float32)
    w = w_ref[row, :]
    sg = 1.0 / (1.0 + jnp.exp(-g))
    si = g * sg
    inner = (si * u).astype(jnp.bfloat16).astype(jnp.float32)
    s = (w * inner).astype(jnp.bfloat16)
    s_ref[0] = s
    ds_ref[row, :] += jnp.sum(p * inner, axis=0, keepdims=True)
    di = w * p
    dg = (di * u * sg * (1.0 + g * (1.0 - sg))).astype(jnp.bfloat16)
    du = (di * si).astype(jnp.bfloat16)
    dgu_ref[0, :h] = dg
    dgu_ref[0, h:] = du
    dgu = jnp.concatenate([dg, du], axis=0)
    block = 512
    for n in range(0, width, block):
        cols = slice(n, n + block)
        dn_acc[:, cols] += lax.dot_general(dgu, wi[:, cols], TN, preferred_element_type=jnp.float32)
        bt_acc[:, cols] += lax.dot_general(s, wd[:, cols], TN, preferred_element_type=jnp.float32)

    @pl.when(c == chunks - 1)
    def _():
        probs = probs_ref[...]
        d_probs = ds_ref[:experts, :] * picked()
        d_logits = probs * (d_probs - jnp.sum(probs * d_probs, axis=0, keepdims=True))
        gate = w_ref[experts:, :]
        d_gate = ds_ref[experts:, :] * gate * (1.0 - gate)
        small = jnp.concatenate([d_logits, d_gate], axis=0)
        high = small.astype(jnp.bfloat16)
        low = (small - high.astype(jnp.float32)).astype(jnp.bfloat16)
        rg_ref[...] = jnp.dot(high, x_ref[...], preferred_element_type=jnp.float32) + jnp.dot(
            low, x_ref[...], preferred_element_type=jnp.float32
        )
        for n in range(0, width, block):
            cols = slice(n, n + block)
            extra = lax.dot_general(high, rw_ref[:, cols], TN, preferred_element_type=jnp.float32)
            extra += lax.dot_general(low, rw_ref[:, cols], TN, preferred_element_type=jnp.float32)
            total = dn_acc[:, cols] + extra
            dn_ref[:, cols] = total.astype(dn_ref.dtype)
            np_ref[:, cols] = jnp.sum(total * x_ref[:, cols].astype(jnp.float32), axis=0, keepdims=True)
        bt_ref[...] = bt_acc[...].astype(bt_ref.dtype)


def ffn(x, d_two, routes_t, router_rows, ei, si, eo, so):
    experts, h2, width = ei.shape
    chunks = experts + si.shape[0]
    h = h2 // 2
    slots = x.shape[0]
    rows = router_rows.shape[0]
    bf, f32 = jnp.bfloat16, jnp.float32
    anywhere = pl.BlockSpec(memory_space=pl.ANY)

    def whole(shape):
        return pl.BlockSpec(shape, lambda c: (0,) * len(shape), pipeline_mode=pl.Buffered(1))

    def chunk(shape):
        return pl.BlockSpec((1, *shape), lambda c: (c, 0, 0))

    return pl.pallas_call(
        functools.partial(ffn_body, experts),
        grid=(chunks,),
        in_specs=[
            whole((slots, width)), whole((slots, width)), whole(routes_t.shape), whole((rows, width)),
            anywhere, anywhere, anywhere, anywhere,
        ],
        out_specs=[
            chunk((h2, slots)), chunk((h, slots)), whole((slots, width)), whole((slots, width)), whole((rows, width)),
            whole((1, width)),
        ],
        out_shape=[
            jax.ShapeDtypeStruct((chunks, h2, slots), bf), jax.ShapeDtypeStruct((chunks, h, slots), bf),
            jax.ShapeDtypeStruct((slots, width), bf), jax.ShapeDtypeStruct((slots, width), bf),
            jax.ShapeDtypeStruct((rows, width), f32), jax.ShapeDtypeStruct((1, width), f32),
        ],
        scratch_shapes=[
            pltpu.VMEM((slots, width), f32), pltpu.VMEM((slots, width), f32),
            pltpu.VMEM((experts, slots), f32), pltpu.VMEM((rows, slots), f32), pltpu.VMEM((rows, slots), f32),
            pltpu.VMEM((2, h2, width), bf), pltpu.VMEM((2, h, width), bf), pltpu.SemaphoreType.DMA((2, 2)),
        ],
        compiler_params=pltpu.CompilerParams(vmem_limit_bytes=62 * MIB),
        cost_estimate=pl.CostEstimate(
            flops=12 * chunks * h * slots * width, bytes_accessed=10 * chunks * h * width + 16 * slots * width,
            transcendentals=chunks * h * slots,
        ),
        name="ffn",
    )(x, d_two, routes_t, router_rows, ei, si, eo, so)


def turn(v):
    half = v.shape[1] // 2
    return jnp.concatenate([v[:, half:], v[:, :half]], axis=1)


def qkv_body(x_ref, w_ref, bias_ref, cos_ref, sin_ref, out_ref):
    j = pl.program_id(0)
    cols = w_ref.shape[2]
    y = jnp.dot(x_ref[...], w_ref[0], preferred_element_type=jnp.float32)
    y = y + bias_ref[0].astype(jnp.float32)

    @pl.when(j < 2)
    def _():
        for head in range(cols // HEAD_DIM):
            place = slice(head * HEAD_DIM, (head + 1) * HEAD_DIM)
            v = y[:, place]
            out_ref[0, :, place] = (v * cos_ref[...] + turn(v) * sin_ref[...]).astype(out_ref.dtype)

    @pl.when(j == 2)
    def _():
        out_ref[0] = y.astype(out_ref.dtype)


def project_qkv(x, w, bias, cos_table, sin_table):
    slots, width = x.shape
    cols = w.shape[2]
    table = pl.BlockSpec((slots, HEAD_DIM), lambda j: (0, 0), pipeline_mode=pl.Buffered(1))
    return pl.pallas_call(
        qkv_body,
        grid=(3,),
        in_specs=[
            pl.BlockSpec((slots, width), lambda j: (0, 0), pipeline_mode=pl.Buffered(1)),
            pl.BlockSpec((1, width, cols), lambda j: (j, 0, 0)),
            pl.BlockSpec((1, 1, cols), lambda j: (j, 0, 0)),
            table, table,
        ],
        out_specs=pl.BlockSpec((1, slots, cols), lambda j: (j, 0, 0)),
        out_shape=jax.ShapeDtypeStruct((3, slots, cols), jnp.bfloat16),
        compiler_params=pltpu.CompilerParams(vmem_limit_bytes=48 * MIB),
        cost_estimate=pl.CostEstimate(
            flops=6 * slots * width * cols, bytes_accessed=2 * slots * width + 6 * width * cols, transcendentals=0
        ),
        name="project_qkv",
    )(x, w, bias, cos_table, sin_table)


def block_probs(length_ref, q, k, start):
    s = lax.dot_general(q, k, NT, preferred_element_type=jnp.float32) * (HEAD_DIM**-0.5)
    row = lax.broadcasted_iota(jnp.int32, s.shape, 0) + start
    col = lax.broadcasted_iota(jnp.int32, s.shape, 1)
    s = jnp.where((col <= row) & (col < length_ref[0]), s, -1000000000.0)
    e = jnp.exp(s - jnp.max(s, axis=1, keepdims=True))
    return e * (1.0 / jnp.sum(e, axis=1, keepdims=True))


def attend_body(rows, length_ref, q_ref, k_ref, v_ref, mixed_ref, mixed_t_ref):
    for start in range(0, q_ref.shape[1], rows):
        here, end = slice(start, start + rows), start + rows
        p = block_probs(length_ref, q_ref[0, here, :], k_ref[0, :end, :], start)
        mixed = jnp.dot(p.astype(jnp.bfloat16), v_ref[0, :end, :], preferred_element_type=jnp.float32)
        mixed_ref[here, :] = mixed.astype(mixed_ref.dtype)
        mixed_t_ref[:, here] = mixed.T.astype(mixed_ref.dtype)


def attend(lengths, qkv):
    _, slots, cols = qkv.shape
    rows = min(256, slots)

    def part(j):
        return pl.BlockSpec((1, slots, HEAD_DIM), lambda h: (j, 0, h))

    return pl.pallas_call(
        functools.partial(attend_body, rows),
        grid=(cols // HEAD_DIM,),
        in_specs=[pl.BlockSpec(memory_space=pltpu.SMEM), part(0), part(1), part(2)],
        out_specs=[
            pl.BlockSpec((slots, HEAD_DIM), lambda h: (0, h)), pl.BlockSpec((HEAD_DIM, slots), lambda h: (h, 0)),
        ],
        out_shape=[
            jax.ShapeDtypeStruct((slots, cols), jnp.bfloat16), jax.ShapeDtypeStruct((cols, slots), jnp.bfloat16),
        ],
        compiler_params=pltpu.CompilerParams(vmem_limit_bytes=32 * MIB),
        cost_estimate=pl.CostEstimate(
            flops=4 * slots * slots * cols, bytes_accessed=10 * slots * cols, transcendentals=slots * slots * cols // HEAD_DIM
        ),
        name="attend",
    )(lengths, qkv, qkv, qkv)


def attend_back_body(
    rows, length_ref, q_ref, k_ref, v_ref, dm_ref, cos_ref, sin_ref, out_ref, out_t_ref, bias_ref, dk_acc, dv_acc
):
    slots = q_ref.shape[1]
    scale = HEAD_DIM**-0.5
    bf, f32 = jnp.bfloat16, jnp.float32

    def finish(j, here, grad):
        if j < 2:
            grad = grad * cos_ref[here, :] - turn(grad) * sin_ref[here, :]
        low = grad.astype(bf)
        out_ref[j, here, :] = low
        out_t_ref[j, :, here] = grad.T.astype(bf)
        return jnp.sum(low.astype(f32), axis=0, keepdims=True)

    dq_sum = jnp.zeros((1, HEAD_DIM), f32)
    starts = list(range(0, slots, rows))[::-1]
    for start in starts:
        here, end = slice(start, start + rows), start + rows
        q, k, v, dm = q_ref[0, here, :], k_ref[0, :end, :], v_ref[0, :end, :], dm_ref[here, :]
        p = block_probs(length_ref, q, k, start)
        dp = lax.dot_general(dm, v, NT, preferred_element_type=f32)
        ds = (p * (dp - jnp.sum(p * dp, axis=1, keepdims=True))).astype(bf)
        dq_sum += finish(0, here, jnp.dot(ds, k, preferred_element_type=f32) * scale)
        dk = lax.dot_general(ds, q, TN, preferred_element_type=f32) * scale
        dv = lax.dot_general(p.astype(bf), dm, TN, preferred_element_type=f32)
        if start == starts[0]:
            dk_acc[...] = dk
            dv_acc[...] = dv
        else:
            dk_acc[:end, :] += dk
            dv_acc[:end, :] += dv
    every = slice(0, slots)
    bias_ref[0] = dq_sum
    bias_ref[1] = finish(1, every, dk_acc[...])
    bias_ref[2] = finish(2, every, dv_acc[...])


def attend_back(lengths, qkv, d_mixed, cos_table, sin_table):
    _, slots, cols = qkv.shape
    rows = min(256, slots)
    bf, f32 = jnp.bfloat16, jnp.float32

    def part(j):
        return pl.BlockSpec((1, slots, HEAD_DIM), lambda h: (j, 0, h))

    table = pl.BlockSpec((slots, HEAD_DIM), lambda h: (0, 0), pipeline_mode=pl.Buffered(1))
    return pl.pallas_call(
        functools.partial(attend_back_body, rows),
        grid=(cols // HEAD_DIM,),
        in_specs=[
            pl.BlockSpec(memory_space=pltpu.SMEM), part(0), part(1), part(2),
            pl.BlockSpec((slots, HEAD_DIM), lambda h: (0, h)), table, table,
        ],
        out_specs=[
            pl.BlockSpec((3, slots, HEAD_DIM), lambda h: (0, 0, h)), pl.BlockSpec((3, HEAD_DIM, slots), lambda h: (0, h, 0)),
            pl.BlockSpec((3, 1, HEAD_DIM), lambda h: (0, 0, h)),
        ],
        out_shape=[
            jax.ShapeDtypeStruct((3, slots, cols), bf), jax.ShapeDtypeStruct((3, cols, slots), bf),
            jax.ShapeDtypeStruct((3, 1, cols), f32),
        ],
        scratch_shapes=[pltpu.VMEM((slots, HEAD_DIM), f32), pltpu.VMEM((slots, HEAD_DIM), f32)],
        compiler_params=pltpu.CompilerParams(vmem_limit_bytes=40 * MIB),
        cost_estimate=pl.CostEstimate(
            flops=10 * slots * slots * cols, bytes_accessed=20 * slots * cols, transcendentals=slots * slots * cols // HEAD_DIM
        ),
        name="attend_back",
    )(lengths, qkv, qkv, qkv, d_mixed, cos_table, sin_table)


def qkv_back_body(d_ref, w_ref, x_ref, out_ref, np_ref):
    total = lax.dot_general(d_ref[0], w_ref[0], NT, preferred_element_type=jnp.float32)
    for j in range(1, 3):
        total += lax.dot_general(d_ref[j], w_ref[j], NT, preferred_element_type=jnp.float32)
    out_ref[...] = total.astype(out_ref.dtype)
    np_ref[...] = jnp.sum(total * x_ref[...].astype(jnp.float32), axis=0, keepdims=True)


def qkv_back(d_qkv, w, x):
    _, slots, cols = d_qkv.shape
    width = w.shape[1]
    block = 512
    return pl.pallas_call(
        qkv_back_body,
        grid=(width // block,),
        in_specs=[
            pl.BlockSpec((3, slots, cols), lambda n: (0, 0, 0), pipeline_mode=pl.Buffered(1)),
            pl.BlockSpec((3, block, cols), lambda n: (0, n, 0)),
            pl.BlockSpec((slots, block), lambda n: (0, n)),
        ],
        out_specs=[pl.BlockSpec((slots, block), lambda n: (0, n)), pl.BlockSpec((1, block), lambda n: (0, n))],
        out_shape=[
            jax.ShapeDtypeStruct((slots, width), jnp.bfloat16), jax.ShapeDtypeStruct((1, width), jnp.float32),
        ],
        compiler_params=pltpu.CompilerParams(vmem_limit_bytes=48 * MIB),
        cost_estimate=pl.CostEstimate(
            flops=6 * slots * width * cols, bytes_accessed=4 * slots * width + 6 * width * cols, transcendentals=0
        ),
        name="qkv_back",
    )(d_qkv, w, x)


def weight_grad_scatter(a, b, r, cid, name, first=0, count=None, cut=None):
    count = a.shape[0] // r if count is None else count
    cut = count if cut is None else cut
    if lax.axis_size("dp") == 8:
        return weight_grad_scatter_kernel(a, b, r, cid, name, first, count, cut)
    product = jnp.dot(a[first * r : (first + count) * r], b, preferred_element_type=jnp.float32)
    result = lax.psum_scatter(
        product.astype(jnp.bfloat16), "dp", scatter_dimension=1, tiled=True
    ).astype(jnp.float32)
    return result[: cut * r], result[cut * r :]


def gather_body(own_ref, out_ref, local_sem, send_left, recv_left, send_right, recv_right):
    me = lax.axis_index("tensor")
    size = lax.axis_size("tensor")
    rows = own_ref.shape[0]
    has_left, has_right = me > 0, me < size - 1

    def block(owner):
        return out_ref.at[pl.ds(pl.multiple_of(owner * rows, rows), rows)]

    def to_left(step):
        source = own_ref if step == 0 else block(me + step)
        return pltpu.make_async_remote_copy(
            src_ref=source, dst_ref=block(me + step), send_sem=send_left.at[step], recv_sem=recv_left.at[step],
            device_id={"tensor": me - 1}, device_id_type=MESH,
        )

    def from_right(step):
        return pltpu.make_async_remote_copy(
            src_ref=own_ref, dst_ref=block(me + 1 + step), send_sem=send_left.at[step], recv_sem=recv_left.at[step],
            device_id={"tensor": me + 1}, device_id_type=MESH,
        )

    def to_right(step):
        source = own_ref if step == 0 else block(me - step)
        return pltpu.make_async_remote_copy(
            src_ref=source, dst_ref=block(me - step), send_sem=send_right.at[step], recv_sem=recv_right.at[step],
            device_id={"tensor": me + 1}, device_id_type=MESH,
        )

    def from_left(step):
        return pltpu.make_async_remote_copy(
            src_ref=own_ref, dst_ref=block(me - 1 - step), send_sem=send_right.at[step], recv_sem=recv_right.at[step],
            device_id={"tensor": me - 1}, device_id_type=MESH,
        )

    barrier = pltpu.get_barrier_semaphore()

    @pl.when(has_left)
    def _():
        pl.semaphore_signal(barrier, inc=1, device_id={"tensor": me - 1}, device_id_type=MESH)

    @pl.when(has_right)
    def _():
        pl.semaphore_signal(barrier, inc=1, device_id={"tensor": me + 1}, device_id_type=MESH)

    pl.semaphore_wait(barrier, has_left.astype(jnp.int32) + has_right.astype(jnp.int32))
    local = pltpu.make_async_copy(own_ref, block(me), local_sem)
    local.start()
    for step in range(size):
        if step > 0:
            @pl.when(me + step < size)
            def _():
                from_right(step - 1).wait_recv()

        @pl.when(has_left & (me + step < size))
        def _():
            to_left(step).start()

        if step > 0:
            @pl.when(me - step >= 0)
            def _():
                from_left(step - 1).wait_recv()

        @pl.when(has_right & (me - step >= 0))
        def _():
            to_right(step).start()

    for step in range(size):
        @pl.when(has_left & (me + step < size))
        def _():
            to_left(step).wait_send()

        @pl.when(has_right & (me - step >= 0))
        def _():
            to_right(step).wait_send()

    local.wait()


def gather_rows(own, cid):
    size = lax.axis_size("tensor")
    rows, width = own.shape
    return pl.pallas_call(
        gather_body,
        in_specs=[pl.BlockSpec(memory_space=pl.ANY)],
        out_specs=pl.BlockSpec(memory_space=pl.ANY),
        out_shape=jax.ShapeDtypeStruct((rows * size, width), own.dtype),
        scratch_shapes=[
            pltpu.SemaphoreType.DMA, *[pltpu.SemaphoreType.DMA((size,))] * 4,
        ],
        compiler_params=pltpu.CompilerParams(collective_id=cid, has_side_effects=True),
        cost_estimate=pl.CostEstimate(flops=0, bytes_accessed=2 * rows * size * width * 2, transcendentals=0),
        name="gather_rows",
    )(own)


def sums_body(
    local_rows, part_ref, out_ref, from_dp, mine, from_tensor, send_dp, recv_dp, send_t, recv_t, send_out, recv_out
):
    size_dp, size_t = lax.axis_size("dp"), lax.axis_size("tensor")
    me_dp, me_t = lax.axis_index("dp"), lax.axis_index("tensor")
    width = mine.shape[1]

    def piece(ref, owner):
        return ref.at[:, pl.ds(pl.multiple_of(owner * width, width), width)]

    barrier = pltpu.get_barrier_semaphore()
    for step in range(1, size_dp):
        peer = lax.rem(me_dp + step, size_dp)
        pl.semaphore_signal(barrier, inc=1, device_id={"dp": peer}, device_id_type=MESH)
    for step in range(1, size_t):
        peer = lax.rem(me_t + step, size_t)
        pl.semaphore_signal(barrier, inc=1, device_id={"tensor": peer}, device_id_type=MESH)
    pl.semaphore_wait(barrier, size_dp + size_t - 2)

    def send(source, target, axis, step, send_sem, recv_sem):
        me, size = (me_dp, size_dp) if axis == "dp" else (me_t, size_t)
        copy = pltpu.make_async_remote_copy(
            src_ref=source, dst_ref=target, send_sem=send_sem.at[step], recv_sem=recv_sem.at[step],
            device_id={axis: lax.rem(me + step, size)}, device_id_type=MESH,
        )
        copy.start()
        return copy

    first = [
        send(piece(part_ref, lax.rem(me_dp + step, size_dp)), from_dp.at[step], "dp", step, send_dp, recv_dp)
        for step in range(1, size_dp)
    ]
    total = piece(part_ref, me_dp)[...]
    for step, copy in enumerate(first, 1):
        copy.wait_recv()
        total = total + from_dp[step]
    mine[...] = total
    second = [send(mine, from_tensor.at[step], "tensor", step, send_t, recv_t) for step in range(1, size_t)]
    for step, copy in enumerate(second, 1):
        copy.wait_recv()
        total = total + from_tensor[step]
    here = piece(out_ref, me_dp)
    here[...] = total
    piece(out_ref.at[local_rows:], me_dp)[...] = mine[local_rows:, :]
    third = [send(here, here, "dp", step, send_out, recv_out) for step in range(1, size_dp)]
    for copy in third:
        copy.wait_recv()
    for copy in first + second + third:
        copy.wait_send()


def small_sums(part, local_rows, cid):
    size_dp, size_t = lax.axis_size("dp"), lax.axis_size("tensor")
    rows, width = part.shape[0], part.shape[1] // size_dp
    vmem = pl.BlockSpec(memory_space=pltpu.VMEM)
    dma = pltpu.SemaphoreType.DMA
    f32 = jnp.float32
    return pl.pallas_call(
        functools.partial(sums_body, local_rows),
        in_specs=[vmem],
        out_specs=vmem,
        out_shape=jax.ShapeDtypeStruct(part.shape, f32),
        scratch_shapes=[
            pltpu.VMEM((size_dp, rows, width), f32), pltpu.VMEM((rows, width), f32), pltpu.VMEM((size_t, rows, width), f32),
            dma((size_dp,)), dma((size_dp,)), dma((size_t,)), dma((size_t,)), dma((size_dp,)), dma((size_dp,)),
        ],
        compiler_params=pltpu.CompilerParams(collective_id=cid, has_side_effects=True),
        name="small_sums",
    )(part)


def on_device(
    tokens,
    lengths,
    routes,
    cotangent,
    norm_one,
    qkv_weight,
    qkv_bias,
    out_weight,
    norm_two,
    router_weight,
    expert_in,
    expert_out,
    shared_in,
    shared_out,
    shared_gate,
):
    own_rows = tokens.shape[0]
    slot_count = routes.shape[0]
    model_width = tokens.shape[1]
    qkv_cols = qkv_weight.shape[2]
    local_heads = qkv_cols // HEAD_DIM
    experts = router_weight.shape[1]
    eff = expert_in.shape[3]
    shared_chunks = shared_out.shape[0] // eff
    chunks = experts + shared_chunks
    bf = jnp.bfloat16
    qkv_cols = qkv_weight.shape[2]
    length = lengths[0]
    tensor_index = lax.axis_index("tensor")
    first_row = tensor_index * own_rows
    live_own = (first_row + jnp.arange(own_rows) < length).astype(jnp.float32)[:, None]
    tokens_f = tokens.astype(jnp.float32)
    gain_one = norm_one.astype(jnp.float32)
    gain_two = norm_two.astype(jnp.float32)
    inv_one = lax.rsqrt(jnp.mean(tokens_f * tokens_f, axis=-1, keepdims=True) + epsilon)
    unit_one = tokens_f * inv_one
    normed_one = lax.all_gather((unit_one * gain_one).astype(bf), "tensor", axis=0, tiled=True)
    cos_table, sin_table = rotary_tables(slot_count, HEAD_DIM)
    qkv_w = qkv_weight.transpose(1, 0, 2)
    ei = expert_in.transpose(0, 2, 3, 1).reshape(experts, 2 * eff, model_width)
    eo = expert_out
    si = (
        shared_in.reshape(model_width, 2, shared_chunks, eff)
        .transpose(2, 1, 3, 0)
        .reshape(shared_chunks, 2 * eff, model_width)
    )
    so = shared_out.reshape(shared_chunks, eff, model_width)
    router_rows = jnp.concatenate(
        [
            router_weight.T,
            shared_gate[None],
            jnp.zeros((-(experts + 1) % 16, model_width), bf),
        ],
        axis=0,
    )
    grad_out = cotangent.astype(jnp.float32) * live_own
    d_two_own = (live_own * grad_out).astype(bf)
    normed_one, si, router_rows, cos_table, sin_table, d_two_own = lax.optimization_barrier(
        (normed_one, si, router_rows, cos_table, sin_table, d_two_own)
    )
    qkv = project_qkv(normed_one, qkv_w, qkv_bias[:, None, :], cos_table, sin_table)
    mixed, mixed_t = attend(lengths, qkv)
    branch_partial = jnp.dot(mixed, out_weight, preferred_element_type=jnp.float32).astype(bf)
    d_two_own, branch_partial = lax.optimization_barrier((d_two_own, branch_partial))
    branch_one = lax.psum_scatter(branch_partial, "tensor", scatter_dimension=0, tiled=True)
    d_two = gather_rows(d_two_own, 1)
    branch_one, d_two = lax.optimization_barrier((branch_one, d_two))
    hidden = tokens_f + live_own * branch_one.astype(jnp.float32)
    inv_two = lax.rsqrt(jnp.mean(hidden * hidden, axis=-1, keepdims=True) + epsilon)
    unit_two = hidden * inv_two
    normed_two = lax.all_gather((unit_two * gain_two).astype(bf), "tensor", axis=0, tiled=True)
    d_gate_up, scaled_inner, d_normed, combined, router_part, norm_two_part = ffn(
        normed_two, d_two, routes.T, router_rows, ei, si, eo, so
    )
    d_gate_up = d_gate_up.reshape(chunks * 2 * eff, slot_count)
    scaled_inner = scaled_inner.reshape(chunks * eff, slot_count)
    grad_two = lax.psum_scatter(d_normed, "tensor", scatter_dimension=0, tiled=True)
    out_grads, shared_out_grad = weight_grad_scatter(
        scaled_inner, d_two, eff, 2, "down_grads", cut=experts
    )
    grad_two = grad_two.astype(jnp.float32)
    grad_hidden = grad_out + norm_back(grad_two, unit_two, inv_two, gain_two)
    d_one_own, out_grads = lax.optimization_barrier(
        ((live_own * grad_hidden).astype(bf), out_grads)
    )
    d_one = lax.all_gather(d_one_own, "tensor", axis=0, tiled=True)
    d_gate_up, _ = lax.optimization_barrier((d_gate_up, d_one_own))
    in_grads_a, _ = weight_grad_scatter(
        d_gate_up, normed_two, eff, 3, "expert_in_grads", 0, 2 * experts
    )
    d_one, in_grads_a, combined, d_gate_up = lax.optimization_barrier(
        (d_one, in_grads_a, combined, d_gate_up)
    )
    branch_two = lax.psum_scatter(combined, "tensor", scatter_dimension=0, tiled=True)
    d_mixed = lax.dot_general(d_one, out_weight, NT, preferred_element_type=jnp.float32).astype(bf)
    d_qkv, d_qkv_t, bias_part = attend_back(lengths, qkv, d_mixed, cos_table, sin_table)
    grad_one, norm_one_part = qkv_back(d_qkv, qkv_w, normed_one)
    grad_one, d_gate_up, d_qkv_t, mixed_t = lax.optimization_barrier(
        (grad_one, d_gate_up, d_qkv_t, mixed_t)
    )
    grad_one_own = lax.psum_scatter(grad_one, "tensor", scatter_dimension=0, tiled=True)
    part = jnp.concatenate(
        [
            router_part[: experts + 1],
            norm_one_part / gain_one[None],
            norm_two_part / gain_two[None],
            jnp.pad(bias_part.reshape(1, 3 * qkv_cols), ((0, 0), (0, model_width - 3 * qkv_cols))),
        ],
        axis=0,
    )
    sums = small_sums(part, experts + 3, 7)
    in_grads_b, _ = weight_grad_scatter(
        d_gate_up, normed_two, eff, 4, "shared_in_grads", 2 * experts, 2 * shared_chunks
    )
    qkv_sum, _ = weight_grad_scatter(
        d_qkv_t.reshape(3 * qkv_cols, slot_count), normed_one, 3 * qkv_cols // 4, 5, "qkv_grads"
    )
    out_sum, _ = weight_grad_scatter(mixed_t, d_one, qkv_cols // 2, 6, "mix_grads")
    output = (hidden + live_own * branch_two.astype(jnp.float32)).astype(bf)
    grad_one = grad_one_own.astype(jnp.float32)
    input_grad = grad_hidden + norm_back(grad_one, unit_one, inv_one, gain_one)
    qkv_bias_grad = sums[experts + 3, : 3 * qkv_cols].reshape(3, qkv_cols)
    own_cols = out_grads.shape[1]
    expert_in_grad = in_grads_a.reshape(experts, 2, eff, own_cols).transpose(0, 3, 1, 2)
    shared_in_grad = (
        in_grads_b.reshape(shared_chunks, 2, eff, own_cols)
        .transpose(3, 1, 0, 2)
        .reshape(own_cols, 2, shared_chunks * eff)
    )
    return (
        output,
        input_grad,
        sums[experts + 1],
        qkv_sum.reshape(3, qkv_cols, own_cols).transpose(2, 0, 1),
        qkv_bias_grad,
        out_sum,
        sums[experts + 2],
        sums[:experts].T,
        expert_in_grad,
        out_grads.reshape(experts, eff, own_cols),
        shared_in_grad,
        shared_out_grad,
        sums[experts],
    )


def solution(mesh):
    in_specs = (
        P(("dp", "tensor"), None),
        P("dp"),
        P("dp", None),
        P(("dp", "tensor"), None),
        P(),
        P(None, None, "tensor"),
        P(None, "tensor"),
        P("tensor", None),
        P(),
        P(),
        P(None, None, None, "tensor"),
        P(None, "tensor", None),
        P(None, None, "tensor"),
        P("tensor", None),
        P(),
    )
    out_specs = (
        P(("dp", "tensor"), None),
        P(("dp", "tensor"), None),
        P(),
        P("dp", None, "tensor"),
        P(None, "tensor"),
        P("tensor", "dp"),
        P(),
        P(),
        P(None, "dp", None, "tensor"),
        P(None, "tensor", "dp"),
        P("dp", None, "tensor"),
        P("tensor", "dp"),
        P(),
    )
    return jax.shard_map(
        on_device, mesh=mesh, in_specs=in_specs, out_specs=out_specs, check_vma=False
    )
```

time: 1000 us -> 905 us (0.905)
  local copies, waits for them, and re-layouts: 140 us -> 75.7 us
  other arithmetic: 87.6 us -> 27.2 us
  Pallas kernels: 585 us -> 643 us
  matrix products: 57.6 us -> 9.72 us
  waiting for transfers between devices: 109 us -> 128 us
    all_gather x2, waiting for transfers between devices: 22.8 us -> 121 us  [the longest x1 81.3 us: on_device(): lax.all_gather((unit_two * gain_two).astype(bf), 'tensor', axis=0, tiled=...]
    reduce_scatter x1, waiting for transfers between devices: 79 us -> 0.02 us  [on_device(): lax.psum_scatter(branch_partial, 'tensor', scatter_dimension=0, tiled=True)]
    dot_general x16 -> x2, matrix products: 57.6 us -> 9.72 us  [the longest x1 5.36 us: on_device(): lax.dot_general(d_one, out_weight, NT, preferred_element_type=jnp.float32)]
    concatenate x7 -> x3, other arithmetic: 47.6 us -> 2.76 us  [the longest x1 1.6 us: on_device(): jnp.concatenate([router_part[:experts + 1], norm_one_part / gain_one[None...]
    pallas_call x6 -> x10, Pallas kernels: 314 us -> 355 us  [the longest x5 288 us: weight_grad_scatter_kernel(): pl.pallas_call(functools.partial(rs_body, nc, cut), grid=(nc + L,), in_sp...]
    slice x14 -> x2, local copies, waits for them, and re-layouts: 29.8 us -> 2.39 us  [the longest x1 1.57 us: on_device(): sums[experts]]
    unnamed x128 -> x68, local copies, waits for them, and re-layouts: 64.9 us -> 56.2 us
  transfers between devices with their start and end apart: 7 -> 7, of which waited for: 3 -> 3; matrix products, arithmetic and copies ran while one was open for 14% -> 7% of each run, Pallas kernels for 44% -> 49%
where the time goes in v2:
time: 905 us; the launch traced here: 900 us
  Pallas kernels  643 us (71%)
  waiting for transfers between devices  128 us (14%)
  local copies, waits for them, and re-layouts  75.7 us (8%)
  other arithmetic  27.2 us (3%)
  between operations  15.5 us (2%)
  matrix products  9.72 us (1%)
    pallas_call x5, Pallas kernels, weight_grad_scatter_kernel(): pl.pallas_call(functools.partial(rs_body, nc, cut), grid=(nc + L,), in_sp...  288 us
    pallas_call x1, Pallas kernels, ffn(): pl.pallas_call(functools.partial(ffn_body, experts), grid=(chunks,), in_s...  151 us
    pallas_call x1, Pallas kernels, gather_rows(): pl.pallas_call(gather_body, in_specs=[pl.BlockSpec(memory_space=pl.ANY)],...  138 us
    all_gather x1, waiting for transfers between devices, on_device(): lax.all_gather((unit_two * gain_two).astype(bf), 'tensor', axis=0, tiled=...  81.3 us
    unnamed x68, local copies, waits for them, and re-layouts  56.2 us
    all_gather x1, waiting for transfers between devices, on_device(): lax.all_gather((unit_one * gain_one).astype(bf), 'tensor', axis=0, tiled=...  39.3 us
    pallas_call x1, Pallas kernels, attend_back(): pl.pallas_call(functools.partial(attend_back_body, rows), grid=(cols // H...  18.3 us
  transfers between devices with their start and end apart: 7, of which 3 were waited for; matrix products, arithmetic and copies ran while one was open for 7% of the time, Pallas kernels for 49%

profile of v2, /device:TPU:0, one launch (start us, length us, event | category | flops | bytes accessed | tf_op | source)
XLA Modules:
  0.0 900.3 jit_solution(3809331310277235742)
XLA Ops:
  13.3 28.8 %copy.31 = bf16[2048,2,1408]{0,2,1:T(8,128)(2,1)} copy(bf16[2048,2,1408]{2,1,0:T(2,128)(2,1)} %param.27) | data formatting | bytes 23068672 | tf_op args[12]
  42.2 10.1 %copy.32 = bf16[4,2,352,2048]{3,2,1,0:T(8,128)(2,1)} copy(bf16[4,2,352,2048]{3,2,0,1:T(8,128)(2,1)} %bitcast.45) | data formatting | bytes 23068672 | tf_op jit(solution)/shard_map/transpose | solution.py:738
  56.9 39.3 %all-gather.4.cloned.1.call-done.x_ref.b_ref = bf16[1024,2048]{1,0:T(8,128)(2,1)} async-done(((bf16[256,2048]{1,0:T(8,128)(2,1)}), bf16[1024,2048]{1,0:T(8,128)(2,1)}) %all-gather.4.cloned.1.call-update) | async-done | bytes 4194320 | tf_op jit(solution)/shard_map/all_gather | solution.py:731
  96.2 11.3 %project_qkv.1.q_ref.k_ref.v_ref = bf16[3,1024,512]{2,1,0:T(8,128)(2,1)S(1)} custom-call(bf16[1024,2048]{1,0:T(8,128)(2,1)} %all-gather.4.cloned.1.call-done.x_ref.b_ref, bf16[3,2048,512]{2,1,0:T(8,128)(2,1)} %bitcast.59, bf16[3,1,512]{2,1,0:T(2,128)(2,1)S(1)} %copy.33.bias_ref, f32[1024,128]{1,0:T(8,128)S(1)} %get-tuple-element.55.cos_ref, ...), custom_call_target="tpu_custom_call" | custom-call | flops 6442450944 | bytes 10485760 | tf_op jit(solution)/shard_map/project_qkv/pallas_call | solution.py:350
  107.5 9.9 %attend.1 = (bf16[1024,512]{1,0:T(8,128)(2,1)S(1)}, bf16[512,1024]{1,0:T(8,128)(2,1)S(1)}) custom-call(s32[1]{0:T(128)} %copy.41.length_ref, bf16[3,1024,512]{2,1,0:T(8,128)(2,1)S(1)} %project_qkv.1.q_ref.k_ref.v_ref, bf16[3,1024,512]{2,1,0:T(8,128)(2,1)S(1)} %project_qkv.1.q_ref.k_ref.v_ref, bf16[3,1024,512]{2,1,0:T(8,128)(2,1)S(1)} %project_qkv.1.q_ref.k_ref.v_ref), custom_call_target="tpu_custom_call" | custom-call | flops 2147483648 | bytes 5242880 | tf_op jit(solution)/shard_map/attend/pallas_call | solution.py:394
  118.5 4.4 convolution_convert_fusion
  123.5 138.0 %gather_rows.1.d_ref.b_ref = bf16[1024,2048]{1,0:T(8,128)(2,1)} custom-call(bf16[256,2048]{1,0:T(8,128)(2,1)} %multiply_convert_fusion.2.own_ref), custom_call_target="tpu_custom_call" | custom-call | bytes 8388608 | tf_op jit(solution)/shard_map/gather_rows/pallas_call | solution.py:609
  265.1 81.3 %all-gather.6.cloned.1.call-done.x_ref.b_ref = bf16[1024,2048]{1,0:T(8,128)(2,1)} async-done(((bf16[256,2048]{1,0:T(8,128)(2,1)}), bf16[1024,2048]{1,0:T(8,128)(2,1)}) %all-gather.6.cloned.1.call-update) | async-done | bytes 4194320 | tf_op jit(solution)/shard_map/all_gather | solution.py:765
  346.4 150.8 %ffn.1 = (bf16[12,704,1024]{2,1,0:T(8,128)(2,1)}, bf16[12,352,1024]{2,1,0:T(8,128)(2,1)}, bf16[1024,2048]{1,0:T(8,128)(2,1)}, bf16[1024,2048]{1,0:T(8,128)(2,1)}, f32[16,2048]{1,0:T(8,128)}, /*index=5*/f32[1,2048]{1,0:T(1,128)}) custom-call(bf16[1024,2048]{1,0:T(8,128)(2,1)} %all-gather.6.cloned.1.call-done.x_ref.b_ref, ...), custom_call_target="tpu_custom_call" | custom-call | flops 106300440576 | bytes 120061952 | tf_op jit(solution)/shard_map/ffn/pallas_call | solution.py:293
  497.3 79.1 %down_grads.1 = (f32[2816,256]{1,0:T(8,128)S(1)}, f32[1408,256]{1,0:T(8,128)S(1)}) custom-call(bf16[4224,1024]{1,0:T(8,128)(2,1)} %bitcast.65, bf16[1024,2048]{1,0:T(8,128)(2,1)} %gather_rows.1.d_ref.b_ref), custom_call_target="tpu_custom_call" | custom-call | flops 17716740096 | bytes 17170432 | tf_op jit(solution)/shard_map/down_grads/pallas_call | solution.py:152
  580.3 3.3 multiply_convert_fusion
  585.9 101.2 %expert_in_grads.1 = (f32[5632,256]{1,0:T(8,128)}, f32[352,256]{1,0:T(8,128)}) custom-call(bf16[8448,1024]{1,0:T(8,128)(2,1)} %bitcast.63, bf16[1024,2048]{1,0:T(8,128)(2,1)S(1)} %copy-done.9), custom_call_target="tpu_custom_call" | custom-call | flops 23622320128 | bytes 21495808 | tf_op jit(solution)/shard_map/expert_in_grads/pallas_call | solution.py:152
  687.2 5.4 convolution_convert_fusion.1.dm_ref
  692.6 18.3 %attend_back.1 = (bf16[3,1024,512]{2,1,0:T(8,128)(2,1)S(1)}, bf16[3,512,1024]{2,1,0:T(8,128)(2,1)S(1)}, f32[3,1,512]{2,1,0:T(1,128)S(1)}) custom-call(s32[1]{0:T(128)} %copy.41.length_ref, bf16[3,1024,512]{2,1,0:T(8,128)(2,1)S(1)} %copy-done.1, bf16[3,1024,512]{2,1,0:T(8,128)(2,1)S(1)} %copy-done.1, bf16[3,1024,512]{2,1,0:T(8,128)(2,1)S(1)} %copy-done.1, ...), custom_call_target="tpu_custom_call" | custom-call | flops 5368709120 | bytes 10485760 | tf_op jit(solution)/shard_map/attend_back/pallas_call | solution.py:459
  712.6 10.3 %qkv_back.1 = (bf16[1024,2048]{1,0:T(8,128)(2,1)}, f32[1,2048]{1,0:T(1,128)S(1)}) custom-call(bf16[3,1024,512]{2,1,0:T(8,128)(2,1)S(1)} %get-tuple-element.74.d_ref, bf16[3,2048,512]{2,1,0:T(8,128)(2,1)} %bitcast.60, bf16[1024,2048]{1,0:T(8,128)(2,1)} %all-gather.4.cloned.1.call-done.x_ref.b_ref), custom_call_target="tpu_custom_call" | custom-call | flops 6442450944 | bytes 14680064 | tf_op jit(solution)/shard_map/qkv_back/pallas_call | solution.py:495
  723.7 56.3 %shared_in_grads.1 = (f32[2816,256]{1,0:T(8,128)S(1)}, f32[352,256]{1,0:T(8,128)}) custom-call(bf16[8448,1024]{1,0:T(8,128)(2,1)} %bitcast.64, bf16[1024,2048]{1,0:T(8,128)(2,1)} %all-gather.6.cloned.1.call-done.x_ref.b_ref), custom_call_target="tpu_custom_call" | custom-call | flops 11811160064 | bytes 12845056 | tf_op jit(solution)/shard_map/shared_in_grads/pallas_call | solution.py:152
  781.8 5.5 copy.36
  790.7 15.4 %mix_grads.1 = (f32[512,256]{1,0:T(8,128)S(1)}, f32[256,256]{1,0:T(8,128)}) custom-call(bf16[512,1024]{1,0:T(8,128)(2,1)S(1)} %copy-done.12, bf16[1024,2048]{1,0:T(8,128)(2,1)S(1)} %copy-done.10), custom_call_target="tpu_custom_call" | custom-call | flops 2147483648 | bytes 5767168 | tf_op jit(solution)/shard_map/mix_grads/pallas_call | solution.py:152
  806.1 35.6 %qkv_grads.1 = (f32[1536,256]{1,0:T(8,128)S(1)}, f32[384,256]{1,0:T(8,128)}) custom-call(bf16[1536,1024]{1,0:T(8,128)(2,1)S(1)} %bitcast.44, bf16[1024,2048]{1,0:T(8,128)(2,1)} %all-gather.4.cloned.1.call-done.x_ref.b_ref), custom_call_target="tpu_custom_call" | custom-call | flops 6442450944 | bytes 8912896 | tf_op jit(solution)/shard_map/qkv_grads/pallas_call | solution.py:152
  842.9 3.0 copy.34
  847.6 17.2 %small_sums.1 = f32[12,2048]{1,0:T(8,128)} custom-call(f32[12,2048]{1,0:T(8,128)} %select_maximum_fusion.part_ref), custom_call_target="tpu_custom_call" | custom-call | tf_op jit(solution)/shard_map/small_sums/pallas_call | solution.py:680
  871.4 6.9 reduce-scatter.9.cloned.1.call-done
  878.3 4.9 fusion.7
  884.0 5.7 copy.43
  (114 shorter events, 42.6 us)
Async XLA Ops:
  7.2 6.1 copy-start.29
  7.2 6.1 copy-start.27
  7.2 89.0 %all-gather.4.cloned.1.call-start = ((), (), s32[]{:S(2)}) async-start(), calls=%async_computation.4 | async-start | bytes 5242880 | tf_op jit(solution)/shard_map/all_gather | solution.py:731
  12.6 249.0 %reduce-scatter.5.cloned.1.call-start = ((), (), s32[]{:S(2)}) async-start(), calls=%async_computation.5 | async-start | bytes 5242880 | tf_op jit(solution)/shard_map/reduce_scatter | solution.py:759
  52.4 3.1 copy-start.20
  54.7 52.8 %copy-start.5 = (f32[1024,128]{1,0:T(8,128)}, f32[1024,128]{1,0:T(8,128)S(1)}, u32[]{:S(2)}) copy-start(f32[1024,128]{1,0:T(8,128)S(1)} %get-tuple-element.55.cos_ref) | copy-start | bytes 1572868
  54.7 52.8 %copy-start.7 = (f32[1024,128]{1,0:T(8,128)}, f32[1024,128]{1,0:T(8,128)S(1)}, u32[]{:S(2)}) copy-start(f32[1024,128]{1,0:T(8,128)S(1)} %get-tuple-element.56.sin_ref) | copy-start | bytes 1572868
  107.5 10.0 %copy-start = (bf16[3,1024,512]{2,1,0:T(8,128)(2,1)}, bf16[3,1024,512]{2,1,0:T(8,128)(2,1)S(1)}, u32[]{:S(2)}) copy-start(bf16[3,1024,512]{2,1,0:T(8,128)(2,1)S(1)} %project_qkv.1.q_ref.k_ref.v_ref) | copy-start | bytes 9437188
  107.5 11.0 %copy-start.30 = (bf16[512,2048]{1,0:T(8,128)(2,1)S(1)}, bf16[512,2048]{1,0:T(8,128)(2,1)}, u32[]{:S(2)}) copy-start(bf16[512,2048]{1,0:T(8,128)(2,1)} %param.22) | copy-start | bytes 6291460
  122.9 223.5 %all-gather.6.cloned.1.call-start = ((), (), s32[]{:S(2)}) async-start(), calls=%async_computation.6 | async-start | bytes 5242880 | tf_op jit(solution)/shard_map/all_gather | solution.py:765
  123.5 138.1 %copy-start.15 = (bf16[256,2048]{1,0:T(8,128)(2,1)S(1)}, bf16[256,2048]{1,0:T(8,128)(2,1)}, u32[]{:S(2)}) copy-start(bf16[256,2048]{1,0:T(8,128)(2,1)} %param.15) | copy-start | bytes 3145732
  265.0 312.5 %reduce-scatter.7.cloned.1.call-start = ((), (), s32[]{:S(2)}) async-start(), calls=%async_computation.7 | async-start | bytes 5242880 | tf_op jit(solution)/shard_map/reduce_scatter | solution.py:771
  497.3 189.9 %all-gather.8.cloned.1.call-start = ((), (), s32[]{:S(2)}) async-start(), calls=%async_computation.8 | async-start | bytes 5242880 | tf_op jit(solution)/shard_map/all_gather | solution.py:780
  577.5 2.8 copy-start.16
  577.5 2.8 copy-start.18
  577.5 2.8 copy-start.19
  583.7 285.6 %reduce-scatter.11.cloned.1.call-start = ((), (), s32[]{:S(2)}) async-start(), calls=%async_computation.10 | async-start | bytes 5242880 | tf_op jit(solution)/shard_map/reduce_scatter | solution.py:795
  687.1 5.4 copy-start.1
  687.1 5.4 copy-start.6
  687.2 5.4 copy-start.8
  722.9 155.4 %reduce-scatter.9.cloned.1.call-start = ((), (), s32[]{:S(2)}) async-start(), calls=%async_computation.9 | async-start | bytes 5242880 | tf_op jit(solution)/shard_map/reduce_scatter | solution.py:788
  790.7 15.4 %copy-start.14 = (bf16[3,512,1024]{2,1,0:T(8,128)(2,1)S(1)}, bf16[3,512,1024]{2,1,0:T(8,128)(2,1)}, u32[]{:S(2)}) copy-start(bf16[3,512,1024]{2,1,0:T(8,128)(2,1)} %copy-done.13) | copy-start | bytes 9437188
  842.9 3.0 copy-start.22
  842.9 26.3 %copy-start.25 = (f32[256]{0:T(256)S(1)}, f32[256]{0:T(256)}, u32[]{:S(2)}) copy-start(f32[256]{0:T(256)} %copy-done.24) | copy-start | bytes 3076
  (14 other events, 19.9 us)
Sparse Core Ops, SparseCore 0:
  12.7 83.4 all-gather.3
  123.0 108.9 reduce-scatter.4
  265.1 81.2 all-gather.5
  497.4 75.2 reduce-scatter.6
  583.8 78.4 all-gather.7
  723.0 74.4 reduce-scatter.10
  800.0 78.2 reduce-scatter.8

commit v3 on v2

--- a/solution.py
+++ b/solution.py
@@ -10,6 +10,7 @@
 HEAD_DIM = 128
 MESH = pl.DeviceIdType.MESH
 LA, LB, LC = 1, 2, 2
+FFN_LAGS = (1, 1, 1)
 MIB = 2**20
 
 
@@ -36,10 +37,23 @@
     return inverse * (d_unit - unit_rows * jnp.mean(d_unit * unit_rows, axis=-1, keepdims=True))
 
 
-def rs_body(nc, cut, a_ref, b_ref, o_ref, o2_ref, own, sa, ra, kt, s1, r1, ku, s2, r2, sem_sa, sem_ra, sem_s1, sem_r1, sem_s2, sem_r2):
-    i = pl.program_id(0)
-    r, w = o_ref.shape
-    hr = r // 2
+def scatter_scratch(r, w):
+    f32, bf = jnp.float32, jnp.bfloat16
+    dma = pltpu.SemaphoreType.DMA
+    h = r // 2
+    return [
+        pltpu.VMEM((2, 4, r, w), f32), pltpu.VMEM((2, 4, r, w), bf), pltpu.VMEM((3, 4, r, w), bf),
+        pltpu.VMEM((3, 2, 2, h, w), f32), pltpu.VMEM((3, 2, 2, h, w), bf), pltpu.VMEM((6, 2, 2, h, w), bf),
+        pltpu.VMEM((3, 2, h, w), f32), pltpu.VMEM((2, 2, h, w), bf), pltpu.VMEM((6, 2, h, w), bf),
+        dma((2,)), dma((3,)), dma((3, 2)), dma((6, 2)), dma((2, 2)), dma((6, 2)),
+    ]
+
+
+def scatter_steps(i, nc, lags, w, scratch, store):
+    own, sa, ra, kt, s1, r1, ku, s2, r2, sem_sa, sem_ra, sem_s1, sem_r1, sem_s2, sem_r2 = scratch
+    la, lb, lc = lags
+    keep_1 = min(3, lb + lc)
+    hr = own.shape[2] // 2
     dp = lax.axis_index("dp")
     k = dp % 2
     x = (dp // 2) % 2
@@ -51,17 +65,20 @@
     def copy_a(c):
         return pltpu.make_async_remote_copy(
             src_ref=sa.at[c % 2], dst_ref=ra.at[c % 3], send_sem=sem_sa.at[c % 2], recv_sem=sem_ra.at[c % 3],
-            device_id={"dp": core_peer}, device_id_type=MESH)
+            device_id={"dp": core_peer}, device_id_type=MESH,
+        )
 
     def copy_1(c, half):
         return pltpu.make_async_remote_copy(
             src_ref=s1.at[c % 3, half], dst_ref=r1.at[c % 6, half], send_sem=sem_s1.at[c % 3, half],
-            recv_sem=sem_r1.at[c % 6, half], device_id={"dp": y_peer if half else x_peer}, device_id_type=MESH)
+            recv_sem=sem_r1.at[c % 6, half], device_id={"dp": y_peer if half else x_peer}, device_id_type=MESH,
+        )
 
     def copy_2(c, half):
         return pltpu.make_async_remote_copy(
             src_ref=s2.at[c % 2, half], dst_ref=r2.at[c % 6, half], send_sem=sem_s2.at[c % 2, half],
-            recv_sem=sem_r2.at[c % 6, half], device_id={"dp": x_peer if half else y_peer}, device_id_type=MESH)
+            recv_sem=sem_r2.at[c % 6, half], device_id={"dp": x_peer if half else y_peer}, device_id_type=MESH,
+        )
 
     @pl.when(i == 0)
     def _():
@@ -70,115 +87,144 @@
             pl.semaphore_signal(barrier, inc=1, device_id={"dp": peer}, device_id_type=MESH)
         pl.semaphore_wait(barrier, 3)
 
-    @pl.when(jnp.logical_and(i >= LA + 3, i < nc + LA + 3))
-    def _():
-        copy_1(i - LA - 3, 0).wait_send()
-        copy_1(i - LA - 3, 1).wait_send()
-
-    @pl.when(jnp.logical_and(i >= LA, i < nc + LA))
-    def _():
-        c = i - LA
+    @pl.when((i >= la + keep_1) & (i < nc + la + keep_1))
+    def _():
+        copy_1(i - la - keep_1, 0).wait_send()
+        copy_1(i - la - keep_1, 1).wait_send()
+
+    @pl.when((i >= la) & (i < nc + la))
+    def _():
+        c = i - la
         copy_a(c).wait_recv()
         for half in range(2):
             rows = slice(half * hr, half * hr + hr)
             keep, other = (1, 2) if half else (2, 1)
+
             def total(role):
                 return own[c % 2, role, rows, :] + ra[c % 3, role, rows, :].astype(jnp.float32)
+
             s1[c % 3, half, 0] = total(other).astype(jnp.bfloat16)
             s1[c % 3, half, 1] = total(3).astype(jnp.bfloat16)
             copy_1(c, half).start()
             kt[c % 3, half, 0] = total(0)
             kt[c % 3, half, 1] = total(keep)
 
-    @pl.when(jnp.logical_and(i >= LA + LB, i < nc + LA + LB))
-    def _():
-        c = i - LA - LB
+    @pl.when((i >= la + lb) & (i < nc + la + lb))
+    def _():
+        c = i - la - lb
+
         @pl.when(c >= 2)
         def _():
             copy_2(c - 2, 0).wait_send()
             copy_2(c - 2, 1).wait_send()
+
         for half in range(2):
             copy_1(c, half).wait_recv()
             s2[c % 2, half] = (kt[c % 3, half, 1] + r1[c % 6, half, 1].astype(jnp.float32)).astype(jnp.bfloat16)
             copy_2(c, half).start()
             ku[c % 3, half] = kt[c % 3, half, 0] + r1[c % 6, half, 0].astype(jnp.float32)
 
-    @pl.when(i >= LA + LB + LC)
-    def _():
-        c = i - LA - LB - LC
+    @pl.when(i >= la + lb + lc)
+    def _():
+        c = i - la - lb - lc
         for half in range(2):
-            rows = slice(half * hr, half * hr + hr)
             copy_2(c, half).wait_recv()
-            result = ku[c % 3, half] + r2[c % 6, half].astype(jnp.float32)
-
-            @pl.when(c < cut)
-            def _():
-                o_ref[rows, :] = result
-
-            @pl.when(c >= cut)
-            def _():
-                o2_ref[rows, :] = result
+            store(c, slice(half * hr, half * hr + hr), ku[c % 3, half] + r2[c % 6, half].astype(jnp.float32))
 
         @pl.when(c >= nc - 2)
         def _():
             copy_2(c, 0).wait_send()
             copy_2(c, 1).wait_send()
 
-    @pl.when(jnp.logical_and(i >= 2, i < nc + 2))
+    @pl.when((i >= 2) & (i < nc + 2))
     def _():
         copy_a(i - 2).wait_send()
 
-    @pl.when(i < nc)
-    def _():
-        a = a_ref[...]
+    def send(product):
         targets = (y * 4 + x * 2, y * 4 + (1 - x) * 2, (1 - y) * 4 + x * 2, (1 - y) * 4 + (1 - x) * 2)
+
+        def cols(role, core):
+            return pl.ds(pl.multiple_of((targets[role] + core) * w, w), w)
+
         for role in range(4):
-            cols = pl.ds(pl.multiple_of((targets[role] + 1 - k) * w, w), w)
-            sa[i % 2, role] = jnp.dot(a, b_ref[:, cols], preferred_element_type=jnp.float32).astype(jnp.bfloat16)
+            sa[i % 2, role] = product(cols(role, 1 - k)).astype(jnp.bfloat16)
         copy_a(i).start()
         for role in range(4):
-            cols = pl.ds(pl.multiple_of((targets[role] + k) * w, w), w)
-            own[i % 2, role] = jnp.dot(a, b_ref[:, cols], preferred_element_type=jnp.float32)
-
-def weight_grad_scatter_kernel(a, b, r, cid, name, first, count, cut):
-    T = a.shape[1]
-    R = count * r
-    D = b.shape[1]
+            own[i % 2, role] = product(cols(role, k))
+
+    return send
+
+
+def rs_body(nc, cut, pairs, *refs):
+    a_refs, b_refs = refs[:pairs], refs[pairs : 2 * pairs]
+    o_ref, o2_ref = refs[2 * pairs : 2 * pairs + 2]
+    i = pl.program_id(0)
+
+    def store(c, rows, result):
+        @pl.when(c < cut)
+        def _():
+            o_ref[rows, :] = result
+
+        @pl.when(c >= cut)
+        def _():
+            o2_ref[rows, :] = result
+
+    send = scatter_steps(i, nc, (LA, LB, LC), o_ref.shape[1], refs[2 * pairs + 2 :], store)
+
+    @pl.when(i < nc)
+    def _():
+        def product(cols):
+            total = jnp.dot(a_refs[0][...], b_refs[0][:, cols], preferred_element_type=jnp.float32)
+            for a_ref, b_ref in zip(a_refs[1:], b_refs[1:]):
+                total += jnp.dot(a_ref[...], b_ref[:, cols], preferred_element_type=jnp.float32)
+            return total
+
+        send(product)
+
+
+def scatter_outs(nc, cut, lag, r, w):
+    rest = max(nc - cut, 1)
+    specs = [
+        pl.BlockSpec((r, w), lambda i: (jnp.clip(i - lag, 0, cut - 1), 0)),
+        pl.BlockSpec((r, w), lambda i: (jnp.clip(i - lag - cut, 0, rest - 1), 0)),
+    ]
+    return specs, [jax.ShapeDtypeStruct((n * r, w), jnp.float32) for n in (cut, rest)]
+
+
+def weight_grad_scatter_kernel(a_list, b_list, r, cid, name, first, count, cut):
+    D = b_list[0].shape[1]
+    T = sum(b.shape[0] for b in b_list)
     w = D // 8
-    nc = count
-    L = LA + LB + LC
-    f32, bf = jnp.float32, jnp.bfloat16
-    dma = pltpu.SemaphoreType.DMA
+    lag = LA + LB + LC
+    out_specs, out_shape = scatter_outs(count, cut, lag, r, w)
     return pl.pallas_call(
-        functools.partial(rs_body, nc, cut),
-        grid=(nc + L,),
-        in_specs=[pl.BlockSpec((r, T), lambda i: (jnp.minimum(i, nc - 1) + first, 0)),
-                  pl.BlockSpec((T, D), lambda i: (0, 0), pipeline_mode=pl.Buffered(1))],
-        out_specs=[
-            pl.BlockSpec((r, w), lambda i: (jnp.clip(i - L, 0, cut - 1), 0)),
-            pl.BlockSpec((r, w), lambda i: (jnp.clip(i - L - cut, 0, max(nc - cut, 1) - 1), 0)),
-        ],
-        out_shape=[
-            jax.ShapeDtypeStruct((cut * r, w), f32),
-            jax.ShapeDtypeStruct((max(nc - cut, 1) * r, w), f32),
-        ],
-        scratch_shapes=[
-            pltpu.VMEM((2, 4, r, w), f32), pltpu.VMEM((2, 4, r, w), bf), pltpu.VMEM((3, 4, r, w), bf),
-            pltpu.VMEM((3, 2, 2, r // 2, w), f32), pltpu.VMEM((3, 2, 2, r // 2, w), bf), pltpu.VMEM((6, 2, 2, r // 2, w), bf),
-            pltpu.VMEM((3, 2, r // 2, w), f32), pltpu.VMEM((2, 2, r // 2, w), bf), pltpu.VMEM((6, 2, r // 2, w), bf),
-            dma((2,)), dma((3,)), dma((3, 2)), dma((6, 2)), dma((2, 2)), dma((6, 2))],
-        compiler_params=pltpu.CompilerParams(vmem_limit_bytes=48 * 2**20, collective_id=cid, has_side_effects=True),
-        cost_estimate=pl.CostEstimate(flops=2 * R * T * D, bytes_accessed=2 * R * T + 2 * T * D + 4 * R * w, transcendentals=0),
-        name=name)(a, b)
+        functools.partial(rs_body, count, cut, len(a_list)),
+        grid=(count + lag,),
+        in_specs=[
+            *[pl.BlockSpec((r, a.shape[1]), lambda i: (jnp.minimum(i, count - 1) + first, 0)) for a in a_list],
+            *[pl.BlockSpec(b.shape, lambda i: (0, 0), pipeline_mode=pl.Buffered(1)) for b in b_list],
+        ],
+        out_specs=out_specs,
+        out_shape=out_shape,
+        scratch_shapes=scatter_scratch(r, w),
+        compiler_params=pltpu.CompilerParams(vmem_limit_bytes=48 * MIB, collective_id=cid, has_side_effects=True),
+        cost_estimate=pl.CostEstimate(
+            flops=2 * count * r * T * D, bytes_accessed=2 * count * r * T + 2 * T * D + 4 * count * r * w, transcendentals=0
+        ),
+        name=name,
+    )(*a_list, *b_list)
 
 
 def ffn_body(
-    experts, x_ref, d_ref, routes_ref, rw_ref, ei_ref, si_ref, eo_ref, so_ref,
-    dgu_ref, s_ref, dn_ref, bt_ref, rg_ref, np_ref,
-    dn_acc, bt_acc, probs_ref, w_ref, ds_ref, wi_buf, wd_buf, sem,
+    experts, chunks, scatter,
+    x_ref, d_ref, routes_ref, rw_ref, ei_ref, si_ref, eo_ref, so_ref, *refs,
 ):
+    if scatter:
+        s_other_ref, d_other_ref, dgu_ref, dn_ref, bt_ref, rg_ref, np_ref, og_ref, og2_ref, *refs = refs
+    else:
+        dgu_ref, dn_ref, bt_ref, rg_ref, np_ref, s_ref, *refs = refs
+    dn_acc, bt_acc, probs_ref, w_ref, ds_ref, wi_buf, wd_buf, sem, *scratch = refs
     c = pl.program_id(0)
-    chunks = pl.num_programs(0)
     h = eo_ref.shape[1]
     slots, width = x_ref.shape
 
@@ -223,34 +269,57 @@
         dn_acc[...] = jnp.zeros_like(dn_acc)
         bt_acc[...] = jnp.zeros_like(bt_acc)
 
-    row = pl.ds(jnp.minimum(c, experts), 1)
-    slot = c % 2
-    pltpu.make_async_copy(ei_ref.at[0], wi_buf.at[slot], sem.at[0, slot]).wait()
-    pltpu.make_async_copy(eo_ref.at[0], wd_buf.at[slot], sem.at[1, slot]).wait()
-    wi = wi_buf.at[slot]
-    wd = wd_buf.at[slot]
-    x = x_ref[...]
-    g = lax.dot_general(wi[:h], x, NT, preferred_element_type=jnp.float32)
-    u = lax.dot_general(wi[h:], x, NT, preferred_element_type=jnp.float32)
-    p = lax.dot_general(wd[...], d_ref[...], NT, preferred_element_type=jnp.float32)
-    w = w_ref[row, :]
-    sg = 1.0 / (1.0 + jnp.exp(-g))
-    si = g * sg
-    inner = (si * u).astype(jnp.bfloat16).astype(jnp.float32)
-    s = (w * inner).astype(jnp.bfloat16)
-    s_ref[0] = s
-    ds_ref[row, :] += jnp.sum(p * inner, axis=0, keepdims=True)
-    di = w * p
-    dg = (di * u * sg * (1.0 + g * (1.0 - sg))).astype(jnp.bfloat16)
-    du = (di * si).astype(jnp.bfloat16)
-    dgu_ref[0, :h] = dg
-    dgu_ref[0, h:] = du
-    dgu = jnp.concatenate([dg, du], axis=0)
+    if scatter:
+        def store(chunk, rows, result):
+            @pl.when(chunk < experts)
+            def _():
+                og_ref[rows, :] = result
+
+            @pl.when(chunk >= experts)
+            def _():
+                og2_ref[rows, :] = result
+
+        send = scatter_steps(c, chunks, FFN_LAGS, og_ref.shape[1], scratch, store)
+
     block = 512
-    for n in range(0, width, block):
-        cols = slice(n, n + block)
-        dn_acc[:, cols] += lax.dot_general(dgu, wi[:, cols], TN, preferred_element_type=jnp.float32)
-        bt_acc[:, cols] += lax.dot_general(s, wd[:, cols], TN, preferred_element_type=jnp.float32)
+
+    @pl.when(c < chunks)
+    def _():
+        row = pl.ds(jnp.minimum(c, experts), 1)
+        slot = c % 2
+        pltpu.make_async_copy(ei_ref.at[0], wi_buf.at[slot], sem.at[0, slot]).wait()
+        pltpu.make_async_copy(eo_ref.at[0], wd_buf.at[slot], sem.at[1, slot]).wait()
+        wi = wi_buf.at[slot]
+        wd = wd_buf.at[slot]
+        x = x_ref[...]
+        g = lax.dot_general(wi[:h], x, NT, preferred_element_type=jnp.float32)
+        u = lax.dot_general(wi[h:], x, NT, preferred_element_type=jnp.float32)
+        p = lax.dot_general(wd[...], d_ref[...], NT, preferred_element_type=jnp.float32)
+        w = w_ref[row, :]
+        sg = 1.0 / (1.0 + jnp.exp(-g))
+        si = g * sg
+        inner = (si * u).astype(jnp.bfloat16).astype(jnp.float32)
+        s = (w * inner).astype(jnp.bfloat16)
+        ds_ref[row, :] += jnp.sum(p * inner, axis=0, keepdims=True)
+        di = w * p
+        dg = (di * u * sg * (1.0 + g * (1.0 - sg))).astype(jnp.bfloat16)
+        du = (di * si).astype(jnp.bfloat16)
+        dgu_ref[0, :h] = dg
+        dgu_ref[0, h:] = du
+        dgu = jnp.concatenate([dg, du], axis=0)
+        if scatter:
+            def product(cols):
+                return jnp.dot(s, d_ref[:, cols], preferred_element_type=jnp.float32) + jnp.dot(
+                    s_other_ref[0], d_other_ref[:, cols], preferred_element_type=jnp.float32
+                )
+
+            send(product)
+        else:
+            s_ref[0] = s
+        for n in range(0, width, block):
+            cols = slice(n, n + block)
+            dn_acc[:, cols] += lax.dot_general(dgu, wi[:, cols], TN, preferred_element_type=jnp.float32)
+            bt_acc[:, cols] += lax.dot_general(s, wd[:, cols], TN, preferred_element_type=jnp.float32)
 
     @pl.when(c == chunks - 1)
     def _():
@@ -275,7 +344,7 @@
         bt_ref[...] = bt_acc[...].astype(bt_ref.dtype)
 
 
-def ffn(x, d_two, routes_t, router_rows, ei, si, eo, so):
+def ffn(x, d_two, routes_t, router_rows, ei, si, eo, so, other=None):
     experts, h2, width = ei.shape
     chunks = experts + si.shape[0]
     h = h2 // 2
@@ -283,41 +352,61 @@
     rows = router_rows.shape[0]
     bf, f32 = jnp.bfloat16, jnp.float32
     anywhere = pl.BlockSpec(memory_space=pl.ANY)
+    scatter = other is not None
 
     def whole(shape):
         return pl.BlockSpec(shape, lambda c: (0,) * len(shape), pipeline_mode=pl.Buffered(1))
 
     def chunk(shape):
-        return pl.BlockSpec((1, *shape), lambda c: (c, 0, 0))
-
+        return pl.BlockSpec((1, *shape), lambda c: (jnp.minimum(c, chunks - 1), 0, 0))
+
+    in_specs = [
+        whole((slots, width)), whole((slots, width)), whole(routes_t.shape), whole((rows, width)),
+        anywhere, anywhere, anywhere, anywhere,
+    ]
+    out_specs = [chunk((h2, slots)), whole((slots, width)), whole((slots, width)), whole((rows, width)), whole((1, width))]
+    out_shape = [
+        jax.ShapeDtypeStruct((chunks, h2, slots), bf), jax.ShapeDtypeStruct((slots, width), bf),
+        jax.ShapeDtypeStruct((slots, width), bf), jax.ShapeDtypeStruct((rows, width), f32),
+        jax.ShapeDtypeStruct((1, width), f32),
+    ]
+    scratch = [
+        pltpu.VMEM((slots, width), f32), pltpu.VMEM((slots, width), f32),
+        pltpu.VMEM((experts, slots), f32), pltpu.VMEM((rows, slots), f32), pltpu.VMEM((rows, slots), f32),
+        pltpu.VMEM((2, h2, width), bf), pltpu.VMEM((2, h, width), bf), pltpu.SemaphoreType.DMA((2, 2)),
+    ]
+    args = [x, d_two, routes_t, router_rows, ei, si, eo, so]
+    if scatter:
+        s_other, d_other = other
+        in_specs += [chunk((h, s_other.shape[2])), whole(d_other.shape)]
+        args += [s_other, d_other]
+        w = width // 8
+        lag = sum(FFN_LAGS)
+        specs, shapes = scatter_outs(chunks, experts, lag, h, w)
+        out_specs += specs
+        out_shape += shapes
+        scratch += scatter_scratch(h, w)
+        grid = (chunks + lag,)
+        params = pltpu.CompilerParams(vmem_limit_bytes=62 * MIB, collective_id=2, has_side_effects=True)
+    else:
+        out_specs.append(chunk((h, slots)))
+        out_shape.append(jax.ShapeDtypeStruct((chunks, h, slots), bf))
+        grid = (chunks,)
+        params = pltpu.CompilerParams(vmem_limit_bytes=62 * MIB)
     return pl.pallas_call(
-        functools.partial(ffn_body, experts),
-        grid=(chunks,),
-        in_specs=[
-            whole((slots, width)), whole((slots, width)), whole(routes_t.shape), whole((rows, width)),
-            anywhere, anywhere, anywhere, anywhere,
-        ],
-        out_specs=[
-            chunk((h2, slots)), chunk((h, slots)), whole((slots, width)), whole((slots, width)), whole((rows, width)),
-            whole((1, width)),
-        ],
-        out_shape=[
-            jax.ShapeDtypeStruct((chunks, h2, slots), bf), jax.ShapeDtypeStruct((chunks, h, slots), bf),
-            jax.ShapeDtypeStruct((slots, width), bf), jax.ShapeDtypeStruct((slots, width), bf),
-            jax.ShapeDtypeStruct((rows, width), f32), jax.ShapeDtypeStruct((1, width), f32),
-        ],
-        scratch_shapes=[
-            pltpu.VMEM((slots, width), f32), pltpu.VMEM((slots, width), f32),
-            pltpu.VMEM((experts, slots), f32), pltpu.VMEM((rows, slots), f32), pltpu.VMEM((rows, slots), f32),
-            pltpu.VMEM((2, h2, width), bf), pltpu.VMEM((2, h, width), bf), pltpu.SemaphoreType.DMA((2, 2)),
-        ],
-        compiler_params=pltpu.CompilerParams(vmem_limit_bytes=62 * MIB),
+        functools.partial(ffn_body, experts, chunks, scatter),
+        grid=grid,
+        in_specs=in_specs,
+        out_specs=out_specs,
+        out_shape=out_shape,
+        scratch_shapes=scratch,
+        compiler_params=params,
         cost_estimate=pl.CostEstimate(
             flops=12 * chunks * h * slots * width, bytes_accessed=10 * chunks * h * width + 16 * slots * width,
             transcendentals=chunks * h * slots,
         ),
-        name="ffn",
-    )(x, d_two, routes_t, router_rows, ei, si, eo, so)
+        name="ffn_scatter" if scatter else "ffn",
+    )(*args)
 
 
 def turn(v):
@@ -512,12 +601,15 @@
     )(d_qkv, w, x)
 
 
-def weight_grad_scatter(a, b, r, cid, name, first=0, count=None, cut=None):
-    count = a.shape[0] // r if count is None else count
+def weight_grad_scatter(a_list, b_list, r, cid, name, first=0, count=None, cut=None):
+    count = a_list[0].shape[0] // r if count is None else count
     cut = count if cut is None else cut
     if lax.axis_size("dp") == 8:
-        return weight_grad_scatter_kernel(a, b, r, cid, name, first, count, cut)
-    product = jnp.dot(a[first * r : (first + count) * r], b, preferred_element_type=jnp.float32)
+        return weight_grad_scatter_kernel(a_list, b_list, r, cid, name, first, count, cut)
+    product = sum(
+        jnp.dot(a[first * r : (first + count) * r], b, preferred_element_type=jnp.float32)
+        for a, b in zip(a_list, b_list)
+    )
     result = lax.psum_scatter(
         product.astype(jnp.bfloat16), "dp", scatter_dimension=1, tiled=True
     ).astype(jnp.float32)
@@ -762,35 +854,58 @@
     hidden = tokens_f + live_own * branch_one.astype(jnp.float32)
     inv_two = lax.rsqrt(jnp.mean(hidden * hidden, axis=-1, keepdims=True) + epsilon)
     unit_two = hidden * inv_two
-    normed_two = lax.all_gather((unit_two * gain_two).astype(bf), "tensor", axis=0, tiled=True)
-    d_gate_up, scaled_inner, d_normed, combined, router_part, norm_two_part = ffn(
-        normed_two, d_two, routes.T, router_rows, ei, si, eo, so
-    )
-    d_gate_up = d_gate_up.reshape(chunks * 2 * eff, slot_count)
-    scaled_inner = scaled_inner.reshape(chunks * eff, slot_count)
-    grad_two = lax.psum_scatter(d_normed, "tensor", scatter_dimension=0, tiled=True)
-    out_grads, shared_out_grad = weight_grad_scatter(
-        scaled_inner, d_two, eff, 2, "down_grads", cut=experts
-    )
-    grad_two = grad_two.astype(jnp.float32)
+    normed_two = (unit_two * gain_two).astype(bf)
+    half = own_rows // 2
+    size_t = lax.axis_size("tensor")
+
+    def halves(rows):
+        return rows.reshape(size_t, 2, half, -1).transpose(1, 0, 2, 3).reshape(2, size_t * half, -1)
+
+    d_a, d_b = halves(d_two)
+    routes_a, routes_b = halves(routes)
+    x_a = lax.all_gather(normed_two[:half], "tensor", axis=0, tiled=True)
+    x_a, second, d_a, d_b = lax.optimization_barrier((x_a, normed_two[half:], d_a, d_b))
+    x_b = lax.all_gather(second, "tensor", axis=0, tiled=True)
+    weights = (router_rows, ei, si, eo, so)
+    dgu_a, dn_a, bt_a, router_a, np_a, s_a = ffn(x_a, d_a, routes_a.T, *weights)
+    x_b, dn_a, bt_a, s_a = lax.optimization_barrier((x_b, dn_a, bt_a, s_a))
+    grad_a = lax.psum_scatter(dn_a, "tensor", scatter_dimension=0, tiled=True)
+    two_a = lax.psum_scatter(bt_a, "tensor", scatter_dimension=0, tiled=True)
+    if lax.axis_size("dp") == 8:
+        dgu_b, dn_b, bt_b, router_b, np_b, out_grads, shared_out_grad = ffn(
+            x_b, d_b, routes_b.T, *weights, other=(s_a, d_a)
+        )
+    else:
+        dgu_b, dn_b, bt_b, router_b, np_b, s_b = ffn(x_b, d_b, routes_b.T, *weights)
+        inner = [s.reshape(chunks * eff, -1) for s in (s_a, s_b)]
+        out_grads, shared_out_grad = weight_grad_scatter(
+            inner, [d_a, d_b], eff, 2, "down_grads", cut=experts
+        )
+    router_part = router_a + router_b
+    norm_two_part = np_a + np_b
+    d_gate_up = [d.reshape(chunks * 2 * eff, -1) for d in (dgu_a, dgu_b)]
+    grad_a, two_a, dn_b = lax.optimization_barrier((grad_a, two_a, dn_b))
+    grad_b = lax.psum_scatter(dn_b, "tensor", scatter_dimension=0, tiled=True)
+    in_grads_b, _ = weight_grad_scatter(
+        d_gate_up, [x_a, x_b], eff, 4, "shared_in_grads", 2 * experts, 2 * shared_chunks
+    )
+    grad_two = jnp.concatenate([grad_a, grad_b], axis=0).astype(jnp.float32)
     grad_hidden = grad_out + norm_back(grad_two, unit_two, inv_two, gain_two)
-    d_one_own, out_grads = lax.optimization_barrier(
-        ((live_own * grad_hidden).astype(bf), out_grads)
+    d_one_own, in_grads_b = lax.optimization_barrier(
+        ((live_own * grad_hidden).astype(bf), in_grads_b)
     )
     d_one = lax.all_gather(d_one_own, "tensor", axis=0, tiled=True)
     d_gate_up, _ = lax.optimization_barrier((d_gate_up, d_one_own))
     in_grads_a, _ = weight_grad_scatter(
-        d_gate_up, normed_two, eff, 3, "expert_in_grads", 0, 2 * experts
-    )
-    d_one, in_grads_a, combined, d_gate_up = lax.optimization_barrier(
-        (d_one, in_grads_a, combined, d_gate_up)
-    )
-    branch_two = lax.psum_scatter(combined, "tensor", scatter_dimension=0, tiled=True)
+        d_gate_up, [x_a, x_b], eff, 3, "expert_in_grads", 0, 2 * experts
+    )
+    d_one, in_grads_a, bt_b = lax.optimization_barrier((d_one, in_grads_a, bt_b))
+    two_b = lax.psum_scatter(bt_b, "tensor", scatter_dimension=0, tiled=True)
     d_mixed = lax.dot_general(d_one, out_weight, NT, preferred_element_type=jnp.float32).astype(bf)
     d_qkv, d_qkv_t, bias_part = attend_back(lengths, qkv, d_mixed, cos_table, sin_table)
     grad_one, norm_one_part = qkv_back(d_qkv, qkv_w, normed_one)
-    grad_one, d_gate_up, d_qkv_t, mixed_t = lax.optimization_barrier(
-        (grad_one, d_gate_up, d_qkv_t, mixed_t)
+    grad_one, d_qkv_t, mixed_t, two_b = lax.optimization_barrier(
+        (grad_one, d_qkv_t, mixed_t, two_b)
     )
     grad_one_own = lax.psum_scatter(grad_one, "tensor", scatter_dimension=0, tiled=True)
     part = jnp.concatenate(
@@ -803,14 +918,12 @@
         axis=0,
     )
     sums = small_sums(part, experts + 3, 7)
-    in_grads_b, _ = weight_grad_scatter(
-        d_gate_up, normed_two, eff, 4, "shared_in_grads", 2 * experts, 2 * shared_chunks
-    )
     qkv_sum, _ = weight_grad_scatter(
-        d_qkv_t.reshape(3 * qkv_cols, slot_count), normed_one, 3 * qkv_cols // 4, 5, "qkv_grads"
-    )
-    out_sum, _ = weight_grad_scatter(mixed_t, d_one, qkv_cols // 2, 6, "mix_grads")
-    output = (hidden + live_own * branch_two.astype(jnp.float32)).astype(bf)
+        [d_qkv_t.reshape(3 * qkv_cols, slot_count)], [normed_one], 3 * qkv_cols // 4, 5, "qkv_grads"
+    )
+    out_sum, _ = weight_grad_scatter([mixed_t], [d_one], qkv_cols // 2, 6, "mix_grads")
+    branch_two = jnp.concatenate([two_a, two_b], axis=0).astype(jnp.float32)
+    output = (hidden + live_own * branch_two).astype(bf)
     grad_one = grad_one_own.astype(jnp.float32)
     input_grad = grad_hidden + norm_back(grad_one, unit_one, inv_one, gain_one)
     qkv_bias_grad = sums[experts + 3, : 3 * qkv_cols].reshape(3, qkv_cols)

time: 905 us -> 826 us (0.913)
  Pallas kernels: 643 us -> 598 us
  waiting for transfers between devices: 128 us -> 86.8 us
    pallas_call x6, Pallas kernels: 438 us -> 394 us  [the longest x4 206 us: weight_grad_scatter_kernel(): pl.pallas_call(functools.partial(rs_body, count, cut, len(a_list)), grid=...]
    all_gather x1 -> x2, waiting for transfers between devices: 81.3 us -> 41 us  [the longest x1 41 us: on_device(): x_a = lax.all_gather(normed_two[:half], 'tensor', axis=0, tiled=True)]
    unnamed x68 -> x93, local copies, waits for them, and re-layouts: 56.2 us -> 55.2 us
  transfers between devices with their start and end apart: 7 -> 10, of which waited for: 3 -> 3; matrix products, arithmetic and copies ran while one was open for 7% -> 8% of each run, Pallas kernels for 49% -> 71%
where the time goes in v3:
time: 826 us; the launch traced here: 816 us
  Pallas kernels  598 us (72%)
  waiting for transfers between devices  86.8 us (11%)
  local copies, waits for them, and re-layouts  79.8 us (10%)
  other arithmetic  24.1 us (3%)
  between operations  15.6 us (2%)
  matrix products  9.72 us (1%)
    pallas_call x4, Pallas kernels, weight_grad_scatter_kernel(): pl.pallas_call(functools.partial(rs_body, count, cut, len(a_list)), grid=...  206 us
    pallas_call x2, Pallas kernels, ffn(): pl.pallas_call(functools.partial(ffn_body, experts, chunks, scatter), gri...  188 us
    pallas_call x1, Pallas kernels, gather_rows(): pl.pallas_call(gather_body, in_specs=[pl.BlockSpec(memory_space=pl.ANY)],...  138 us
    unnamed x93, local copies, waits for them, and re-layouts  55.2 us
    all_gather x1, waiting for transfers between devices, on_device(): x_a = lax.all_gather(normed_two[:half], 'tensor', axis=0, tiled=True)  41 us
    all_gather x1, waiting for transfers between devices, on_device(): lax.all_gather((unit_one * gain_one).astype(bf), 'tensor', axis=0, tiled=...  39.3 us
    pallas_call x1, Pallas kernels, attend_back(): pl.pallas_call(functools.partial(attend_back_body, rows), grid=(cols // H...  18.4 us
    pallas_call x1, Pallas kernels, small_sums(): pl.pallas_call(functools.partial(sums_body, local_rows), in_specs=[vmem],...  16.9 us
  transfers between devices with their start and end apart: 10, of which 3 were waited for; matrix products, arithmetic and copies ran while one was open for 8% of the time, Pallas kernels for 71%

profile of v3, /device:TPU:0, one launch (start us, length us, event | category | flops | bytes accessed | tf_op | source)
XLA Modules:
  0.0 815.8 jit_solution(341099871118703055)
XLA Ops:
  10.1 2.5 fusion.3
  13.3 28.9 %copy.33 = bf16[2048,2,1408]{0,2,1:T(8,128)(2,1)} copy(bf16[2048,2,1408]{2,1,0:T(2,128)(2,1)} %param.27) | data formatting | bytes 23068672 | tf_op args[12]
  42.2 10.1 %copy.34 = bf16[4,2,352,2048]{3,2,1,0:T(8,128)(2,1)} copy(bf16[4,2,352,2048]{3,2,0,1:T(8,128)(2,1)} %bitcast.70) | data formatting | bytes 23068672 | tf_op jit(solution)/shard_map/transpose | solution.py:830
  56.9 39.3 %all-gather.5.cloned.1.call-done.x_ref.refs_1_ = bf16[1024,2048]{1,0:T(8,128)(2,1)} async-done(((bf16[256,2048]{1,0:T(8,128)(2,1)}), bf16[1024,2048]{1,0:T(8,128)(2,1)}) %all-gather.5.cloned.1.call-update) | async-done | bytes 4194320 | tf_op jit(solution)/shard_map/all_gather | solution.py:823
  96.2 11.3 %project_qkv.1.q_ref.k_ref.v_ref = bf16[3,1024,512]{2,1,0:T(8,128)(2,1)S(1)} custom-call(bf16[1024,2048]{1,0:T(8,128)(2,1)} %all-gather.5.cloned.1.call-done.x_ref.refs_1_, bf16[3,2048,512]{2,1,0:T(8,128)(2,1)} %bitcast.95, bf16[3,1,512]{2,1,0:T(2,128)(2,1)S(1)} %copy.35.bias_ref, f32[1024,128]{1,0:T(8,128)S(1)} %get-tuple-element.71.cos_ref, ...), custom_call_target="tpu_custom_call" | custom-call | flops 6442450944 | bytes 10485760 | tf_op jit(solution)/shard_map/project_qkv/pallas_call | solution.py:439
  107.5 9.9 %attend.1 = (bf16[1024,512]{1,0:T(8,128)(2,1)S(1)}, bf16[512,1024]{1,0:T(8,128)(2,1)S(1)}) custom-call(s32[1]{0:T(128)} %copy.53.length_ref, bf16[3,1024,512]{2,1,0:T(8,128)(2,1)S(1)} %project_qkv.1.q_ref.k_ref.v_ref, bf16[3,1024,512]{2,1,0:T(8,128)(2,1)S(1)} %project_qkv.1.q_ref.k_ref.v_ref, bf16[3,1024,512]{2,1,0:T(8,128)(2,1)S(1)} %project_qkv.1.q_ref.k_ref.v_ref), custom_call_target="tpu_custom_call" | custom-call | flops 2147483648 | bytes 5242880 | tf_op jit(solution)/shard_map/attend/pallas_call | solution.py:483
  118.5 4.4 convolution_convert_fusion
  123.5 138.0 %gather_rows.1 = bf16[1024,2048]{1,0:T(8,128)(2,1)} custom-call(bf16[256,2048]{1,0:T(8,128)(2,1)} %multiply_convert_fusion.2.own_ref), custom_call_target="tpu_custom_call" | custom-call | bytes 8388608 | tf_op jit(solution)/shard_map/gather_rows/pallas_call | solution.py:701
  265.9 2.5 copy.47
  270.7 41.0 %all-gather.7.cloned.1.call-done.x_ref.refs_2_ = bf16[512,2048]{1,0:T(8,128)(2,1)} async-done(((bf16[128,2048]{1,0:T(8,128)(2,1)}), bf16[512,2048]{1,0:T(8,128)(2,1)}) %all-gather.7.cloned.1.call-update) | async-done | bytes 2097168 | tf_op jit(solution)/shard_map/all_gather | solution.py:866
  312.0 75.9 %ffn.1 = (bf16[12,704,512]{2,1,0:T(8,128)(2,1)}, bf16[512,2048]{1,0:T(8,128)(2,1)}, bf16[512,2048]{1,0:T(8,128)(2,1)}, f32[16,2048]{1,0:T(8,128)}, f32[1,2048]{1,0:T(1,128)}, /*index=5*/bf16[12,352,512]{2,1,0:T(8,128)(2,1)}) custom-call(bf16[512,2048]{1,0:T(8,128)(2,1)} %all-gather.7.cloned.1.call-done.x_ref.refs_2_, bf16[512,2048]{1,0:T(8,128)(2,1)} %bitcast.82, ...), custom_call_target="tpu_custom_call" | custom-call | flops 53150220288 | bytes 103284736 | tf_op jit(solution)/shard_map/ffn/pallas_call | solution.py:396
  388.8 111.9 %ffn_scatter.1 = (bf16[12,704,512]{2,1,0:T(8,128)(2,1)}, bf16[512,2048]{1,0:T(8,128)(2,1)}, bf16[512,2048]{1,0:T(8,128)(2,1)}, f32[16,2048]{1,0:T(8,128)}, f32[1...) custom-call(bf16[512,2048]{1,0:T(8,128)(2,1)} %all-gather.9.cloned.1.call-done.x_ref.refs_3_, ...), custom_call_target="tpu_custom_call" | custom-call | flops 53150220288 | bytes 103284736 | tf_op jit(solution)/shard_map/ffn_scatter/pallas_call | solution.py:396
  503.9 54.5 %shared_in_grads.1 = (f32[2816,256]{1,0:T(8,128)}, f32[352,256]{1,0:T(8,128)}) custom-call(bf16[8448,512]{1,0:T(8,128)(2,1)} %bitcast.99, bf16[8448,512]{1,0:T(8,128)(2,1)} %bitcast.101, bf16[512,2048]{1,0:T(8,128)(2,1)S(1)} %copy-done.7, bf16[512,2048]{1,0:T(8,128)(2,1)S(1)} %copy-done.8), custom_call_target="tpu_custom_call" | custom-call | flops 11811160064 | bytes 12845056 | tf_op jit(solution)/shard_map/shared_in_grads/pallas_call | solution.py:200
  564.8 100.9 %expert_in_grads.1 = (f32[5632,256]{1,0:T(8,128)}, f32[352,256]{1,0:T(8,128)}) custom-call(bf16[8448,512]{1,0:T(8,128)(2,1)} %bitcast.100, bf16[8448,512]{1,0:T(8,128)(2,1)} %bitcast.102, bf16[512,2048]{1,0:T(8,128)(2,1)S(1)} %copy-done.7, bf16[512,2048]{1,0:T(8,128)(2,1)S(1)} %copy-done.9), custom_call_target="tpu_custom_call" | custom-call | flops 23622320128 | bytes 21495808 | tf_op jit(solution)/shard_map/expert_in_grads/pallas_call | solution.py:200
  665.8 5.4 convolution_convert_fusion.1.dm_ref
  671.2 18.4 %attend_back.1 = (bf16[3,1024,512]{2,1,0:T(8,128)(2,1)S(1)}, bf16[3,512,1024]{2,1,0:T(8,128)(2,1)S(1)}, f32[3,1,512]{2,1,0:T(1,128)S(1)}) custom-call(s32[1]{0:T(128)} %copy.53.length_ref, bf16[3,1024,512]{2,1,0:T(8,128)(2,1)S(1)} %copy-done.1, bf16[3,1024,512]{2,1,0:T(8,128)(2,1)S(1)} %copy-done.1, bf16[3,1024,512]{2,1,0:T(8,128)(2,1)S(1)} %copy-done.1, ...), custom_call_target="tpu_custom_call" | custom-call | flops 5368709120 | bytes 10485760 | tf_op jit(solution)/shard_map/attend_back/pallas_call | solution.py:548
  691.4 10.3 %qkv_back.1 = (bf16[1024,2048]{1,0:T(8,128)(2,1)}, f32[1,2048]{1,0:T(1,128)S(1)}) custom-call(bf16[3,1024,512]{2,1,0:T(8,128)(2,1)S(1)} %get-tuple-element.104.d_ref, bf16[3,2048,512]{2,1,0:T(8,128)(2,1)} %bitcast.96, bf16[1024,2048]{1,0:T(8,128)(2,1)} %all-gather.5.cloned.1.call-done.x_ref.refs_1_), custom_call_target="tpu_custom_call" | custom-call | flops 6442450944 | bytes 14680064 | tf_op jit(solution)/shard_map/qkv_back/pallas_call | solution.py:584
  701.7 5.7 reduce-scatter.15.cloned.1.call-done
  711.2 5.8 copy.40
  717.7 16.9 %small_sums.1 = f32[12,2048]{1,0:T(8,128)} custom-call(f32[12,2048]{1,0:T(8,128)} %select_maximum_fusion.part_ref), custom_call_target="tpu_custom_call" | custom-call | tf_op jit(solution)/shard_map/small_sums/pallas_call | solution.py:772
  741.2 15.9 %mix_grads.1 = (f32[512,256]{1,0:T(8,128)S(1)}, f32[256,256]{1,0:T(8,128)}) custom-call(bf16[512,1024]{1,0:T(8,128)(2,1)S(1)} %copy-done.11, bf16[1024,2048]{1,0:T(8,128)(2,1)S(1)} %copy-done.6), custom_call_target="tpu_custom_call" | custom-call | flops 2147483648 | bytes 5767168 | tf_op jit(solution)/shard_map/mix_grads/pallas_call | solution.py:200
  757.1 34.5 %qkv_grads.1 = (f32[1536,256]{1,0:T(8,128)S(1)}, f32[384,256]{1,0:T(8,128)}) custom-call(bf16[1536,1024]{1,0:T(8,128)(2,1)S(1)} %bitcast.69, bf16[1024,2048]{1,0:T(8,128)(2,1)} %all-gather.5.cloned.1.call-done.x_ref.refs_1_), custom_call_target="tpu_custom_call" | custom-call | flops 6442450944 | bytes 8912896 | tf_op jit(solution)/shard_map/qkv_grads/pallas_call | solution.py:200
  795.2 5.4 fusion.7
  801.4 2.9 copy.55
  (156 shorter events, 47.9 us)
Async XLA Ops:
  7.2 6.1 copy-start.39
  7.2 6.1 copy-start.37
  7.2 89.0 %all-gather.5.cloned.1.call-start = ((), (), s32[]{:S(2)}) async-start(), calls=%async_computation.6 | async-start | bytes 5242880 | tf_op jit(solution)/shard_map/all_gather | solution.py:823
  12.6 249.0 %reduce-scatter.7.cloned.1.call-start = ((), (), s32[]{:S(2)}) async-start(), calls=%async_computation.7 | async-start | bytes 5242880 | tf_op jit(solution)/shard_map/reduce_scatter | solution.py:851
  54.7 52.8 %copy-start.2 = (f32[1024,128]{1,0:T(8,128)}, f32[1024,128]{1,0:T(8,128)S(1)}, u32[]{:S(2)}) copy-start(f32[1024,128]{1,0:T(8,128)S(1)} %get-tuple-element.71.cos_ref) | copy-start | bytes 1572868
  54.7 52.8 %copy-start.4 = (f32[1024,128]{1,0:T(8,128)}, f32[1024,128]{1,0:T(8,128)S(1)}, u32[]{:S(2)}) copy-start(f32[1024,128]{1,0:T(8,128)S(1)} %get-tuple-element.72.sin_ref) | copy-start | bytes 1572868
  107.5 10.0 %copy-start = (bf16[3,1024,512]{2,1,0:T(8,128)(2,1)}, bf16[3,1024,512]{2,1,0:T(8,128)(2,1)S(1)}, u32[]{:S(2)}) copy-start(bf16[3,1024,512]{2,1,0:T(8,128)(2,1)S(1)} %project_qkv.1.q_ref.k_ref.v_ref) | copy-start | bytes 9437188
  107.5 11.0 %copy-start.40 = (bf16[512,2048]{1,0:T(8,128)(2,1)S(1)}, bf16[512,2048]{1,0:T(8,128)(2,1)}, u32[]{:S(2)}) copy-start(bf16[512,2048]{1,0:T(8,128)(2,1)} %param.22) | copy-start | bytes 6291460
  122.9 188.8 %all-gather.7.cloned.1.call-start = ((), (), s32[]{:S(2)}) async-start(), calls=%async_computation.8 | async-start | bytes 2621440 | tf_op jit(solution)/shard_map/all_gather | solution.py:866
  123.5 138.1 %copy-start.14 = (bf16[256,2048]{1,0:T(8,128)(2,1)S(1)}, bf16[256,2048]{1,0:T(8,128)(2,1)}, u32[]{:S(2)}) copy-start(bf16[256,2048]{1,0:T(8,128)(2,1)} %param.15) | copy-start | bytes 3145732
  265.1 122.8 %all-gather.9.cloned.1.call-start = ((), (), s32[]{:S(2)}) async-start(), calls=%async_computation.9 | async-start | bytes 2621440 | tf_op jit(solution)/shard_map/all_gather | solution.py:868
  311.7 189.1 %reduce-scatter.9.cloned.1.call-start = ((), (), s32[]{:S(2)}) async-start(), calls=%async_computation.10 | async-start | bytes 2621440 | tf_op jit(solution)/shard_map/reduce_scatter | solution.py:872
  388.0 112.9 %reduce-scatter.11.cloned.1.call-start = ((), (), s32[]{:S(2)}) async-start(), calls=%async_computation.11 | async-start | bytes 2621440 | tf_op jit(solution)/shard_map/reduce_scatter | solution.py:873
  388.5 170.0 %reduce-scatter.13.cloned.1.call-start = ((), (), s32[]{:S(2)}) async-start(), calls=%async_computation.12 | async-start | bytes 2621440 | tf_op jit(solution)/shard_map/reduce_scatter | solution.py:888
  500.8 164.8 %all-gather.11.cloned.1.call-start = ((), (), s32[]{:S(2)}) async-start(), calls=%async_computation.13 | async-start | bytes 5242880 | tf_op jit(solution)/shard_map/all_gather | solution.py:897
  563.1 144.3 %reduce-scatter.15.cloned.1.call-start = ((), (), s32[]{:S(2)}) async-start(), calls=%async_computation.14 | async-start | bytes 2621440 | tf_op jit(solution)/shard_map/reduce_scatter | solution.py:903
  665.7 5.4 copy-start.1
  665.7 127.6 %reduce-scatter.17.cloned.1.call-start = ((), (), s32[]{:S(2)}) async-start(), calls=%async_computation.15 | async-start | bytes 5242880 | tf_op jit(solution)/shard_map/reduce_scatter | solution.py:910
  665.7 5.4 copy-start.3
  711.2 5.8 copy-start.28
  711.2 27.9 %copy-start.11 = (bf16[512,1024]{1,0:T(8,128)(2,1)S(1)}, bf16[512,1024]{1,0:T(8,128)(2,1)}, u32[]{:S(2)}) copy-start(bf16[512,1024]{1,0:T(8,128)(2,1)} %copy-done.10) | copy-start | bytes 3145732
  741.2 15.9 %copy-start.13 = (bf16[3,512,1024]{2,1,0:T(8,128)(2,1)S(1)}, bf16[3,512,1024]{2,1,0:T(8,128)(2,1)}, u32[]{:S(2)}) copy-start(bf16[3,512,1024]{2,1,0:T(8,128)(2,1)} %copy-done.12) | copy-start | bytes 9437188
  795.2 6.2 slice-start
  795.2 6.2 slice-start.1
  (29 other events, 54.2 us)
Sparse Core Ops, SparseCore 0:
  12.7 83.4 all-gather.4
  123.0 109.0 reduce-scatter.6
  265.3 46.3 all-gather.6
  313.8 44.6 all-gather.8
  388.1 42.5 reduce-scatter.8
  432.8 43.2 reduce-scatter.10
  501.0 41.2 reduce-scatter.12
  563.2 78.1 all-gather.10
  665.8 41.5 reduce-scatter.14
  710.2 77.1 reduce-scatter.16

commit v4 on v3

--- a/solution.py
+++ b/solution.py
@@ -616,59 +616,29 @@
     return result[: cut * r], result[cut * r :]
 
 
-def gather_body(own_ref, out_ref, local_sem, send_left, recv_left, send_right, recv_right):
-    me = lax.axis_index("tensor")
-    size = lax.axis_size("tensor")
-    rows = own_ref.shape[0]
+def line_gather(me, size, own, block, local_sem, sems):
+    send_left, recv_left, send_right, recv_right = sems
     has_left, has_right = me > 0, me < size - 1
 
-    def block(owner):
-        return out_ref.at[pl.ds(pl.multiple_of(owner * rows, rows), rows)]
+    def remote(source, owner, send, recv, step, to):
+        return pltpu.make_async_remote_copy(
+            src_ref=source, dst_ref=block(owner), send_sem=send.at[step], recv_sem=recv.at[step],
+            device_id={"tensor": to}, device_id_type=MESH,
+        )
 
     def to_left(step):
-        source = own_ref if step == 0 else block(me + step)
-        return pltpu.make_async_remote_copy(
-            src_ref=source, dst_ref=block(me + step), send_sem=send_left.at[step], recv_sem=recv_left.at[step],
-            device_id={"tensor": me - 1}, device_id_type=MESH,
-        )
-
-    def from_right(step):
-        return pltpu.make_async_remote_copy(
-            src_ref=own_ref, dst_ref=block(me + 1 + step), send_sem=send_left.at[step], recv_sem=recv_left.at[step],
-            device_id={"tensor": me + 1}, device_id_type=MESH,
-        )
+        return remote(own if step == 0 else block(me + step), me + step, send_left, recv_left, step, me - 1)
 
     def to_right(step):
-        source = own_ref if step == 0 else block(me - step)
-        return pltpu.make_async_remote_copy(
-            src_ref=source, dst_ref=block(me - step), send_sem=send_right.at[step], recv_sem=recv_right.at[step],
-            device_id={"tensor": me + 1}, device_id_type=MESH,
-        )
-
-    def from_left(step):
-        return pltpu.make_async_remote_copy(
-            src_ref=own_ref, dst_ref=block(me - 1 - step), send_sem=send_right.at[step], recv_sem=recv_right.at[step],
-            device_id={"tensor": me - 1}, device_id_type=MESH,
-        )
-
-    barrier = pltpu.get_barrier_semaphore()
-
-    @pl.when(has_left)
-    def _():
-        pl.semaphore_signal(barrier, inc=1, device_id={"tensor": me - 1}, device_id_type=MESH)
-
-    @pl.when(has_right)
-    def _():
-        pl.semaphore_signal(barrier, inc=1, device_id={"tensor": me + 1}, device_id_type=MESH)
-
-    pl.semaphore_wait(barrier, has_left.astype(jnp.int32) + has_right.astype(jnp.int32))
-    local = pltpu.make_async_copy(own_ref, block(me), local_sem)
-    local.start()
-    for step in range(size):
-        if step > 0:
+        return remote(own if step == 0 else block(me - step), me - step, send_right, recv_right, step, me + 1)
+
+    def advance(step):
+        if step == 0:
+            pltpu.make_async_copy(own, block(me), local_sem).start()
+        else:
             @pl.when(me + step < size)
             def _():
-                from_right(step - 1).wait_recv()
+                remote(own, me + step, send_left, recv_left, step - 1, me + 1).wait_recv()
 
         @pl.when(has_left & (me + step < size))
         def _():
@@ -677,39 +647,180 @@
         if step > 0:
             @pl.when(me - step >= 0)
             def _():
-                from_left(step - 1).wait_recv()
+                remote(own, me - step, send_right, recv_right, step - 1, me - 1).wait_recv()
 
         @pl.when(has_right & (me - step >= 0))
         def _():
             to_right(step).start()
 
-    for step in range(size):
-        @pl.when(has_left & (me + step < size))
-        def _():
-            to_left(step).wait_send()
-
-        @pl.when(has_right & (me - step >= 0))
-        def _():
-            to_right(step).wait_send()
-
-    local.wait()
-
-
-def gather_rows(own, cid):
+    def finish():
+        for step in range(size):
+            @pl.when(has_left & (me + step < size))
+            def _():
+                to_left(step).wait_send()
+
+            @pl.when(has_right & (me - step >= 0))
+            def _():
+                to_right(step).wait_send()
+
+        pltpu.make_async_copy(own, block(me), local_sem).wait()
+
+    return advance, finish
+
+
+def line_barrier(me, size):
+    barrier = pltpu.get_barrier_semaphore()
+    has_left, has_right = me > 0, me < size - 1
+
+    @pl.when(has_left)
+    def _():
+        pl.semaphore_signal(barrier, inc=1, device_id={"tensor": me - 1}, device_id_type=MESH)
+
+    @pl.when(has_right)
+    def _():
+        pl.semaphore_signal(barrier, inc=1, device_id={"tensor": me + 1}, device_id_type=MESH)
+
+    pl.semaphore_wait(barrier, has_left.astype(jnp.int32) + has_right.astype(jnp.int32))
+
+
+def branch_body(
+    length_ref, part_ref, tokens_ref, gain_ref, cot_ref, hidden_ref, second_ref, xa_ref, da_ref, db_ref,
+    from_left, from_right, normed, local_sem, send_r, recv_r, send_l, recv_l, *sems,
+):
+    me = lax.axis_index("tensor")
     size = lax.axis_size("tensor")
-    rows, width = own.shape
+    rows = tokens_ref.shape[0]
+    half = rows // 2
+    bf, f32 = jnp.bfloat16, jnp.float32
+    has_left, has_right = me > 0, me < size - 1
+    line_barrier(me, size)
+
+    def place(ref, owner):
+        return ref.at[pl.ds(pl.multiple_of(owner * half, half), half)]
+
+    def own_cot(h):
+        return cot_ref.at[pl.ds(h * half, half)]
+
+    def part(ref, owner, h):
+        return ref.at[owner, pl.ds(h * half, half)]
+
+    def direction(right):
+        slots, send, recv = (from_left, send_r, recv_r) if right else (from_right, send_l, recv_l)
+        to = me + 1 if right else me - 1
+        before = me if right else size - 1 - me
+        has_to = has_right if right else has_left
+        has_from = has_left if right else has_right
+
+        def copy(source, target, t):
+            return pltpu.make_async_remote_copy(
+                src_ref=source, dst_ref=target, send_sem=send.at[t], recv_sem=recv.at[t],
+                device_id={"tensor": to}, device_id_type=MESH,
+            )
+
+        def sent(t):
+            copy(part(part_ref, 0, 0), part(slots, 0, 0), t).wait_send()
+
+        def step(t):
+            s, h = t // 2, t % 2
+            gathered = (da_ref, db_ref)[h]
+            if t >= 2:
+                @pl.when(has_to)
+                def _():
+                    sent(t - 2)
+
+            @pl.when(s <= before)
+            def _():
+                owner = me - s if right else me + s
+                if s > 0:
+                    copy(own_cot(h), place(gathered, owner), t - 2).wait_recv()
+
+                @pl.when(has_to)
+                def _():
+                    copy(own_cot(h) if s == 0 else place(gathered, owner), place(gathered, owner), t).start()
+
+            @pl.when(s > before)
+            def _():
+                owner = size + me - s if right else me + s - size
+
+                @pl.when(has_from)
+                def _():
+                    copy(part(part_ref, owner, h), part(slots, owner, h), t - 2).wait_recv()
+                    both = part(slots, owner, h)
+                    both[...] = (both[...].astype(f32) + part(part_ref, owner, h)[...].astype(f32)).astype(bf)
+                    copy(both, part(slots, owner, h), t).start()
+
+                @pl.when(jnp.logical_not(has_from))
+                def _():
+                    copy(part(part_ref, owner, h), part(slots, owner, h), t).start()
+
+        def last():
+            @pl.when(has_to)
+            def _():
+                sent(2 * size - 2)
+                sent(2 * size - 1)
+
+            @pl.when(has_from)
+            def _():
+                for h in range(2):
+                    copy(part(part_ref, me, h), part(slots, me, h), 2 * size - 2 + h).wait_recv()
+                hidden_ref[...] += slots[me].astype(f32)
+
+        return step, last
+
+    local = [
+        pltpu.make_async_copy(own_cot(h), place(ref, me), local_sem.at[h]) for h, ref in enumerate((da_ref, db_ref))
+    ]
+    for copy in local:
+        copy.start()
+    step_r, last_r = direction(True)
+    step_l, last_l = direction(False)
+    for t in range(2 * size):
+        step_r(t)
+        step_l(t)
+    hidden_ref[...] = part_ref[me].astype(f32)
+    last_r()
+    last_l()
+    row = lax.broadcasted_iota(jnp.int32, (rows, 1), 0) + me * rows
+    live = jnp.where(row < length_ref[0], 1.0, 0.0)
+    hidden = tokens_ref[...].astype(f32) + live * hidden_ref[...]
+    hidden_ref[...] = hidden
+    inverse = lax.rsqrt(jnp.mean(hidden * hidden, axis=1, keepdims=True) + epsilon)
+    normed[...] = (hidden * inverse * gain_ref[...].astype(f32)).astype(bf)
+    step_x, finish_x = line_gather(
+        me, size, normed.at[:half], lambda owner: place(xa_ref, owner), local_sem.at[2], sems
+    )
+    for j in range(size):
+        step_x(j)
+    second_ref[...] = normed[half:, :]
+    for copy in local:
+        copy.wait()
+    finish_x()
+
+
+def finish_branch(lengths, part, tokens, gain, cot, cid):
+    size = lax.axis_size("tensor")
+    rows, width = tokens.shape
+    half = rows // 2
+    bf, f32 = jnp.bfloat16, jnp.float32
+    vmem = pl.BlockSpec(memory_space=pltpu.VMEM)
+    anywhere = pl.BlockSpec(memory_space=pl.ANY)
+    dma = pltpu.SemaphoreType.DMA
+    gathered = jax.ShapeDtypeStruct((size * half, width), bf)
     return pl.pallas_call(
-        gather_body,
-        in_specs=[pl.BlockSpec(memory_space=pl.ANY)],
-        out_specs=pl.BlockSpec(memory_space=pl.ANY),
-        out_shape=jax.ShapeDtypeStruct((rows * size, width), own.dtype),
+        branch_body,
+        in_specs=[pl.BlockSpec(memory_space=pltpu.SMEM), vmem, vmem, vmem, anywhere],
+        out_specs=[vmem, vmem, anywhere, anywhere, anywhere],
+        out_shape=[
+            jax.ShapeDtypeStruct((rows, width), f32), jax.ShapeDtypeStruct((half, width), bf), gathered, gathered, gathered,
+        ],
         scratch_shapes=[
-            pltpu.SemaphoreType.DMA, *[pltpu.SemaphoreType.DMA((size,))] * 4,
-        ],
-        compiler_params=pltpu.CompilerParams(collective_id=cid, has_side_effects=True),
-        cost_estimate=pl.CostEstimate(flops=0, bytes_accessed=2 * rows * size * width * 2, transcendentals=0),
-        name="gather_rows",
-    )(own)
+            pltpu.VMEM((size, rows, width), bf), pltpu.VMEM((size, rows, width), bf), pltpu.VMEM((rows, width), bf),
+            dma((3,)), *[dma((2 * size,))] * 4, *[dma((size,))] * 4,
+        ],
+        compiler_params=pltpu.CompilerParams(vmem_limit_bytes=48 * MIB, collective_id=cid, has_side_effects=True),
+        cost_estimate=pl.CostEstimate(flops=0, bytes_accessed=24 * rows * size * width, transcendentals=0),
+        name="finish_branch",
+    )(lengths, part.reshape(size, rows, width), tokens, gain[None], cot)
 
 
 def sums_body(
@@ -847,24 +958,16 @@
     qkv = project_qkv(normed_one, qkv_w, qkv_bias[:, None, :], cos_table, sin_table)
     mixed, mixed_t = attend(lengths, qkv)
     branch_partial = jnp.dot(mixed, out_weight, preferred_element_type=jnp.float32).astype(bf)
-    d_two_own, branch_partial = lax.optimization_barrier((d_two_own, branch_partial))
-    branch_one = lax.psum_scatter(branch_partial, "tensor", scatter_dimension=0, tiled=True)
-    d_two = gather_rows(d_two_own, 1)
-    branch_one, d_two = lax.optimization_barrier((branch_one, d_two))
-    hidden = tokens_f + live_own * branch_one.astype(jnp.float32)
+    size_t = lax.axis_size("tensor")
+    half = own_rows // 2
+    hidden, second, x_a, d_a, d_b = finish_branch(
+        lengths, branch_partial, tokens, norm_two, d_two_own, 1
+    )
     inv_two = lax.rsqrt(jnp.mean(hidden * hidden, axis=-1, keepdims=True) + epsilon)
     unit_two = hidden * inv_two
-    normed_two = (unit_two * gain_two).astype(bf)
-    half = own_rows // 2
-    size_t = lax.axis_size("tensor")
-
-    def halves(rows):
-        return rows.reshape(size_t, 2, half, -1).transpose(1, 0, 2, 3).reshape(2, size_t * half, -1)
-
-    d_a, d_b = halves(d_two)
-    routes_a, routes_b = halves(routes)
-    x_a = lax.all_gather(normed_two[:half], "tensor", axis=0, tiled=True)
-    x_a, second, d_a, d_b = lax.optimization_barrier((x_a, normed_two[half:], d_a, d_b))
+    routes_a, routes_b = (
+        routes.reshape(size_t, 2, half, -1).transpose(1, 0, 2, 3).reshape(2, size_t * half, -1)
+    )
     x_b = lax.all_gather(second, "tensor", axis=0, tiled=True)
     weights = (router_rows, ei, si, eo, so)
     dgu_a, dn_a, bt_a, router_a, np_a, s_a = ffn(x_a, d_a, routes_a.T, *weights)

time: 826 us -> 777 us (0.941)
  waiting for transfers between devices: 86.8 us -> 46.3 us
    all_gather x1 -> x0, waiting for transfers between devices: 41 us -> none  [on_device(): x_a = lax.all_gather(normed_two[:half], 'tensor', axis=0, tiled=True)]
    unnamed x93 -> x91, local copies, waits for them, and re-layouts: 55.2 us -> 59.6 us
  transfers between devices with their start and end apart: 10 -> 8, of which waited for: 3 -> 2; matrix products, arithmetic and copies ran while one was open for 8% -> 9% of each run, Pallas kernels for 71% -> 57%
where the time goes in v4:
time: 777 us; the launch traced here: 767 us
  Pallas kernels  592 us (76%)
  local copies, waits for them, and re-layouts  81.6 us (11%)
  waiting for transfers between devices  46.3 us (6%)
  other arithmetic  20.9 us (3%)
  between operations  15.6 us (2%)
  matrix products  9.72 us (1%)
    pallas_call x4, Pallas kernels, weight_grad_scatter_kernel(): pl.pallas_call(functools.partial(rs_body, count, cut, len(a_list)), grid=...  206 us
    pallas_call x2, Pallas kernels, ffn(): pl.pallas_call(functools.partial(ffn_body, experts, chunks, scatter), gri...  188 us
    pallas_call x1, Pallas kernels, finish_branch(): pl.pallas_call(branch_body, in_specs=[pl.BlockSpec(memory_space=pltpu.SME...  132 us
    unnamed x91, local copies, waits for them, and re-layouts  59.6 us
    all_gather x1, waiting for transfers between devices, on_device(): lax.all_gather((unit_one * gain_one).astype(bf), 'tensor', axis=0, tiled=...  39.6 us
    pallas_call x1, Pallas kernels, attend_back(): pl.pallas_call(functools.partial(attend_back_body, rows), grid=(cols // H...  18.5 us
    pallas_call x1, Pallas kernels, small_sums(): pl.pallas_call(functools.partial(sums_body, local_rows), in_specs=[vmem],...  16.1 us
  transfers between devices with their start and end apart: 8, of which 2 were waited for; matrix products, arithmetic and copies ran while one was open for 9% of the time, Pallas kernels for 57%

profile of v4, /device:TPU:0, one launch (start us, length us, event | category | flops | bytes accessed | tf_op | source)
XLA Modules:
  0.0 767.2 jit_solution(2573830094959352344)
XLA Ops:
  13.4 28.9 %copy.32 = bf16[2048,2,1408]{0,2,1:T(8,128)(2,1)} copy(bf16[2048,2,1408]{2,1,0:T(2,128)(2,1)} %param.27) | data formatting | bytes 23068672 | tf_op args[12]
  42.3 10.1 %copy.33 = bf16[4,2,352,2048]{3,2,1,0:T(8,128)(2,1)} copy(bf16[4,2,352,2048]{3,2,0,1:T(8,128)(2,1)} %bitcast.65) | data formatting | bytes 23068672 | tf_op jit(solution)/shard_map/transpose | solution.py:941
  56.6 39.6 %all-gather.4.cloned.1.call-done.x_ref.refs_1_ = bf16[1024,2048]{1,0:T(8,128)(2,1)} async-done(((bf16[256,2048]{1,0:T(8,128)(2,1)}), bf16[1024,2048]{1,0:T(8,128)(2,1)}) %all-gather.4.cloned.1.call-update) | async-done | bytes 4194320 | tf_op jit(solution)/shard_map/all_gather | solution.py:934
  96.2 11.1 %project_qkv.1.q_ref.k_ref.v_ref = bf16[3,1024,512]{2,1,0:T(8,128)(2,1)S(1)} custom-call(bf16[1024,2048]{1,0:T(8,128)(2,1)} %all-gather.4.cloned.1.call-done.x_ref.refs_1_, bf16[3,2048,512]{2,1,0:T(8,128)(2,1)} %bitcast.84, bf16[3,1,512]{2,1,0:T(2,128)(2,1)S(1)} %copy.34.bias_ref, f32[1024,128]{1,0:T(8,128)S(1)} %get-tuple-element.67.cos_ref, ...), custom_call_target="tpu_custom_call" | custom-call | flops 6442450944 | bytes 10485760 | tf_op jit(solution)/shard_map/project_qkv/pallas_call | solution.py:439
  107.4 9.9 %attend.1 = (bf16[1024,512]{1,0:T(8,128)(2,1)S(1)}, bf16[512,1024]{1,0:T(8,128)(2,1)S(1)}) custom-call(s32[1]{0:T(128)} %copy.49.length_ref, bf16[3,1024,512]{2,1,0:T(8,128)(2,1)S(1)} %project_qkv.1.q_ref.k_ref.v_ref, bf16[3,1024,512]{2,1,0:T(8,128)(2,1)S(1)} %project_qkv.1.q_ref.k_ref.v_ref, bf16[3,1024,512]{2,1,0:T(8,128)(2,1)S(1)} %project_qkv.1.q_ref.k_ref.v_ref), custom_call_target="tpu_custom_call" | custom-call | flops 2147483648 | bytes 5242880 | tf_op jit(solution)/shard_map/attend/pallas_call | solution.py:483
  117.4 4.4 convolution_convert_fusion
  121.7 132.1 %finish_branch.1 = (f32[256,2048]{1,0:T(8,128)S(1)}, bf16[128,2048]{1,0:T(8,128)(2,1)}, bf16[512,2048]{1,0:T(8,128)(2,1)}, bf16[512,2048]{1,0:T(8,128)(2,1)}, bf16[512,2048]{1,0:T(8,128)(2,1)}) custom-call(s32[1]{0:T(128)} %copy.49.length_ref, bf16[4,256,2048]{2,1,0:T(8,128)(2,1)} %bitcast.70, bf16[256,2048]{1,0:T(8,128)(2,1)S(1)} %copy-done.4, ...), custom_call_target="tpu_custom_call" | custom-call | bytes 50331648 | tf_op jit(solution)/shard_map/finish_branch/pallas_call | solution.py:809
  255.2 75.9 %ffn.1 = (bf16[12,704,512]{2,1,0:T(8,128)(2,1)}, bf16[512,2048]{1,0:T(8,128)(2,1)}, bf16[512,2048]{1,0:T(8,128)(2,1)}, f32[16,2048]{1,0:T(8,128)}, f32[1,2048]{1,0:T(1,128)}, /*index=5*/bf16[12,352,512]{2,1,0:T(8,128)(2,1)}) custom-call(bf16[512,2048]{1,0:T(8,128)(2,1)} %get-tuple-element.73.x_ref.refs_2_, ...), custom_call_target="tpu_custom_call" | custom-call | flops 53150220288 | bytes 103284736 | tf_op jit(solution)/shard_map/ffn/pallas_call | solution.py:396
  332.4 112.0 %ffn_scatter.1 = (bf16[12,704,512]{2,1,0:T(8,128)(2,1)}, bf16[512,2048]{1,0:T(8,128)(2,1)}, bf16[512,2048]{1,0:T(8,128)(2,1)}, f32[16,2048]{1,0:T(8,128)}, f32[1...) custom-call(bf16[512,2048]{1,0:T(8,128)(2,1)} %all-gather.6.cloned.1.call-done.x_ref.refs_3_, ...), custom_call_target="tpu_custom_call" | custom-call | flops 53150220288 | bytes 103284736 | tf_op jit(solution)/shard_map/ffn_scatter/pallas_call | solution.py:396
  448.2 54.5 %shared_in_grads.1 = (f32[2816,256]{1,0:T(8,128)}, f32[352,256]{1,0:T(8,128)}) custom-call(bf16[8448,512]{1,0:T(8,128)(2,1)} %bitcast.88, bf16[8448,512]{1,0:T(8,128)(2,1)} %bitcast.90, bf16[512,2048]{1,0:T(8,128)(2,1)S(1)} %copy-done.14, bf16[512,2048]{1,0:T(8,128)(2,1)S(1)} %copy-done.16), custom_call_target="tpu_custom_call" | custom-call | flops 11811160064 | bytes 12845056 | tf_op jit(solution)/shard_map/shared_in_grads/pallas_call | solution.py:200
  510.4 100.9 %expert_in_grads.1 = (f32[5632,256]{1,0:T(8,128)}, f32[352,256]{1,0:T(8,128)}) custom-call(bf16[8448,512]{1,0:T(8,128)(2,1)} %bitcast.89, bf16[8448,512]{1,0:T(8,128)(2,1)} %bitcast.91, bf16[512,2048]{1,0:T(8,128)(2,1)S(1)} %copy-done.15, bf16[512,2048]{1,0:T(8,128)(2,1)S(1)} %copy-done.17), custom_call_target="tpu_custom_call" | custom-call | flops 23622320128 | bytes 21495808 | tf_op jit(solution)/shard_map/expert_in_grads/pallas_call | solution.py:200
  611.5 5.4 convolution_convert_fusion.1.dm_ref
  616.9 18.5 %attend_back.1 = (bf16[3,1024,512]{2,1,0:T(8,128)(2,1)S(1)}, bf16[3,512,1024]{2,1,0:T(8,128)(2,1)S(1)}, f32[3,1,512]{2,1,0:T(1,128)S(1)}) custom-call(s32[1]{0:T(128)} %copy.49.length_ref, bf16[3,1024,512]{2,1,0:T(8,128)(2,1)S(1)} %copy-done.3, bf16[3,1024,512]{2,1,0:T(8,128)(2,1)S(1)} %copy-done.3, bf16[3,1024,512]{2,1,0:T(8,128)(2,1)S(1)} %copy-done.3, ...), custom_call_target="tpu_custom_call" | custom-call | flops 5368709120 | bytes 10485760 | tf_op jit(solution)/shard_map/attend_back/pallas_call | solution.py:548
  637.2 10.3 %qkv_back.1 = (bf16[1024,2048]{1,0:T(8,128)(2,1)}, f32[1,2048]{1,0:T(1,128)S(1)}) custom-call(bf16[3,1024,512]{2,1,0:T(8,128)(2,1)S(1)} %get-tuple-element.98.d_ref, bf16[3,2048,512]{2,1,0:T(8,128)(2,1)} %bitcast.85, bf16[1024,2048]{1,0:T(8,128)(2,1)} %all-gather.4.cloned.1.call-done.x_ref.refs_1_), custom_call_target="tpu_custom_call" | custom-call | flops 6442450944 | bytes 14680064 | tf_op jit(solution)/shard_map/qkv_back/pallas_call | solution.py:584
  647.5 6.0 reduce-scatter.12.cloned.1.call-done
  654.5 3.6 copy.37
  658.1 5.8 copy.38
  664.6 16.1 %small_sums.1 = f32[12,2048]{1,0:T(8,128)} custom-call(f32[12,2048]{1,0:T(8,128)} %select_maximum_fusion.part_ref), custom_call_target="tpu_custom_call" | custom-call | tf_op jit(solution)/shard_map/small_sums/pallas_call | solution.py:883
  687.3 15.9 %mix_grads.1 = (f32[512,256]{1,0:T(8,128)S(1)}, f32[256,256]{1,0:T(8,128)}) custom-call(bf16[512,1024]{1,0:T(8,128)(2,1)S(1)} %copy-done.19, bf16[1024,2048]{1,0:T(8,128)(2,1)S(1)} %copy-done.13), custom_call_target="tpu_custom_call" | custom-call | flops 2147483648 | bytes 5767168 | tf_op jit(solution)/shard_map/mix_grads/pallas_call | solution.py:200
  703.2 34.8 %qkv_grads.1 = (f32[1536,256]{1,0:T(8,128)S(1)}, f32[384,256]{1,0:T(8,128)}) custom-call(bf16[1536,1024]{1,0:T(8,128)(2,1)S(1)} %bitcast.64, bf16[1024,2048]{1,0:T(8,128)(2,1)} %all-gather.4.cloned.1.call-done.x_ref.refs_1_), custom_call_target="tpu_custom_call" | custom-call | flops 6442450944 | bytes 8912896 | tf_op jit(solution)/shard_map/qkv_grads/pallas_call | solution.py:200
  739.2 3.0 copy.36
  742.3 2.6 add_convert_fusion
  746.8 3.2 fusion.7
  750.8 5.9 copy.51
  (145 shorter events, 41.2 us)
Async XLA Ops:
  7.2 6.1 copy-start.40
  7.2 6.2 copy-start.39
  7.2 6.2 copy-start.35
  7.2 6.2 copy-start.36
  7.2 89.0 %all-gather.4.cloned.1.call-start = ((), (), s32[]{:S(2)}) async-start(), calls=%async_computation.5 | async-start | bytes 5242880 | tf_op jit(solution)/shard_map/all_gather | solution.py:934
  12.6 318.6 %all-gather.6.cloned.1.call-start = ((), (), s32[]{:S(2)}) async-start(), calls=%async_computation.6 | async-start | bytes 2621440 | tf_op jit(solution)/shard_map/all_gather | solution.py:971
  54.8 52.5 %copy-start.7 = (f32[1024,128]{1,0:T(8,128)}, f32[1024,128]{1,0:T(8,128)S(1)}, u32[]{:S(2)}) copy-start(f32[1024,128]{1,0:T(8,128)S(1)} %get-tuple-element.67.cos_ref) | copy-start | bytes 1572868
  54.8 52.5 %copy-start.9 = (f32[1024,128]{1,0:T(8,128)}, f32[1024,128]{1,0:T(8,128)S(1)}, u32[]{:S(2)}) copy-start(f32[1024,128]{1,0:T(8,128)S(1)} %get-tuple-element.68.sin_ref) | copy-start | bytes 1572868
  107.4 10.0 %copy-start.2 = (bf16[3,1024,512]{2,1,0:T(8,128)(2,1)}, bf16[3,1024,512]{2,1,0:T(8,128)(2,1)S(1)}, u32[]{:S(2)}) copy-start(bf16[3,1024,512]{2,1,0:T(8,128)(2,1)S(1)} %project_qkv.1.q_ref.k_ref.v_ref) | copy-start | bytes 9437188
  107.4 10.0 %copy-start.41 = (bf16[512,2048]{1,0:T(8,128)(2,1)S(1)}, bf16[512,2048]{1,0:T(8,128)(2,1)}, u32[]{:S(2)}) copy-start(bf16[512,2048]{1,0:T(8,128)(2,1)} %param.22) | copy-start | bytes 6291460
  255.2 189.2 %reduce-scatter.6.cloned.1.call-start = ((), (), s32[]{:S(2)}) async-start(), calls=%async_computation.7 | async-start | bytes 2621440 | tf_op jit(solution)/shard_map/reduce_scatter | solution.py:975
  331.2 113.2 %reduce-scatter.8.cloned.1.call-start = ((), (), s32[]{:S(2)}) async-start(), calls=%async_computation.8 | async-start | bytes 2621440 | tf_op jit(solution)/shard_map/reduce_scatter | solution.py:976
  331.8 171.0 %reduce-scatter.10.cloned.1.call-start = ((), (), s32[]{:S(2)}) async-start(), calls=%async_computation.9 | async-start | bytes 2621440 | tf_op jit(solution)/shard_map/reduce_scatter | solution.py:991
  444.5 166.9 %all-gather.8.cloned.1.call-start = ((), (), s32[]{:S(2)}) async-start(), calls=%async_computation.10 | async-start | bytes 5242880 | tf_op jit(solution)/shard_map/all_gather | solution.py:1000
  507.0 146.4 %reduce-scatter.12.cloned.1.call-start = ((), (), s32[]{:S(2)}) async-start(), calls=%async_computation.11 | async-start | bytes 2621440 | tf_op jit(solution)/shard_map/reduce_scatter | solution.py:1006
  611.4 5.5 copy-start.8
  611.4 5.5 copy-start.10
  611.4 133.4 %reduce-scatter.14.cloned.1.call-start = ((), (), s32[]{:S(2)}) async-start(), calls=%async_computation.12 | async-start | bytes 5242880 | tf_op jit(solution)/shard_map/reduce_scatter | solution.py:1013
  611.5 5.4 copy-start.3
  658.1 5.8 copy-start.29
  658.1 27.1 %copy-start.19 = (bf16[512,1024]{1,0:T(8,128)(2,1)S(1)}, bf16[512,1024]{1,0:T(8,128)(2,1)}, u32[]{:S(2)}) copy-start(bf16[512,1024]{1,0:T(8,128)(2,1)} %copy-done.18) | copy-start | bytes 3145732
  687.3 15.9 %copy-start.21 = (bf16[3,512,1024]{2,1,0:T(8,128)(2,1)S(1)}, bf16[3,512,1024]{2,1,0:T(8,128)(2,1)}, u32[]{:S(2)}) copy-start(bf16[3,512,1024]{2,1,0:T(8,128)(2,1)} %copy-done.20) | copy-start | bytes 9437188
  703.2 34.9 %copy-start.11 = (f32[512,256]{1,0:T(8,128)}, f32[512,256]{1,0:T(8,128)S(1)}, u32[]{:S(2)}) copy-start(f32[512,256]{1,0:T(8,128)S(1)} %get-tuple-element.164) | copy-start | bytes 1572868
  750.8 5.9 copy-start.24
  (26 other events, 51.3 us)
Sparse Core Ops, SparseCore 0:
  12.7 83.4 all-gather.3
  255.3 45.3 all-gather.5
  331.4 43.2 reduce-scatter.5
  377.5 43.1 reduce-scatter.7
  444.6 41.9 reduce-scatter.9
  507.2 78.7 all-gather.7
  611.5 41.8 reduce-scatter.11
  656.3 77.0 reduce-scatter.13

commit v5 on v4

--- a/solution.py
+++ b/solution.py
@@ -49,7 +49,7 @@
     ]
 
 
-def scatter_steps(i, nc, lags, w, scratch, store):
+def scatter_steps(i, nc, lags, w, scratch, store, greet=None):
     own, sa, ra, kt, s1, r1, ku, s2, r2, sem_sa, sem_ra, sem_s1, sem_r1, sem_s2, sem_r2 = scratch
     la, lb, lc = lags
     keep_1 = min(3, lb + lc)
@@ -82,6 +82,9 @@
 
     @pl.when(i == 0)
     def _():
+        if greet is not None:
+            greet()
+            return
         barrier = pltpu.get_barrier_semaphore()
         for peer in (core_peer, x_peer, y_peer):
             pl.semaphore_signal(barrier, inc=1, device_id={"dp": peer}, device_id_type=MESH)
@@ -163,11 +166,11 @@
     def store(c, rows, result):
         @pl.when(c < cut)
         def _():
-            o_ref[rows, :] = result
+            o_ref[rows, :] = result.astype(o_ref.dtype)
 
         @pl.when(c >= cut)
         def _():
-            o2_ref[rows, :] = result
+            o2_ref[rows, :] = result.astype(o2_ref.dtype)
 
     send = scatter_steps(i, nc, (LA, LB, LC), o_ref.shape[1], refs[2 * pairs + 2 :], store)
 
@@ -188,7 +191,7 @@
         pl.BlockSpec((r, w), lambda i: (jnp.clip(i - lag, 0, cut - 1), 0)),
         pl.BlockSpec((r, w), lambda i: (jnp.clip(i - lag - cut, 0, rest - 1), 0)),
     ]
-    return specs, [jax.ShapeDtypeStruct((n * r, w), jnp.float32) for n in (cut, rest)]
+    return specs, [jax.ShapeDtypeStruct((n * r, w), jnp.bfloat16) for n in (cut, rest)]
 
 
 def weight_grad_scatter_kernel(a_list, b_list, r, cid, name, first, count, cut):
@@ -273,11 +276,11 @@
         def store(chunk, rows, result):
             @pl.when(chunk < experts)
             def _():
-                og_ref[rows, :] = result
+                og_ref[rows, :] = result.astype(og_ref.dtype)
 
             @pl.when(chunk >= experts)
             def _():
-                og2_ref[rows, :] = result
+                og2_ref[rows, :] = result.astype(og2_ref.dtype)
 
         send = scatter_steps(c, chunks, FFN_LAGS, og_ref.shape[1], scratch, store)
 
@@ -610,9 +613,7 @@
         jnp.dot(a[first * r : (first + count) * r], b, preferred_element_type=jnp.float32)
         for a, b in zip(a_list, b_list)
     )
-    result = lax.psum_scatter(
-        product.astype(jnp.bfloat16), "dp", scatter_dimension=1, tiled=True
-    ).astype(jnp.float32)
+    result = lax.psum_scatter(product.astype(jnp.bfloat16), "dp", scatter_dimension=1, tiled=True)
     return result[: cut * r], result[cut * r :]
 
 
@@ -823,9 +824,8 @@
     )(lengths, part.reshape(size, rows, width), tokens, gain[None], cot)
 
 
-def sums_body(
-    local_rows, part_ref, out_ref, from_dp, mine, from_tensor, send_dp, recv_dp, send_t, recv_t, send_out, recv_out
-):
+def small_sum_phases(local_rows, part_ref, out_ref, scratch):
+    staged, landed, from_dp, mine, from_tensor, send_dp, recv_dp, send_t, recv_t, send_out, recv_out = scratch
     size_dp, size_t = lax.axis_size("dp"), lax.axis_size("tensor")
     me_dp, me_t = lax.axis_index("dp"), lax.axis_index("tensor")
     width = mine.shape[1]
@@ -833,65 +833,153 @@
     def piece(ref, owner):
         return ref.at[:, pl.ds(pl.multiple_of(owner * width, width), width)]
 
-    barrier = pltpu.get_barrier_semaphore()
-    for step in range(1, size_dp):
-        peer = lax.rem(me_dp + step, size_dp)
-        pl.semaphore_signal(barrier, inc=1, device_id={"dp": peer}, device_id_type=MESH)
-    for step in range(1, size_t):
-        peer = lax.rem(me_t + step, size_t)
-        pl.semaphore_signal(barrier, inc=1, device_id={"tensor": peer}, device_id_type=MESH)
-    pl.semaphore_wait(barrier, size_dp + size_t - 2)
-
-    def send(source, target, axis, step, send_sem, recv_sem):
+    def greet():
+        barrier = pltpu.get_barrier_semaphore()
+        for step in range(1, size_dp):
+            peer = lax.rem(me_dp + step, size_dp)
+            pl.semaphore_signal(barrier, inc=1, device_id={"dp": peer}, device_id_type=MESH)
+        for step in range(1, size_t):
+            peer = lax.rem(me_t + step, size_t)
+            pl.semaphore_signal(barrier, inc=1, device_id={"tensor": peer}, device_id_type=MESH)
+        pl.semaphore_wait(barrier, size_dp + size_t - 2)
+
+    def copy(source, target, axis, step, send_sem, recv_sem):
         me, size = (me_dp, size_dp) if axis == "dp" else (me_t, size_t)
-        copy = pltpu.make_async_remote_copy(
+        return pltpu.make_async_remote_copy(
             src_ref=source, dst_ref=target, send_sem=send_sem.at[step], recv_sem=recv_sem.at[step],
             device_id={axis: lax.rem(me + step, size)}, device_id_type=MESH,
         )
-        copy.start()
-        return copy
-
-    first = [
-        send(piece(part_ref, lax.rem(me_dp + step, size_dp)), from_dp.at[step], "dp", step, send_dp, recv_dp)
-        for step in range(1, size_dp)
-    ]
-    total = piece(part_ref, me_dp)[...]
-    for step, copy in enumerate(first, 1):
-        copy.wait_recv()
-        total = total + from_dp[step]
-    mine[...] = total
-    second = [send(mine, from_tensor.at[step], "tensor", step, send_t, recv_t) for step in range(1, size_t)]
-    for step, copy in enumerate(second, 1):
-        copy.wait_recv()
-        total = total + from_tensor[step]
-    here = piece(out_ref, me_dp)
-    here[...] = total
-    piece(out_ref.at[local_rows:], me_dp)[...] = mine[local_rows:, :]
-    third = [send(here, here, "dp", step, send_out, recv_out) for step in range(1, size_dp)]
-    for copy in third:
-        copy.wait_recv()
-    for copy in first + second + third:
-        copy.wait_send()
-
-
-def small_sums(part, local_rows, cid):
+
+    def to_owner(step):
+        return copy(piece(staged, lax.rem(me_dp + step, size_dp)), from_dp.at[step], "dp", step, send_dp, recv_dp)
+
+    def to_tensor(step):
+        return copy(mine, from_tensor.at[step], "tensor", step, send_t, recv_t)
+
+    def to_all(step):
+        here = piece(landed, me_dp)
+        return copy(here, here, "dp", step, send_out, recv_out)
+
+    def first():
+        staged[...] = part_ref[...]
+        for step in range(1, size_dp):
+            to_owner(step).start()
+
+    def second():
+        total = piece(staged, me_dp)[...]
+        for step in range(1, size_dp):
+            to_owner(step).wait_recv()
+            total = total + from_dp[step]
+        mine[...] = total
+        for step in range(1, size_t):
+            to_tensor(step).start()
+
+    def third():
+        total = mine[...]
+        for step in range(1, size_t):
+            to_tensor(step).wait_recv()
+            total = total + from_tensor[step]
+        piece(landed, me_dp)[...] = total
+        piece(landed.at[local_rows:], me_dp)[...] = mine[local_rows:, :]
+        for step in range(1, size_dp):
+            to_all(step).start()
+
+    def last():
+        for step in range(1, size_dp):
+            to_all(step).wait_recv()
+        out_ref[...] = landed[...]
+        for step in range(1, size_dp):
+            to_owner(step).wait_send()
+            to_all(step).wait_send()
+        for step in range(1, size_t):
+            to_tensor(step).wait_send()
+
+    return greet, first, second, third, last
+
+
+def small_sum_scratch(shape):
     size_dp, size_t = lax.axis_size("dp"), lax.axis_size("tensor")
-    rows, width = part.shape[0], part.shape[1] // size_dp
-    vmem = pl.BlockSpec(memory_space=pltpu.VMEM)
+    rows, width = shape[0], shape[1] // size_dp
     dma = pltpu.SemaphoreType.DMA
     f32 = jnp.float32
+    return [
+        pltpu.VMEM(shape, f32), pltpu.VMEM(shape, f32),
+        pltpu.VMEM((size_dp, rows, width), f32), pltpu.VMEM((rows, width), f32), pltpu.VMEM((size_t, rows, width), f32),
+        dma((size_dp,)), dma((size_dp,)), dma((size_t,)), dma((size_t,)), dma((size_dp,)), dma((size_dp,)),
+    ]
+
+
+def sums_body(local_rows, part_ref, out_ref, *scratch):
+    for phase in small_sum_phases(local_rows, part_ref, out_ref, scratch):
+        phase()
+
+
+def small_sums(part, local_rows, cid):
+    vmem = pl.BlockSpec(memory_space=pltpu.VMEM)
     return pl.pallas_call(
         functools.partial(sums_body, local_rows),
         in_specs=[vmem],
         out_specs=vmem,
-        out_shape=jax.ShapeDtypeStruct(part.shape, f32),
-        scratch_shapes=[
-            pltpu.VMEM((size_dp, rows, width), f32), pltpu.VMEM((rows, width), f32), pltpu.VMEM((size_t, rows, width), f32),
-            dma((size_dp,)), dma((size_dp,)), dma((size_t,)), dma((size_t,)), dma((size_dp,)), dma((size_dp,)),
-        ],
+        out_shape=jax.ShapeDtypeStruct(part.shape, jnp.float32),
+        scratch_shapes=small_sum_scratch(part.shape),
         compiler_params=pltpu.CompilerParams(collective_id=cid, has_side_effects=True),
         name="small_sums",
     )(part)
+
+
+def attention_grads_body(nc, cut, local_rows, a_ref, a2_ref, b_ref, b2_ref, part_ref, o_ref, o2_ref, sums_ref, *scratch):
+    i = pl.program_id(0)
+    greet, *phases = small_sum_phases(local_rows, part_ref, sums_ref, scratch[:11])
+    steps = nc + LA + LB + LC
+
+    def store(c, rows, result):
+        @pl.when(c < cut)
+        def _():
+            o_ref[rows, :] = result.astype(o_ref.dtype)
+
+        @pl.when(c >= cut)
+        def _():
+            o2_ref[rows, :] = result.astype(o2_ref.dtype)
+
+    send = scatter_steps(i, nc, (LA, LB, LC), o_ref.shape[1], scratch[11:], store, greet)
+    for when, phase in zip((0, 4, 8, steps - 1), phases):
+        pl.when(i == when)(phase)
+
+    @pl.when(i < cut)
+    def _():
+        send(lambda cols: jnp.dot(a_ref[...], b_ref[:, cols], preferred_element_type=jnp.float32))
+
+    @pl.when((i >= cut) & (i < nc))
+    def _():
+        send(lambda cols: jnp.dot(a2_ref[...], b2_ref[:, cols], preferred_element_type=jnp.float32))
+
+
+def attention_grads(a, b, a2, b2, part, local_rows, r, cid):
+    T, D = b.shape
+    w = D // 8
+    cut, rest = a.shape[0] // r, a2.shape[0] // r
+    nc = cut + rest
+    lag = LA + LB + LC
+    out_specs, out_shape = scatter_outs(nc, cut, lag, r, w)
+
+    def whole(shape):
+        return pl.BlockSpec(shape, lambda i: (0, 0), pipeline_mode=pl.Buffered(1))
+
+    return pl.pallas_call(
+        functools.partial(attention_grads_body, nc, cut, local_rows),
+        grid=(nc + lag,),
+        in_specs=[
+            pl.BlockSpec((r, T), lambda i: (jnp.minimum(i, cut - 1), 0)),
+            pl.BlockSpec((r, T), lambda i: (jnp.clip(i - cut, 0, rest - 1), 0)),
+            whole((T, D)), whole((T, D)), whole(part.shape),
+        ],
+        out_specs=[*out_specs, whole(part.shape)],
+        out_shape=[*out_shape, jax.ShapeDtypeStruct(part.shape, jnp.float32)],
+        scratch_shapes=[*small_sum_scratch(part.shape), *scatter_scratch(r, w)],
+        compiler_params=pltpu.CompilerParams(vmem_limit_bytes=48 * MIB, collective_id=cid, has_side_effects=True),
+        cost_estimate=pl.CostEstimate(flops=2 * nc * r * T * D, bytes_accessed=2 * nc * r * T + 4 * T * D, transcendentals=0),
+        name="attention_grads",
+    )(a, a2, b, b2, part)
 
 
 def on_device(
@@ -989,6 +1077,7 @@
     d_gate_up = [d.reshape(chunks * 2 * eff, -1) for d in (dgu_a, dgu_b)]
     grad_a, two_a, dn_b = lax.optimization_barrier((grad_a, two_a, dn_b))
     grad_b = lax.psum_scatter(dn_b, "tensor", scatter_dimension=0, tiled=True)
+    two_b = lax.psum_scatter(bt_b, "tensor", scatter_dimension=0, tiled=True)
     in_grads_b, _ = weight_grad_scatter(
         d_gate_up, [x_a, x_b], eff, 4, "shared_in_grads", 2 * experts, 2 * shared_chunks
     )
@@ -1002,8 +1091,7 @@
     in_grads_a, _ = weight_grad_scatter(
         d_gate_up, [x_a, x_b], eff, 3, "expert_in_grads", 0, 2 * experts
     )
-    d_one, in_grads_a, bt_b = lax.optimization_barrier((d_one, in_grads_a, bt_b))
-    two_b = lax.psum_scatter(bt_b, "tensor", scatter_dimension=0, tiled=True)
+    d_one, in_grads_a = lax.optimization_barrier((d_one, in_grads_a))
     d_mixed = lax.dot_general(d_one, out_weight, NT, preferred_element_type=jnp.float32).astype(bf)
     d_qkv, d_qkv_t, bias_part = attend_back(lengths, qkv, d_mixed, cos_table, sin_table)
     grad_one, norm_one_part = qkv_back(d_qkv, qkv_w, normed_one)
@@ -1020,36 +1108,41 @@
         ],
         axis=0,
     )
-    sums = small_sums(part, experts + 3, 7)
-    qkv_sum, _ = weight_grad_scatter(
-        [d_qkv_t.reshape(3 * qkv_cols, slot_count)], [normed_one], 3 * qkv_cols // 4, 5, "qkv_grads"
-    )
-    out_sum, _ = weight_grad_scatter([mixed_t], [d_one], qkv_cols // 2, 6, "mix_grads")
+    d_qkv_t = d_qkv_t.reshape(3 * qkv_cols, slot_count)
+    if lax.axis_size("dp") == 8:
+        qkv_sum, out_sum, sums = attention_grads(
+            d_qkv_t, normed_one, mixed_t, d_one, part, experts + 3, qkv_cols // 2, 5
+        )
+    else:
+        sums = small_sums(part, experts + 3, 7)
+        qkv_sum, _ = weight_grad_scatter([d_qkv_t], [normed_one], qkv_cols, 5, "qkv_grads")
+        out_sum, _ = weight_grad_scatter([mixed_t], [d_one], qkv_cols, 6, "mix_grads")
     branch_two = jnp.concatenate([two_a, two_b], axis=0).astype(jnp.float32)
     output = (hidden + live_own * branch_two).astype(bf)
     grad_one = grad_one_own.astype(jnp.float32)
     input_grad = grad_hidden + norm_back(grad_one, unit_one, inv_one, gain_one)
     qkv_bias_grad = sums[experts + 3, : 3 * qkv_cols].reshape(3, qkv_cols)
     own_cols = out_grads.shape[1]
-    expert_in_grad = in_grads_a.reshape(experts, 2, eff, own_cols).transpose(0, 3, 1, 2)
+    expert_in_grad = in_grads_a.astype(jnp.float32).reshape(experts, 2, eff, own_cols).transpose(0, 3, 1, 2)
     shared_in_grad = (
         in_grads_b.reshape(shared_chunks, 2, eff, own_cols)
         .transpose(3, 1, 0, 2)
         .reshape(own_cols, 2, shared_chunks * eff)
+        .astype(jnp.float32)
     )
     return (
         output,
         input_grad,
         sums[experts + 1],
-        qkv_sum.reshape(3, qkv_cols, own_cols).transpose(2, 0, 1),
+        qkv_sum.astype(jnp.float32).reshape(3, qkv_cols, own_cols).transpose(2, 0, 1),
         qkv_bias_grad,
-        out_sum,
+        out_sum.astype(jnp.float32),
         sums[experts + 2],
         sums[:experts].T,
         expert_in_grad,
-        out_grads.reshape(experts, eff, own_cols),
+        out_grads.astype(jnp.float32).reshape(experts, eff, own_cols),
         shared_in_grad,
-        shared_out_grad,
+        shared_out_grad.astype(jnp.float32),
         sums[experts],
     )
 

time: 777 us -> 745 us (0.959)
  Pallas kernels: 592 us -> 570 us
  local copies, waits for them, and re-layouts: 81.6 us -> 64.2 us
  other arithmetic: 20.9 us -> 30.4 us
    pallas_call x4 -> x2, Pallas kernels: 206 us -> 155 us  [weight_grad_scatter_kernel(): pl.pallas_call(functools.partial(rs_body, count, cut, len(a_list)), grid=...]
    pallas_call x1, Pallas kernels: 16.1 us -> 45.9 us  [attention_grads(): pl.pallas_call(functools.partial(attention_grads_body, nc, cut, local_row...]
    unnamed x91 -> x97, local copies, waits for them, and re-layouts: 59.6 us -> 48 us
  transfers between devices with their start and end apart: 8 -> 8, of which waited for: 2 -> 2; matrix products, arithmetic and copies ran while one was open for 9% -> 10% of each run, Pallas kernels for 57% -> 57%
where the time goes in v5:
time: 745 us; the launch traced here: 735 us
  Pallas kernels  570 us (77%)
  local copies, waits for them, and re-layouts  64.2 us (9%)
  waiting for transfers between devices  44 us (6%)
  other arithmetic  30.4 us (4%)
  between operations  15.7 us (2%)
  matrix products  9.78 us (1%)
    pallas_call x2, Pallas kernels, ffn(): pl.pallas_call(functools.partial(ffn_body, experts, chunks, scatter), gri...  188 us
    pallas_call x2, Pallas kernels, weight_grad_scatter_kernel(): pl.pallas_call(functools.partial(rs_body, count, cut, len(a_list)), grid=...  155 us
    pallas_call x1, Pallas kernels, finish_branch(): pl.pallas_call(branch_body, in_specs=[pl.BlockSpec(memory_space=pltpu.SME...  132 us
    unnamed x97, local copies, waits for them, and re-layouts  48 us
    pallas_call x1, Pallas kernels, attention_grads(): pl.pallas_call(functools.partial(attention_grads_body, nc, cut, local_row...  45.9 us
    all_gather x1, waiting for transfers between devices, on_device(): lax.all_gather((unit_one * gain_one).astype(bf), 'tensor', axis=0, tiled=...  39.5 us
    pallas_call x1, Pallas kernels, attend_back(): pl.pallas_call(functools.partial(attend_back_body, rows), grid=(cols // H...  18.3 us
  transfers between devices with their start and end apart: 8, of which 2 were waited for; matrix products, arithmetic and copies ran while one was open for 10% of the time, Pallas kernels for 57%

profile of v5, /device:TPU:0, one launch (start us, length us, event | category | flops | bytes accessed | tf_op | source)
XLA Modules:
  0.0 735.3 jit_solution(7946738651612443829)
XLA Ops:
  10.0 2.5 fusion.3
  13.2 28.9 %copy.32 = bf16[2048,2,1408]{0,2,1:T(8,128)(2,1)} copy(bf16[2048,2,1408]{2,1,0:T(2,128)(2,1)} %param.27) | data formatting | bytes 23068672 | tf_op args[12]
  42.2 10.2 %copy.33 = bf16[4,2,352,2048]{3,2,1,0:T(8,128)(2,1)} copy(bf16[4,2,352,2048]{3,2,0,1:T(8,128)(2,1)} %bitcast.70) | data formatting | bytes 23068672 | tf_op jit(solution)/shard_map/transpose | solution.py:1029
  52.6 1.9 fusion.9
  56.7 39.5 %all-gather.4.cloned.1.call-done.x_ref.b_ref = bf16[1024,2048]{1,0:T(8,128)(2,1)} async-done(((bf16[256,2048]{1,0:T(8,128)(2,1)}), bf16[1024,2048]{1,0:T(8,128)(2,1)}) %all-gather.4.cloned.1.call-update) | async-done | bytes 4194320 | tf_op jit(solution)/shard_map/all_gather | solution.py:1022
  96.2 11.1 %project_qkv.1.q_ref.k_ref.v_ref = bf16[3,1024,512]{2,1,0:T(8,128)(2,1)S(1)} custom-call(bf16[1024,2048]{1,0:T(8,128)(2,1)} %all-gather.4.cloned.1.call-done.x_ref.b_ref, bf16[3,2048,512]{2,1,0:T(8,128)(2,1)} %bitcast.88, bf16[3,1,512]{2,1,0:T(2,128)(2,1)S(1)} %copy.34.bias_ref, f32[1024,128]{1,0:T(8,128)S(1)} %get-tuple-element.67.cos_ref, ...), custom_call_target="tpu_custom_call" | custom-call | flops 6442450944 | bytes 10485760 | tf_op jit(solution)/shard_map/project_qkv/pallas_call | solution.py:442
  107.3 9.9 %attend.1 = (bf16[1024,512]{1,0:T(8,128)(2,1)S(1)}, bf16[512,1024]{1,0:T(8,128)(2,1)S(1)}) custom-call(s32[1]{0:T(128)} %copy.45.length_ref, bf16[3,1024,512]{2,1,0:T(8,128)(2,1)S(1)} %project_qkv.1.q_ref.k_ref.v_ref, bf16[3,1024,512]{2,1,0:T(8,128)(2,1)S(1)} %project_qkv.1.q_ref.k_ref.v_ref, bf16[3,1024,512]{2,1,0:T(8,128)(2,1)S(1)} %project_qkv.1.q_ref.k_ref.v_ref), custom_call_target="tpu_custom_call" | custom-call | flops 2147483648 | bytes 5242880 | tf_op jit(solution)/shard_map/attend/pallas_call | solution.py:486
  117.3 4.4 convolution_convert_fusion
  121.7 132.0 %finish_branch.1 = (f32[256,2048]{1,0:T(8,128)S(1)}, bf16[128,2048]{1,0:T(8,128)(2,1)}, bf16[512,2048]{1,0:T(8,128)(2,1)}, bf16[512,2048]{1,0:T(8,128)(2,1)}, bf16[512,2048]{1,0:T(8,128)(2,1)}) custom-call(s32[1]{0:T(128)} %copy.45.length_ref, bf16[4,256,2048]{2,1,0:T(8,128)(2,1)} %bitcast.74, bf16[256,2048]{1,0:T(8,128)(2,1)S(1)} %copy-done.4, ...), custom_call_target="tpu_custom_call" | custom-call | bytes 50331648 | tf_op jit(solution)/shard_map/finish_branch/pallas_call | solution.py:810
  255.1 75.9 %ffn.1 = (bf16[12,704,512]{2,1,0:T(8,128)(2,1)}, bf16[512,2048]{1,0:T(8,128)(2,1)}, bf16[512,2048]{1,0:T(8,128)(2,1)}, f32[16,2048]{1,0:T(8,128)}, f32[1,2048]{1,0:T(1,128)}, /*index=5*/bf16[12,352,512]{2,1,0:T(8,128)(2,1)}) custom-call(bf16[512,2048]{1,0:T(8,128)(2,1)} %get-tuple-element.73.x_ref.refs_2_, ...), custom_call_target="tpu_custom_call" | custom-call | flops 53150220288 | bytes 103284736 | tf_op jit(solution)/shard_map/ffn/pallas_call | solution.py:399
  332.1 111.8 %ffn_scatter.1 = (bf16[12,704,512]{2,1,0:T(8,128)(2,1)}, bf16[512,2048]{1,0:T(8,128)(2,1)}, bf16[512,2048]{1,0:T(8,128)(2,1)}, f32[16,2048]{1,0:T(8,128)}, f32[1...) custom-call(bf16[512,2048]{1,0:T(8,128)(2,1)} %all-gather.6.cloned.1.call-done.x_ref.refs_3_, ...), custom_call_target="tpu_custom_call" | custom-call | flops 53150220288 | bytes 103284736 | tf_op jit(solution)/shard_map/ffn_scatter/pallas_call | solution.py:399
  447.8 54.3 %shared_in_grads.1 = (bf16[2816,256]{1,0:T(8,128)(2,1)S(1)}, bf16[352,256]{1,0:T(8,128)(2,1)}) custom-call(bf16[8448,512]{1,0:T(8,128)(2,1)} %bitcast.92, bf16[8448,512]{1,0:T(8,128)(2,1)} %bitcast.94, bf16[512,2048]{1,0:T(8,128)(2,1)S(1)} %copy-done.10, bf16[512,2048]{1,0:T(8,128)(2,1)S(1)} %copy-done.12), custom_call_target="tpu_custom_call" | custom-call | flops 11811160064 | bytes 12845056 | tf_op jit(solution)/shard_map/shared_in_grads/pallas_call | solution.py:203
  504.0 2.4 multiply_convert_fusion
  510.6 100.8 %expert_in_grads.1 = (bf16[5632,256]{1,0:T(8,128)(2,1)}, bf16[352,256]{1,0:T(8,128)(2,1)}) custom-call(bf16[8448,512]{1,0:T(8,128)(2,1)} %bitcast.93, bf16[8448,512]{1,0:T(8,128)(2,1)} %bitcast.95, bf16[512,2048]{1,0:T(8,128)(2,1)S(1)} %copy-done.11, bf16[512,2048]{1,0:T(8,128)(2,1)S(1)} %copy-done.13), custom_call_target="tpu_custom_call" | custom-call | flops 23622320128 | bytes 21495808 | tf_op jit(solution)/shard_map/expert_in_grads/pallas_call | solution.py:203
  611.5 5.4 convolution_convert_fusion.1.dm_ref
  616.9 18.3 %attend_back.1 = (bf16[3,1024,512]{2,1,0:T(8,128)(2,1)S(1)}, bf16[3,512,1024]{2,1,0:T(8,128)(2,1)S(1)}, f32[3,1,512]{2,1,0:T(1,128)S(1)}) custom-call(s32[1]{0:T(128)} %copy.45.length_ref, bf16[3,1024,512]{2,1,0:T(8,128)(2,1)S(1)} %copy-done.3, bf16[3,1024,512]{2,1,0:T(8,128)(2,1)S(1)} %copy-done.3, bf16[3,1024,512]{2,1,0:T(8,128)(2,1)S(1)} %copy-done.3, ...), custom_call_target="tpu_custom_call" | custom-call | flops 5368709120 | bytes 10485760 | tf_op jit(solution)/shard_map/attend_back/pallas_call | solution.py:551
  636.9 10.4 %qkv_back.1 = (bf16[1024,2048]{1,0:T(8,128)(2,1)}, f32[1,2048]{1,0:T(1,128)S(1)}) custom-call(bf16[3,1024,512]{2,1,0:T(8,128)(2,1)S(1)} %get-tuple-element.97.d_ref, bf16[3,2048,512]{2,1,0:T(8,128)(2,1)} %bitcast.89, bf16[1024,2048]{1,0:T(8,128)(2,1)} %all-gather.4.cloned.1.call-done.x_ref.b_ref), custom_call_target="tpu_custom_call" | custom-call | flops 6442450944 | bytes 14680064 | tf_op jit(solution)/shard_map/qkv_back/pallas_call | solution.py:587
  647.3 3.3 convert.10
  655.0 5.6 copy.38
  661.9 1.9 copy-done.17
  663.8 45.9 %attention_grads.1 = (bf16[1536,256]{1,0:T(8,128)(2,1)S(1)}, bf16[512,256]{1,0:T(8,128)(2,1)S(1)}, f32[12,2048]{1,0:T(8,128)S(1)}) custom-call(bf16[1536,1024]{1,0:T(8,128)(2,1)S(1)} %bitcast.69, bf16[512,1024]{1,0:T(8,128)(2,1)S(1)} %copy-done.15, bf16[1024,2048]{1,0:T(8,128)(2,1)} %all-gather.4.cloned.1.call-done.x_ref.b_ref, ...), custom_call_target="tpu_custom_call" | custom-call | flops 8589934592 | bytes 12582912 | tf_op jit(solution)/shard_map/attention_grads/pallas_call | solution.py:968
  712.6 5.1 convert_bitcast_fusion
  720.2 3.1 reduce-scatter.14.cloned.1.call-done
  725.1 3.1 fusion.7
  (153 shorter events, 32.0 us)
Async XLA Ops:
  7.2 89.0 %all-gather.4.cloned.1.call-start = ((), (), s32[]{:S(2)}) async-start(), calls=%async_computation.5 | async-start | bytes 5242880 | tf_op jit(solution)/shard_map/all_gather | solution.py:1022
  12.5 318.5 %all-gather.6.cloned.1.call-start = ((), (), s32[]{:S(2)}) async-start(), calls=%async_computation.6 | async-start | bytes 2621440 | tf_op jit(solution)/shard_map/all_gather | solution.py:1059
  42.2 10.2 %copy-start.44 = (bf16[2048]{0:T(1024)(128)(2,1)S(1)}, bf16[2048]{0:T(1024)(128)(2,1)}, u32[]{:S(2)}) copy-start(bf16[2048]{0:T(1024)(128)(2,1)} %param.29) | copy-start | bytes 12292
  42.2 10.2 %copy-start.45 = (bf16[3,512]{1,0:T(4,128)(2,1)S(1)}, bf16[3,512]{1,0:T(4,128)(2,1)}, u32[]{:S(2)}) copy-start(bf16[3,512]{1,0:T(4,128)(2,1)} %param.21) | copy-start | bytes 9220
  42.2 10.2 %copy-start.40 = (bf16[2048]{0:T(1024)(128)(2,1)S(1)}, bf16[2048]{0:T(1024)(128)(2,1)}, u32[]{:S(2)}) copy-start(bf16[2048]{0:T(1024)(128)(2,1)} %param.23) | copy-start | bytes 12292
  42.2 10.2 %copy-start.41 = (s32[1024,4]{0,1:T(4,128)S(1)}, s32[1024,4]{0,1:T(4,128)}, u32[]{:S(2)}) copy-start(s32[1024,4]{0,1:T(4,128)} %param.17) | copy-start | bytes 49156
  52.6 451.4 %copy-start.38 = (f32[256]{0:T(256)}, f32[256]{0:T(256)S(1)}, u32[]{:S(2)}) copy-start(f32[256]{0:T(256)S(1)} %compare_convert_fusion) | copy-start | bytes 3076
  54.9 52.4 %copy-start.6 = (f32[1024,128]{1,0:T(8,128)}, f32[1024,128]{1,0:T(8,128)S(1)}, u32[]{:S(2)}) copy-start(f32[1024,128]{1,0:T(8,128)S(1)} %get-tuple-element.67.cos_ref) | copy-start | bytes 1572868
  54.9 52.4 %copy-start.8 = (f32[1024,128]{1,0:T(8,128)}, f32[1024,128]{1,0:T(8,128)S(1)}, u32[]{:S(2)}) copy-start(f32[1024,128]{1,0:T(8,128)S(1)} %get-tuple-element.68.sin_ref) | copy-start | bytes 1572868
  107.3 10.0 %copy-start.2 = (bf16[3,1024,512]{2,1,0:T(8,128)(2,1)}, bf16[3,1024,512]{2,1,0:T(8,128)(2,1)S(1)}, u32[]{:S(2)}) copy-start(bf16[3,1024,512]{2,1,0:T(8,128)(2,1)S(1)} %project_qkv.1.q_ref.k_ref.v_ref) | copy-start | bytes 9437188
  107.3 10.0 %copy-start.46 = (bf16[512,2048]{1,0:T(8,128)(2,1)S(1)}, bf16[512,2048]{1,0:T(8,128)(2,1)}, u32[]{:S(2)}) copy-start(bf16[512,2048]{1,0:T(8,128)(2,1)} %param.22) | copy-start | bytes 6291460
  255.1 188.9 %reduce-scatter.6.cloned.1.call-start = ((), (), s32[]{:S(2)}) async-start(), calls=%async_computation.7 | async-start | bytes 2621440 | tf_op jit(solution)/shard_map/reduce_scatter | solution.py:1063
  331.1 112.9 %reduce-scatter.8.cloned.1.call-start = ((), (), s32[]{:S(2)}) async-start(), calls=%async_computation.8 | async-start | bytes 2621440 | tf_op jit(solution)/shard_map/reduce_scatter | solution.py:1064
  331.7 170.4 %reduce-scatter.10.cloned.1.call-start = ((), (), s32[]{:S(2)}) async-start(), calls=%async_computation.9 | async-start | bytes 2621440 | tf_op jit(solution)/shard_map/reduce_scatter | solution.py:1079
  444.0 167.4 %all-gather.8.cloned.1.call-start = ((), (), s32[]{:S(2)}) async-start(), calls=%async_computation.10 | async-start | bytes 5242880 | tf_op jit(solution)/shard_map/all_gather | solution.py:1089
  444.1 59.9 %copy-start.30 = (f32[2048]{0:T(1024)}, f32[2048]{0:T(1024)S(1)}, u32[]{:S(2)}) copy-start(f32[2048]{0:T(1024)S(1)} %convert_element_type.105) | copy-start | bytes 24580
  506.5 140.8 %reduce-scatter.12.cloned.1.call-start = ((), (), s32[]{:S(2)}) async-start(), calls=%async_computation.11 | async-start | bytes 2621440 | tf_op jit(solution)/shard_map/reduce_scatter | solution.py:1080
  507.2 216.1 %reduce-scatter.14.cloned.1.call-start = ((), (), s32[]{:S(2)}) async-start(), calls=%async_computation.12 | async-start | bytes 5242880 | tf_op jit(solution)/shard_map/reduce_scatter | solution.py:1101
  655.0 5.6 copy-start.28
  655.0 5.6 copy-start.26
  655.0 5.6 copy-start.35
  712.6 6.3 copy-start.24
  712.6 6.3 copy-start.25
  712.6 6.3 copy-start.39
  (31 other events, 82.9 us)
Sparse Core Ops, SparseCore 0:
  12.7 83.4 all-gather.3
  255.2 45.3 all-gather.5
  331.2 43.2 reduce-scatter.5
  377.3 43.1 reduce-scatter.7
  444.1 42.0 reduce-scatter.9
  506.6 78.7 all-gather.7
  587.8 42.3 reduce-scatter.11
  647.4 75.8 reduce-scatter.13

commit v6 on v5

--- a/solution.py
+++ b/solution.py
@@ -219,17 +219,39 @@
 
 
 def ffn_body(
-    experts, chunks, scatter,
+    experts, chunks, scatter, gather,
     x_ref, d_ref, routes_ref, rw_ref, ei_ref, si_ref, eo_ref, so_ref, *refs,
 ):
     if scatter:
         s_other_ref, d_other_ref, dgu_ref, dn_ref, bt_ref, rg_ref, np_ref, og_ref, og2_ref, *refs = refs
     else:
+        if gather:
+            own_x_ref, own_d_ref, *refs = refs
         dgu_ref, dn_ref, bt_ref, rg_ref, np_ref, s_ref, *refs = refs
+        if gather:
+            all_x_ref, all_d_ref, *refs = refs
     dn_acc, bt_acc, probs_ref, w_ref, ds_ref, wi_buf, wd_buf, sem, *scratch = refs
     c = pl.program_id(0)
     h = eo_ref.shape[1]
     slots, width = x_ref.shape
+    if gather:
+        me, size = lax.axis_index("tensor"), lax.axis_size("tensor")
+        local_sem, *sems = scratch
+        lines = []
+        for number, (own, out) in enumerate(((own_x_ref, all_x_ref), (own_d_ref, all_d_ref))):
+            def block(owner, out=out, rows=own.shape[0]):
+                return out.at[pl.ds(pl.multiple_of(owner * rows, rows), rows)]
+
+            lines.append(
+                line_gather(me, size, own, block, local_sem.at[number], sems[4 * number : 4 * number + 4])
+            )
+        for hop in range(size - 1):
+            @pl.when(c == -(-hop * (chunks - 1) // (size - 1)))
+            def _():
+                if hop == 0:
+                    line_barrier(me, size)
+                for advance, _ in lines:
+                    advance(hop)
 
     def fetch(step):
         slot = step % 2
@@ -324,7 +346,7 @@
             dn_acc[:, cols] += lax.dot_general(dgu, wi[:, cols], TN, preferred_element_type=jnp.float32)
             bt_acc[:, cols] += lax.dot_general(s, wd[:, cols], TN, preferred_element_type=jnp.float32)
 
-    @pl.when(c == chunks - 1)
+    @pl.when(c == (chunks if scatter else chunks - 1))
     def _():
         probs = probs_ref[...]
         d_probs = ds_ref[:experts, :] * picked()
@@ -345,9 +367,13 @@
             dn_ref[:, cols] = total.astype(dn_ref.dtype)
             np_ref[:, cols] = jnp.sum(total * x_ref[:, cols].astype(jnp.float32), axis=0, keepdims=True)
         bt_ref[...] = bt_acc[...].astype(bt_ref.dtype)
-
-
-def ffn(x, d_two, routes_t, router_rows, ei, si, eo, so, other=None):
+        if gather:
+            for advance, finish in lines:
+                advance(size - 1)
+                finish()
+
+
+def ffn(x, d_two, routes_t, router_rows, ei, si, eo, so, other=None, own=None):
     experts, h2, width = ei.shape
     chunks = experts + si.shape[0]
     h = h2 // 2
@@ -396,8 +422,17 @@
         out_shape.append(jax.ShapeDtypeStruct((chunks, h, slots), bf))
         grid = (chunks,)
         params = pltpu.CompilerParams(vmem_limit_bytes=62 * MIB)
+        if own is not None:
+            size = lax.axis_size("tensor")
+            dma = pltpu.SemaphoreType.DMA
+            in_specs += [anywhere, anywhere]
+            args += own
+            out_specs += [anywhere, anywhere]
+            out_shape += [jax.ShapeDtypeStruct((size * a.shape[0], width), bf) for a in own]
+            scratch += [dma((2,)), *[dma((size,))] * 8]
+            params = pltpu.CompilerParams(vmem_limit_bytes=62 * MIB, collective_id=8, has_side_effects=True)
     return pl.pallas_call(
-        functools.partial(ffn_body, experts, chunks, scatter),
+        functools.partial(ffn_body, experts, chunks, scatter, own is not None),
         grid=grid,
         in_specs=in_specs,
         out_specs=out_specs,
@@ -685,25 +720,25 @@
 
 
 def branch_body(
-    length_ref, part_ref, tokens_ref, gain_ref, cot_ref, hidden_ref, second_ref, xa_ref, da_ref, db_ref,
+    length_ref, part_ref, tokens_ref, gain_ref, cot_ref, hidden_ref, second_ref, xa_ref, da_ref,
     from_left, from_right, normed, local_sem, send_r, recv_r, send_l, recv_l, *sems,
 ):
     me = lax.axis_index("tensor")
     size = lax.axis_size("tensor")
     rows = tokens_ref.shape[0]
-    half = rows // 2
+    half, quarter = rows // 2, rows // 4
     bf, f32 = jnp.bfloat16, jnp.float32
     has_left, has_right = me > 0, me < size - 1
     line_barrier(me, size)
 
-    def place(ref, owner):
-        return ref.at[pl.ds(pl.multiple_of(owner * half, half), half)]
+    def gathered(owner, h):
+        return da_ref.at[pl.ds(pl.multiple_of(owner * half + h * quarter, quarter), quarter)]
 
     def own_cot(h):
-        return cot_ref.at[pl.ds(h * half, half)]
-
-    def part(ref, owner, h):
-        return ref.at[owner, pl.ds(h * half, half)]
+        return cot_ref.at[pl.ds(h * quarter, quarter)]
+
+    def part(ref, owner, which):
+        return ref.at[owner, pl.ds(pl.multiple_of(which * quarter, quarter), quarter)]
 
     def direction(right):
         slots, send, recv = (from_left, send_r, recv_r) if right else (from_right, send_l, recv_l)
@@ -718,64 +753,60 @@
                 device_id={"tensor": to}, device_id_type=MESH,
             )
 
-        def sent(t):
-            copy(part(part_ref, 0, 0), part(slots, 0, 0), t).wait_send()
+        def sends(s):
+            return has_to & (s - before - 1 < 2 * (size - 1 - before))
 
         def step(t):
             s, h = t // 2, t % 2
-            gathered = (da_ref, db_ref)[h]
             if t >= 2:
-                @pl.when(has_to)
+                @pl.when(sends(s - 1))
                 def _():
-                    sent(t - 2)
-
-            @pl.when(s <= before)
+                    copy(part(part_ref, 0, 0), part(slots, 0, 0), t - 2).wait_send()
+
+            if s < size:
+                @pl.when(s <= before)
+                def _():
+                    owner = me - s if right else me + s
+                    if s > 0:
+                        copy(own_cot(h), gathered(owner, h), t - 2).wait_recv()
+
+                    @pl.when(has_to)
+                    def _():
+                        copy(own_cot(h) if s == 0 else gathered(owner, h), gathered(owner, h), t).start()
+
+            @pl.when((s > before) & sends(s))
             def _():
-                owner = me - s if right else me + s
-                if s > 0:
-                    copy(own_cot(h), place(gathered, owner), t - 2).wait_recv()
-
-                @pl.when(has_to)
-                def _():
-                    copy(own_cot(h) if s == 0 else place(gathered, owner), place(gathered, owner), t).start()
-
-            @pl.when(s > before)
-            def _():
-                owner = size + me - s if right else me + s - size
+                r = s - before - 1
+                owner = size - 1 - r // 2 if right else r // 2
+                which = 2 * (r % 2) + h
 
                 @pl.when(has_from)
                 def _():
-                    copy(part(part_ref, owner, h), part(slots, owner, h), t - 2).wait_recv()
-                    both = part(slots, owner, h)
-                    both[...] = (both[...].astype(f32) + part(part_ref, owner, h)[...].astype(f32)).astype(bf)
-                    copy(both, part(slots, owner, h), t).start()
+                    both = part(slots, owner, which)
+                    copy(part(part_ref, owner, which), both, t - 2).wait_recv()
+                    both[...] = (both[...].astype(f32) + part(part_ref, owner, which)[...].astype(f32)).astype(bf)
+                    copy(both, both, t).start()
 
                 @pl.when(jnp.logical_not(has_from))
                 def _():
-                    copy(part(part_ref, owner, h), part(slots, owner, h), t).start()
+                    copy(part(part_ref, owner, which), part(slots, owner, which), t).start()
 
         def last():
-            @pl.when(has_to)
-            def _():
-                sent(2 * size - 2)
-                sent(2 * size - 1)
-
             @pl.when(has_from)
             def _():
-                for h in range(2):
-                    copy(part(part_ref, me, h), part(slots, me, h), 2 * size - 2 + h).wait_recv()
+                for which in range(4):
+                    t = 2 * (before + 2 * (size - 1 - before)) + which
+                    copy(part(part_ref, me, which), part(slots, me, which), t).wait_recv()
                 hidden_ref[...] += slots[me].astype(f32)
 
         return step, last
 
-    local = [
-        pltpu.make_async_copy(own_cot(h), place(ref, me), local_sem.at[h]) for h, ref in enumerate((da_ref, db_ref))
-    ]
+    local = [pltpu.make_async_copy(own_cot(h), gathered(me, h), local_sem.at[h]) for h in range(2)]
     for copy in local:
         copy.start()
     step_r, last_r = direction(True)
     step_l, last_l = direction(False)
-    for t in range(2 * size):
+    for t in range(2 * (2 * size - 1) + 2):
         step_r(t)
         step_l(t)
     hidden_ref[...] = part_ref[me].astype(f32)
@@ -788,7 +819,8 @@
     inverse = lax.rsqrt(jnp.mean(hidden * hidden, axis=1, keepdims=True) + epsilon)
     normed[...] = (hidden * inverse * gain_ref[...].astype(f32)).astype(bf)
     step_x, finish_x = line_gather(
-        me, size, normed.at[:half], lambda owner: place(xa_ref, owner), local_sem.at[2], sems
+        me, size, normed.at[:half], lambda owner: xa_ref.at[pl.ds(pl.multiple_of(owner * half, half), half)],
+        local_sem.at[2], sems,
     )
     for j in range(size):
         step_x(j)
@@ -810,13 +842,13 @@
     return pl.pallas_call(
         branch_body,
         in_specs=[pl.BlockSpec(memory_space=pltpu.SMEM), vmem, vmem, vmem, anywhere],
-        out_specs=[vmem, vmem, anywhere, anywhere, anywhere],
+        out_specs=[vmem, vmem, anywhere, anywhere],
         out_shape=[
-            jax.ShapeDtypeStruct((rows, width), f32), jax.ShapeDtypeStruct((half, width), bf), gathered, gathered, gathered,
+            jax.ShapeDtypeStruct((rows, width), f32), jax.ShapeDtypeStruct((half, width), bf), gathered, gathered,
         ],
         scratch_shapes=[
             pltpu.VMEM((size, rows, width), bf), pltpu.VMEM((size, rows, width), bf), pltpu.VMEM((rows, width), bf),
-            dma((3,)), *[dma((2 * size,))] * 4, *[dma((size,))] * 4,
+            dma((3,)), *[dma((4 * size,))] * 4, *[dma((size,))] * 4,
         ],
         compiler_params=pltpu.CompilerParams(vmem_limit_bytes=48 * MIB, collective_id=cid, has_side_effects=True),
         cost_estimate=pl.CostEstimate(flops=0, bytes_accessed=24 * rows * size * width, transcendentals=0),
@@ -1048,7 +1080,7 @@
     branch_partial = jnp.dot(mixed, out_weight, preferred_element_type=jnp.float32).astype(bf)
     size_t = lax.axis_size("tensor")
     half = own_rows // 2
-    hidden, second, x_a, d_a, d_b = finish_branch(
+    hidden, second, x_a, d_a = finish_branch(
         lengths, branch_partial, tokens, norm_two, d_two_own, 1
     )
     inv_two = lax.rsqrt(jnp.mean(hidden * hidden, axis=-1, keepdims=True) + epsilon)
@@ -1056,10 +1088,10 @@
     routes_a, routes_b = (
         routes.reshape(size_t, 2, half, -1).transpose(1, 0, 2, 3).reshape(2, size_t * half, -1)
     )
-    x_b = lax.all_gather(second, "tensor", axis=0, tiled=True)
     weights = (router_rows, ei, si, eo, so)
-    dgu_a, dn_a, bt_a, router_a, np_a, s_a = ffn(x_a, d_a, routes_a.T, *weights)
-    x_b, dn_a, bt_a, s_a = lax.optimization_barrier((x_b, dn_a, bt_a, s_a))
+    dgu_a, dn_a, bt_a, router_a, np_a, s_a, x_b, d_b = ffn(
+        x_a, d_a, routes_a.T, *weights, own=[second, d_two_own[half:]]
+    )
     grad_a = lax.psum_scatter(dn_a, "tensor", scatter_dimension=0, tiled=True)
     two_a = lax.psum_scatter(bt_a, "tensor", scatter_dimension=0, tiled=True)
     if lax.axis_size("dp") == 8:

time: 745 us -> 734 us (0.985)
  Pallas kernels: 570 us -> 558 us
    pallas_call x1, Pallas kernels: 132 us -> 120 us  [finish_branch(): pl.pallas_call(branch_body, in_specs=[pl.BlockSpec(memory_space=pltpu.SME...]
    unnamed x97 -> x99, local copies, waits for them, and re-layouts: 48 us -> 48.8 us
  transfers between devices with their start and end apart: 8 -> 7, of which waited for: 2 -> 2; matrix products, arithmetic and copies ran while one was open for 10% -> 10% of each run, Pallas kernels for 57% -> 47%
where the time goes in v6:
time: 734 us; the launch traced here: 724 us
  Pallas kernels  558 us (76%)
  local copies, waits for them, and re-layouts  65.8 us (9%)
  waiting for transfers between devices  44.1 us (6%)
  other arithmetic  30.2 us (4%)
  between operations  15.9 us (2%)
  matrix products  9.74 us (1%)
    pallas_call x2, Pallas kernels, ffn(): pl.pallas_call(functools.partial(ffn_body, experts, chunks, scatter, own...  187 us
    pallas_call x2, Pallas kernels, weight_grad_scatter_kernel(): pl.pallas_call(functools.partial(rs_body, count, cut, len(a_list)), grid=...  155 us
    pallas_call x1, Pallas kernels, finish_branch(): pl.pallas_call(branch_body, in_specs=[pl.BlockSpec(memory_space=pltpu.SME...  120 us
    unnamed x99, local copies, waits for them, and re-layouts  48.8 us
    pallas_call x1, Pallas kernels, attention_grads(): pl.pallas_call(functools.partial(attention_grads_body, nc, cut, local_row...  46.8 us
    all_gather x1, waiting for transfers between devices, on_device(): lax.all_gather((unit_one * gain_one).astype(bf), 'tensor', axis=0, tiled=...  39.5 us
    pallas_call x1, Pallas kernels, attend_back(): pl.pallas_call(functools.partial(attend_back_body, rows), grid=(cols // H...  18.3 us
  transfers between devices with their start and end apart: 7, of which 2 were waited for; matrix products, arithmetic and copies ran while one was open for 10% of the time, Pallas kernels for 47%

profile of v6, /device:TPU:0, one launch (start us, length us, event | category | flops | bytes accessed | tf_op | source)
XLA Modules:
  0.0 724.3 jit_solution(17014462876607090600)
XLA Ops:
  10.1 2.5 fusion.3
  13.4 28.9 %copy.32 = bf16[2048,2,1408]{0,2,1:T(8,128)(2,1)} copy(bf16[2048,2,1408]{2,1,0:T(2,128)(2,1)} %param.27) | data formatting | bytes 23068672 | tf_op args[12]
  42.4 10.1 %copy.33 = bf16[4,2,352,2048]{3,2,1,0:T(8,128)(2,1)} copy(bf16[4,2,352,2048]{3,2,0,1:T(8,128)(2,1)} %bitcast.70) | data formatting | bytes 23068672 | tf_op jit(solution)/shard_map/transpose | solution.py:1061
  52.6 1.9 fusion.9
  56.7 39.5 %all-gather.3.cloned.1.call-done.x_ref.b_ref = bf16[1024,2048]{1,0:T(8,128)(2,1)} async-done(((bf16[256,2048]{1,0:T(8,128)(2,1)}), bf16[1024,2048]{1,0:T(8,128)(2,1)}) %all-gather.3.cloned.1.call-update) | async-done | bytes 4194320 | tf_op jit(solution)/shard_map/all_gather | solution.py:1054
  97.1 11.1 %project_qkv.1.q_ref.k_ref.v_ref = bf16[3,1024,512]{2,1,0:T(8,128)(2,1)S(1)} custom-call(bf16[1024,2048]{1,0:T(8,128)(2,1)} %all-gather.3.cloned.1.call-done.x_ref.b_ref, bf16[3,2048,512]{2,1,0:T(8,128)(2,1)} %bitcast.88, bf16[3,1,512]{2,1,0:T(2,128)(2,1)S(1)} %copy.34.bias_ref, f32[1024,128]{1,0:T(8,128)S(1)} %get-tuple-element.64.cos_ref, ...), custom_call_target="tpu_custom_call" | custom-call | flops 6442450944 | bytes 10485760 | tf_op jit(solution)/shard_map/project_qkv/pallas_call | solution.py:477
  108.2 9.9 %attend.1 = (bf16[1024,512]{1,0:T(8,128)(2,1)S(1)}, bf16[512,1024]{1,0:T(8,128)(2,1)S(1)}) custom-call(s32[1]{0:T(128)} %copy.45.length_ref, bf16[3,1024,512]{2,1,0:T(8,128)(2,1)S(1)} %project_qkv.1.q_ref.k_ref.v_ref, bf16[3,1024,512]{2,1,0:T(8,128)(2,1)S(1)} %project_qkv.1.q_ref.k_ref.v_ref, bf16[3,1024,512]{2,1,0:T(8,128)(2,1)S(1)} %project_qkv.1.q_ref.k_ref.v_ref), custom_call_target="tpu_custom_call" | custom-call | flops 2147483648 | bytes 5242880 | tf_op jit(solution)/shard_map/attend/pallas_call | solution.py:521
  118.2 4.4 convolution_convert_fusion
  122.6 119.8 %finish_branch.1 = (f32[256,2048]{1,0:T(8,128)S(1)}, bf16[128,2048]{1,0:T(8,128)(2,1)S(1)}, bf16[512,2048]{1,0:T(8,128)(2,1)}, bf16[512,2048]{1,0:T(8,128)(2,1)}) custom-call(s32[1]{0:T(128)} %copy.45.length_ref, bf16[4,256,2048]{2,1,0:T(8,128)(2,1)} %bitcast.74, bf16[256,2048]{1,0:T(8,128)(2,1)S(1)} %copy-done.4, ...), custom_call_target="tpu_custom_call" | custom-call | bytes 50331648 | tf_op jit(solution)/shard_map/finish_branch/pallas_call | solution.py:842
  244.5 77.2 %ffn.1 = (bf16[12,704,512]{2,1,0:T(8,128)(2,1)}, bf16[512,2048]{1,0:T(8,128)(2,1)}, bf16[512,2048]{1,0:T(8,128)(2,1)}, f32[16,2048]{1,0:T(8,128)}, f32[1,2048]{1...) custom-call(bf16[512,2048]{1,0:T(8,128)(2,1)} %get-tuple-element.69.x_ref.refs_2_, ...), custom_call_target="tpu_custom_call" | custom-call | flops 53150220288 | bytes 103284736 | tf_op jit(solution)/shard_map/ffn/pallas_call | solution.py:434
  322.8 109.5 %ffn_scatter.1 = (bf16[12,704,512]{2,1,0:T(8,128)(2,1)}, bf16[512,2048]{1,0:T(8,128)(2,1)}, bf16[512,2048]{1,0:T(8,128)(2,1)}, f32[16,2048]{1,0:T(8,128)}, f32[1...) custom-call(bf16[512,2048]{1,0:T(8,128)(2,1)} %get-tuple-element.76.x_ref.refs_3_, ...), custom_call_target="tpu_custom_call" | custom-call | flops 53150220288 | bytes 103284736 | tf_op jit(solution)/shard_map/ffn_scatter/pallas_call | solution.py:434
  436.1 54.2 %shared_in_grads.1 = (bf16[2816,256]{1,0:T(8,128)(2,1)S(1)}, bf16[352,256]{1,0:T(8,128)(2,1)}) custom-call(bf16[8448,512]{1,0:T(8,128)(2,1)} %bitcast.92, bf16[8448,512]{1,0:T(8,128)(2,1)} %bitcast.94, bf16[512,2048]{1,0:T(8,128)(2,1)S(1)} %copy-done.10, bf16[512,2048]{1,0:T(8,128)(2,1)S(1)} %copy-done.17), custom_call_target="tpu_custom_call" | custom-call | flops 11811160064 | bytes 12845056 | tf_op jit(solution)/shard_map/shared_in_grads/pallas_call | solution.py:203
  492.2 2.4 multiply_convert_fusion
  498.7 100.7 %expert_in_grads.1 = (bf16[5632,256]{1,0:T(8,128)(2,1)}, bf16[352,256]{1,0:T(8,128)(2,1)}) custom-call(bf16[8448,512]{1,0:T(8,128)(2,1)} %bitcast.93, bf16[8448,512]{1,0:T(8,128)(2,1)} %bitcast.95, bf16[512,2048]{1,0:T(8,128)(2,1)S(1)} %copy-done.11, bf16[512,2048]{1,0:T(8,128)(2,1)S(1)} %copy-done.18), custom_call_target="tpu_custom_call" | custom-call | flops 23622320128 | bytes 21495808 | tf_op jit(solution)/shard_map/expert_in_grads/pallas_call | solution.py:203
  599.5 5.4 convolution_convert_fusion.1.dm_ref
  604.9 18.3 %attend_back.1 = (bf16[3,1024,512]{2,1,0:T(8,128)(2,1)S(1)}, bf16[3,512,1024]{2,1,0:T(8,128)(2,1)S(1)}, f32[3,1,512]{2,1,0:T(1,128)S(1)}) custom-call(s32[1]{0:T(128)} %copy.45.length_ref, bf16[3,1024,512]{2,1,0:T(8,128)(2,1)S(1)} %copy-done.3, bf16[3,1024,512]{2,1,0:T(8,128)(2,1)S(1)} %copy-done.3, bf16[3,1024,512]{2,1,0:T(8,128)(2,1)S(1)} %copy-done.3, ...), custom_call_target="tpu_custom_call" | custom-call | flops 5368709120 | bytes 10485760 | tf_op jit(solution)/shard_map/attend_back/pallas_call | solution.py:586
  624.8 10.4 %qkv_back.1 = (bf16[1024,2048]{1,0:T(8,128)(2,1)}, f32[1,2048]{1,0:T(1,128)S(1)}) custom-call(bf16[3,1024,512]{2,1,0:T(8,128)(2,1)S(1)} %get-tuple-element.91.d_ref, bf16[3,2048,512]{2,1,0:T(8,128)(2,1)} %bitcast.89, bf16[1024,2048]{1,0:T(8,128)(2,1)} %all-gather.3.cloned.1.call-done.x_ref.b_ref), custom_call_target="tpu_custom_call" | custom-call | flops 6442450944 | bytes 14680064 | tf_op jit(solution)/shard_map/qkv_back/pallas_call | solution.py:622
  635.3 2.4 convert_element_type.116
  640.9 1.9 copy.37
  642.8 5.6 copy.38
  651.6 46.8 %attention_grads.1 = (bf16[1536,256]{1,0:T(8,128)(2,1)S(1)}, bf16[512,256]{1,0:T(8,128)(2,1)S(1)}, f32[12,2048]{1,0:T(8,128)S(1)}) custom-call(bf16[1536,1024]{1,0:T(8,128)(2,1)S(1)} %bitcast.69, bf16[512,1024]{1,0:T(8,128)(2,1)S(1)} %copy-done.13, bf16[1024,2048]{1,0:T(8,128)(2,1)} %all-gather.3.cloned.1.call-done.x_ref.b_ref, ...), custom_call_target="tpu_custom_call" | custom-call | flops 8589934592 | bytes 12582912 | tf_op jit(solution)/shard_map/attention_grads/pallas_call | solution.py:1000
  701.3 5.1 convert_bitcast_fusion
  709.0 3.1 reduce-scatter.14.cloned.1.call-done
  713.9 3.1 fusion.7
  (153 shorter events, 34.0 us)
Async XLA Ops:
  7.2 6.1 copy-start.46
  7.2 6.1 copy-start.45
  7.2 6.2 copy-start.41
  7.2 6.2 copy-start.42
  7.2 89.0 %all-gather.3.cloned.1.call-start = ((), (), s32[]{:S(2)}) async-start(), calls=%async_computation.5 | async-start | bytes 5242880 | tf_op jit(solution)/shard_map/all_gather | solution.py:1054
  12.6 419.7 %reduce-scatter.6.cloned.1.call-start = ((), (), s32[]{:S(2)}) async-start(), calls=%async_computation.6 | async-start | bytes 2621440 | tf_op jit(solution)/shard_map/reduce_scatter | solution.py:1095
  52.6 439.6 %copy-start.39 = (f32[256]{0:T(256)}, f32[256]{0:T(256)S(1)}, u32[]{:S(2)}) copy-start(f32[256]{0:T(256)S(1)} %compare_convert_fusion) | copy-start | bytes 3076
  54.9 53.3 %copy-start.6 = (f32[1024,128]{1,0:T(8,128)}, f32[1024,128]{1,0:T(8,128)S(1)}, u32[]{:S(2)}) copy-start(f32[1024,128]{1,0:T(8,128)S(1)} %get-tuple-element.64.cos_ref) | copy-start | bytes 1572868
  54.9 53.3 %copy-start.8 = (f32[1024,128]{1,0:T(8,128)}, f32[1024,128]{1,0:T(8,128)S(1)}, u32[]{:S(2)}) copy-start(f32[1024,128]{1,0:T(8,128)S(1)} %get-tuple-element.65.sin_ref) | copy-start | bytes 1572868
  108.2 10.0 %copy-start.2 = (bf16[3,1024,512]{2,1,0:T(8,128)(2,1)}, bf16[3,1024,512]{2,1,0:T(8,128)(2,1)S(1)}, u32[]{:S(2)}) copy-start(bf16[3,1024,512]{2,1,0:T(8,128)(2,1)S(1)} %project_qkv.1.q_ref.k_ref.v_ref) | copy-start | bytes 9437188
  108.2 10.0 %copy-start.47 = (bf16[512,2048]{1,0:T(8,128)(2,1)S(1)}, bf16[512,2048]{1,0:T(8,128)(2,1)}, u32[]{:S(2)}) copy-start(bf16[512,2048]{1,0:T(8,128)(2,1)} %param.22) | copy-start | bytes 6291460
  321.8 110.5 %reduce-scatter.8.cloned.1.call-start = ((), (), s32[]{:S(2)}) async-start(), calls=%async_computation.7 | async-start | bytes 2621440 | tf_op jit(solution)/shard_map/reduce_scatter | solution.py:1096
  322.5 167.8 %reduce-scatter.10.cloned.1.call-start = ((), (), s32[]{:S(2)}) async-start(), calls=%async_computation.8 | async-start | bytes 2621440 | tf_op jit(solution)/shard_map/reduce_scatter | solution.py:1111
  432.3 167.1 %all-gather.5.cloned.1.call-start = ((), (), s32[]{:S(2)}) async-start(), calls=%async_computation.9 | async-start | bytes 5242880 | tf_op jit(solution)/shard_map/all_gather | solution.py:1121
  432.4 59.8 %copy-start.31 = (f32[2048]{0:T(1024)}, f32[2048]{0:T(1024)S(1)}, u32[]{:S(2)}) copy-start(f32[2048]{0:T(1024)S(1)} %convert_element_type.105) | copy-start | bytes 24580
  494.7 140.6 %reduce-scatter.12.cloned.1.call-start = ((), (), s32[]{:S(2)}) async-start(), calls=%async_computation.10 | async-start | bytes 2621440 | tf_op jit(solution)/shard_map/reduce_scatter | solution.py:1112
  495.3 216.9 %reduce-scatter.14.cloned.1.call-start = ((), (), s32[]{:S(2)}) async-start(), calls=%async_computation.11 | async-start | bytes 5242880 | tf_op jit(solution)/shard_map/reduce_scatter | solution.py:1133
  599.5 5.4 copy-start.3
  642.8 5.6 copy-start.29
  642.8 5.6 copy-start.27
  642.8 5.6 copy-start.36
  701.3 6.3 copy-start.25
  701.3 6.3 copy-start.26
  701.3 6.3 copy-start.40
  (31 other events, 79.9 us)
Sparse Core Ops, SparseCore 0:
  12.7 83.4 all-gather.2
  321.9 43.6 reduce-scatter.5
  368.0 43.1 reduce-scatter.7
  432.4 42.6 reduce-scatter.9
  494.8 79.5 all-gather.4
  576.6 42.4 reduce-scatter.11
  635.4 76.6 reduce-scatter.13

commit v7 on v6

--- a/solution.py
+++ b/solution.py
@@ -12,6 +12,7 @@
 LA, LB, LC = 1, 2, 2
 FFN_LAGS = (1, 1, 1)
 MIB = 2**20
+ATTEND_HEADS = 1
 
 
 epsilon = 1e-06
@@ -513,7 +514,7 @@
 
 def attend(lengths, qkv):
     _, slots, cols = qkv.shape
-    rows = min(256, slots)
+    rows = min(512, slots)
 
     def part(j):
         return pl.BlockSpec((1, slots, HEAD_DIM), lambda h: (j, 0, h))
@@ -540,66 +541,72 @@
     rows, length_ref, q_ref, k_ref, v_ref, dm_ref, cos_ref, sin_ref, out_ref, out_t_ref, bias_ref, dk_acc, dv_acc
 ):
     slots = q_ref.shape[1]
+    heads = [slice(n, n + HEAD_DIM) for n in range(0, q_ref.shape[2], HEAD_DIM)]
     scale = HEAD_DIM**-0.5
     bf, f32 = jnp.bfloat16, jnp.float32
 
-    def finish(j, here, grad):
+    def finish(j, here, head, grad):
         if j < 2:
             grad = grad * cos_ref[here, :] - turn(grad) * sin_ref[here, :]
         low = grad.astype(bf)
-        out_ref[j, here, :] = low
-        out_t_ref[j, :, here] = grad.T.astype(bf)
+        out_ref[j, here, head] = low
+        out_t_ref[j, head, here] = grad.T.astype(bf)
         return jnp.sum(low.astype(f32), axis=0, keepdims=True)
 
-    dq_sum = jnp.zeros((1, HEAD_DIM), f32)
+    dq_sums = [jnp.zeros((1, HEAD_DIM), f32) for _ in heads]
     starts = list(range(0, slots, rows))[::-1]
     for start in starts:
         here, end = slice(start, start + rows), start + rows
-        q, k, v, dm = q_ref[0, here, :], k_ref[0, :end, :], v_ref[0, :end, :], dm_ref[here, :]
-        p = block_probs(length_ref, q, k, start)
-        dp = lax.dot_general(dm, v, NT, preferred_element_type=f32)
-        ds = (p * (dp - jnp.sum(p * dp, axis=1, keepdims=True))).astype(bf)
-        dq_sum += finish(0, here, jnp.dot(ds, k, preferred_element_type=f32) * scale)
-        dk = lax.dot_general(ds, q, TN, preferred_element_type=f32) * scale
-        dv = lax.dot_general(p.astype(bf), dm, TN, preferred_element_type=f32)
-        if start == starts[0]:
-            dk_acc[...] = dk
-            dv_acc[...] = dv
-        else:
-            dk_acc[:end, :] += dk
-            dv_acc[:end, :] += dv
+        for n, head in enumerate(heads):
+            q, k, v = q_ref[0, here, head], k_ref[0, :end, head], v_ref[0, :end, head]
+            dm = dm_ref[here, head]
+            p = block_probs(length_ref, q, k, start)
+            dp = lax.dot_general(dm, v, NT, preferred_element_type=f32)
+            ds = (p * (dp - jnp.sum(p * dp, axis=1, keepdims=True))).astype(bf)
+            dq_sums[n] += finish(0, here, head, jnp.dot(ds, k, preferred_element_type=f32) * scale)
+            dk = lax.dot_general(ds, q, TN, preferred_element_type=f32) * scale
+            dv = lax.dot_general(p.astype(bf), dm, TN, preferred_element_type=f32)
+            if start == starts[0]:
+                dk_acc[n] = dk
+                dv_acc[n] = dv
+            else:
+                dk_acc[n, :end, :] += dk
+                dv_acc[n, :end, :] += dv
     every = slice(0, slots)
-    bias_ref[0] = dq_sum
-    bias_ref[1] = finish(1, every, dk_acc[...])
-    bias_ref[2] = finish(2, every, dv_acc[...])
+    for n, head in enumerate(heads):
+        bias_ref[0, :, head] = dq_sums[n]
+        bias_ref[1, :, head] = finish(1, every, head, dk_acc[n])
+        bias_ref[2, :, head] = finish(2, every, head, dv_acc[n])
 
 
 def attend_back(lengths, qkv, d_mixed, cos_table, sin_table):
     _, slots, cols = qkv.shape
-    rows = min(256, slots)
+    rows = min(512, slots)
     bf, f32 = jnp.bfloat16, jnp.float32
+    together = ATTEND_HEADS
+    wide = together * HEAD_DIM
 
     def part(j):
-        return pl.BlockSpec((1, slots, HEAD_DIM), lambda h: (j, 0, h))
+        return pl.BlockSpec((1, slots, wide), lambda h: (j, 0, h))
 
     table = pl.BlockSpec((slots, HEAD_DIM), lambda h: (0, 0), pipeline_mode=pl.Buffered(1))
     return pl.pallas_call(
         functools.partial(attend_back_body, rows),
-        grid=(cols // HEAD_DIM,),
+        grid=(cols // wide,),
         in_specs=[
             pl.BlockSpec(memory_space=pltpu.SMEM), part(0), part(1), part(2),
-            pl.BlockSpec((slots, HEAD_DIM), lambda h: (0, h)), table, table,
+            pl.BlockSpec((slots, wide), lambda h: (0, h)), table, table,
         ],
         out_specs=[
-            pl.BlockSpec((3, slots, HEAD_DIM), lambda h: (0, 0, h)), pl.BlockSpec((3, HEAD_DIM, slots), lambda h: (0, h, 0)),
-            pl.BlockSpec((3, 1, HEAD_DIM), lambda h: (0, 0, h)),
+            pl.BlockSpec((3, slots, wide), lambda h: (0, 0, h)), pl.BlockSpec((3, wide, slots), lambda h: (0, h, 0)),
+            pl.BlockSpec((3, 1, wide), lambda h: (0, 0, h)),
         ],
         out_shape=[
             jax.ShapeDtypeStruct((3, slots, cols), bf), jax.ShapeDtypeStruct((3, cols, slots), bf),
             jax.ShapeDtypeStruct((3, 1, cols), f32),
         ],
-        scratch_shapes=[pltpu.VMEM((slots, HEAD_DIM), f32), pltpu.VMEM((slots, HEAD_DIM), f32)],
-        compiler_params=pltpu.CompilerParams(vmem_limit_bytes=40 * MIB),
+        scratch_shapes=[pltpu.VMEM((together, slots, HEAD_DIM), f32)] * 2,
+        compiler_params=pltpu.CompilerParams(vmem_limit_bytes=56 * MIB),
         cost_estimate=pl.CostEstimate(
             flops=10 * slots * slots * cols, bytes_accessed=20 * slots * cols, transcendentals=slots * slots * cols // HEAD_DIM
         ),

time: 734 us -> 733 us (level)
    unnamed x99 -> x89, local copies, waits for them, and re-layouts: 48.8 us -> 49 us
where the time goes in v7:
time: 733 us; the launch traced here: 723 us
  Pallas kernels  556 us (76%)
  local copies, waits for them, and re-layouts  65.9 us (9%)
  waiting for transfers between devices  44.1 us (6%)
  other arithmetic  30.2 us (4%)
  between operations  15.8 us (2%)
  matrix products  10.6 us (1%)
    pallas_call x2, Pallas kernels, ffn(): pl.pallas_call(functools.partial(ffn_body, experts, chunks, scatter, own...  187 us
    pallas_call x2, Pallas kernels, weight_grad_scatter_kernel(): pl.pallas_call(functools.partial(rs_body, count, cut, len(a_list)), grid=...  155 us
    pallas_call x1, Pallas kernels, finish_branch(): pl.pallas_call(branch_body, in_specs=[pl.BlockSpec(memory_space=pltpu.SME...  120 us
    unnamed x89, local copies, waits for them, and re-layouts  49 us
    pallas_call x1, Pallas kernels, attention_grads(): pl.pallas_call(functools.partial(attention_grads_body, nc, cut, local_row...  46.8 us
    all_gather x1, waiting for transfers between devices, on_device(): lax.all_gather((unit_one * gain_one).astype(bf), 'tensor', axis=0, tiled=...  39.6 us
    pallas_call x1, Pallas kernels, attend_back(): pl.pallas_call(functools.partial(attend_back_body, rows), grid=(cols // w...  16.4 us
  transfers between devices with their start and end apart: 7, of which 2 were waited for; matrix products, arithmetic and copies ran while one was open for 10% of the time, Pallas kernels for 47%

profile of v7, /device:TPU:0, one launch (start us, length us, event | category | flops | bytes accessed | tf_op | source)
XLA Modules:
  0.0 722.9 jit_solution(10007741373406261134)
XLA Ops:
  10.1 2.5 fusion.3
  13.4 28.9 %copy.32 = bf16[2048,2,1408]{0,2,1:T(8,128)(2,1)} copy(bf16[2048,2,1408]{2,1,0:T(2,128)(2,1)} %param.27) | data formatting | bytes 23068672 | tf_op args[12]
  42.3 10.2 %copy.33 = bf16[4,2,352,2048]{3,2,1,0:T(8,128)(2,1)} copy(bf16[4,2,352,2048]{3,2,0,1:T(8,128)(2,1)} %bitcast.69) | data formatting | bytes 23068672 | tf_op jit(solution)/shard_map/transpose | solution.py:1068
  52.6 1.9 fusion.9
  56.7 39.6 %all-gather.3.cloned.1.call-done.x_ref.b_ref = bf16[1024,2048]{1,0:T(8,128)(2,1)} async-done(((bf16[256,2048]{1,0:T(8,128)(2,1)}), bf16[1024,2048]{1,0:T(8,128)(2,1)}) %all-gather.3.cloned.1.call-update) | async-done | bytes 4194320 | tf_op jit(solution)/shard_map/all_gather | solution.py:1061
  97.1 11.1 %project_qkv.1.q_ref.k_ref.v_ref = bf16[3,1024,512]{2,1,0:T(8,128)(2,1)S(1)} custom-call(bf16[1024,2048]{1,0:T(8,128)(2,1)} %all-gather.3.cloned.1.call-done.x_ref.b_ref, bf16[3,2048,512]{2,1,0:T(8,128)(2,1)} %bitcast.88, bf16[3,1,512]{2,1,0:T(2,128)(2,1)S(1)} %copy.34.bias_ref, f32[1024,128]{1,0:T(8,128)S(1)} %get-tuple-element.64.cos_ref, ...), custom_call_target="tpu_custom_call" | custom-call | flops 6442450944 | bytes 10485760 | tf_op jit(solution)/shard_map/project_qkv/pallas_call | solution.py:478
  108.2 9.4 %attend.1 = (bf16[1024,512]{1,0:T(8,128)(2,1)S(1)}, bf16[512,1024]{1,0:T(8,128)(2,1)S(1)}) custom-call(s32[1]{0:T(128)} %copy.45.length_ref, bf16[3,1024,512]{2,1,0:T(8,128)(2,1)S(1)} %project_qkv.1.q_ref.k_ref.v_ref, bf16[3,1024,512]{2,1,0:T(8,128)(2,1)S(1)} %project_qkv.1.q_ref.k_ref.v_ref, bf16[3,1024,512]{2,1,0:T(8,128)(2,1)S(1)} %project_qkv.1.q_ref.k_ref.v_ref), custom_call_target="tpu_custom_call" | custom-call | flops 2147483648 | bytes 5242880 | tf_op jit(solution)/shard_map/attend/pallas_call | solution.py:522
  117.7 4.4 convolution_convert_fusion
  122.1 119.8 %finish_branch.1 = (f32[256,2048]{1,0:T(8,128)S(1)}, bf16[128,2048]{1,0:T(8,128)(2,1)S(1)}, bf16[512,2048]{1,0:T(8,128)(2,1)}, bf16[512,2048]{1,0:T(8,128)(2,1)}) custom-call(s32[1]{0:T(128)} %copy.45.length_ref, bf16[4,256,2048]{2,1,0:T(8,128)(2,1)} %bitcast.73, bf16[256,2048]{1,0:T(8,128)(2,1)S(1)} %copy-done.3, ...), custom_call_target="tpu_custom_call" | custom-call | bytes 50331648 | tf_op jit(solution)/shard_map/finish_branch/pallas_call | solution.py:849
  243.9 77.3 %ffn.1 = (bf16[12,704,512]{2,1,0:T(8,128)(2,1)}, bf16[512,2048]{1,0:T(8,128)(2,1)}, bf16[512,2048]{1,0:T(8,128)(2,1)}, f32[16,2048]{1,0:T(8,128)}, f32[1,2048]{1...) custom-call(bf16[512,2048]{1,0:T(8,128)(2,1)} %get-tuple-element.69.x_ref.refs_2_, ...), custom_call_target="tpu_custom_call" | custom-call | flops 53150220288 | bytes 103284736 | tf_op jit(solution)/shard_map/ffn/pallas_call | solution.py:435
  322.2 109.6 %ffn_scatter.1 = (bf16[12,704,512]{2,1,0:T(8,128)(2,1)}, bf16[512,2048]{1,0:T(8,128)(2,1)}, bf16[512,2048]{1,0:T(8,128)(2,1)}, f32[16,2048]{1,0:T(8,128)}, f32[1...) custom-call(bf16[512,2048]{1,0:T(8,128)(2,1)} %get-tuple-element.76.x_ref.refs_3_, ...), custom_call_target="tpu_custom_call" | custom-call | flops 53150220288 | bytes 103284736 | tf_op jit(solution)/shard_map/ffn_scatter/pallas_call | solution.py:435
  435.7 54.2 %shared_in_grads.1 = (bf16[2816,256]{1,0:T(8,128)(2,1)S(1)}, bf16[352,256]{1,0:T(8,128)(2,1)}) custom-call(bf16[8448,512]{1,0:T(8,128)(2,1)} %bitcast.92, bf16[8448,512]{1,0:T(8,128)(2,1)} %bitcast.94, bf16[512,2048]{1,0:T(8,128)(2,1)S(1)} %copy-done.7, bf16[512,2048]{1,0:T(8,128)(2,1)S(1)} %copy-done.14), custom_call_target="tpu_custom_call" | custom-call | flops 11811160064 | bytes 12845056 | tf_op jit(solution)/shard_map/shared_in_grads/pallas_call | solution.py:204
  491.8 2.5 multiply_convert_fusion
  498.3 100.7 %expert_in_grads.1 = (bf16[5632,256]{1,0:T(8,128)(2,1)}, bf16[352,256]{1,0:T(8,128)(2,1)}) custom-call(bf16[8448,512]{1,0:T(8,128)(2,1)} %bitcast.93, bf16[8448,512]{1,0:T(8,128)(2,1)} %bitcast.95, bf16[512,2048]{1,0:T(8,128)(2,1)S(1)} %copy-done.8, bf16[512,2048]{1,0:T(8,128)(2,1)S(1)} %copy-done.15), custom_call_target="tpu_custom_call" | custom-call | flops 23622320128 | bytes 21495808 | tf_op jit(solution)/shard_map/expert_in_grads/pallas_call | solution.py:204
  599.1 6.2 convolution_convert_fusion.1.dm_ref
  605.3 16.4 %attend_back.1 = (bf16[3,1024,512]{2,1,0:T(8,128)(2,1)}, bf16[3,512,1024]{2,1,0:T(8,128)(2,1)}, f32[3,1,512]{2,1,0:T(1,128)}) custom-call(s32[1]{0:T(128)} %copy.45.length_ref, bf16[3,1024,512]{2,1,0:T(8,128)(2,1)} %copy-done.2, bf16[3,1024,512]{2,1,0:T(8,128)(2,1)} %copy-done.2, bf16[3,1024,512]{2,1,0:T(8,128)(2,1)} %copy-done.2, ...), custom_call_target="tpu_custom_call" | custom-call | flops 5368709120 | bytes 10485760 | tf_op jit(solution)/shard_map/attend_back/pallas_call | solution.py:593
  623.6 10.3 %qkv_back.1 = (bf16[1024,2048]{1,0:T(8,128)(2,1)}, f32[1,2048]{1,0:T(1,128)S(1)}) custom-call(bf16[3,1024,512]{2,1,0:T(8,128)(2,1)S(1)} %copy-done.13, bf16[3,2048,512]{2,1,0:T(8,128)(2,1)} %bitcast.89, bf16[1024,2048]{1,0:T(8,128)(2,1)} %all-gather.3.cloned.1.call-done.x_ref.b_ref), custom_call_target="tpu_custom_call" | custom-call | flops 6442450944 | bytes 14680064 | tf_op jit(solution)/shard_map/qkv_back/pallas_call | solution.py:629
  634.0 2.4 convert_element_type.116
  641.4 5.6 copy.38
  648.3 1.9 copy-done.12
  650.2 46.8 %attention_grads.1 = (bf16[1536,256]{1,0:T(8,128)(2,1)S(1)}, bf16[512,256]{1,0:T(8,128)(2,1)S(1)}, f32[12,2048]{1,0:T(8,128)S(1)}) custom-call(bf16[1536,1024]{1,0:T(8,128)(2,1)S(1)} %bitcast.68, bf16[512,1024]{1,0:T(8,128)(2,1)S(1)} %copy-done.10, bf16[1024,2048]{1,0:T(8,128)(2,1)} %all-gather.3.cloned.1.call-done.x_ref.b_ref, ...), custom_call_target="tpu_custom_call" | custom-call | flops 8589934592 | bytes 12582912 | tf_op jit(solution)/shard_map/attention_grads/pallas_call | solution.py:1007
  699.9 5.1 convert_bitcast_fusion
  707.5 3.2 reduce-scatter.14.cloned.1.call-done
  712.5 3.1 fusion.7
  (143 shorter events, 34.2 us)
Async XLA Ops:
  7.2 6.1 copy-start.41
  7.2 6.2 copy-start.40
  7.2 6.2 copy-start.35
  7.2 6.2 copy-start.36
  7.2 89.0 %all-gather.3.cloned.1.call-start = ((), (), s32[]{:S(2)}) async-start(), calls=%async_computation.5 | async-start | bytes 5242880 | tf_op jit(solution)/shard_map/all_gather | solution.py:1061
  12.6 419.2 %reduce-scatter.6.cloned.1.call-start = ((), (), s32[]{:S(2)}) async-start(), calls=%async_computation.6 | async-start | bytes 2621440 | tf_op jit(solution)/shard_map/reduce_scatter | solution.py:1102
  52.6 439.2 %copy-start.33 = (f32[256]{0:T(256)}, f32[256]{0:T(256)S(1)}, u32[]{:S(2)}) copy-start(f32[256]{0:T(256)S(1)} %compare_convert_fusion) | copy-start | bytes 3076
  54.9 53.3 %copy-start.5 = (f32[1024,128]{1,0:T(8,128)}, f32[1024,128]{1,0:T(8,128)S(1)}, u32[]{:S(2)}) copy-start(f32[1024,128]{1,0:T(8,128)S(1)} %get-tuple-element.64.cos_ref) | copy-start | bytes 1572868
  54.9 53.3 %copy-start.6 = (f32[1024,128]{1,0:T(8,128)}, f32[1024,128]{1,0:T(8,128)S(1)}, u32[]{:S(2)}) copy-start(f32[1024,128]{1,0:T(8,128)S(1)} %get-tuple-element.65.sin_ref) | copy-start | bytes 1572868
  108.2 9.4 %copy-start.2 = (bf16[3,1024,512]{2,1,0:T(8,128)(2,1)}, bf16[3,1024,512]{2,1,0:T(8,128)(2,1)S(1)}, u32[]{:S(2)}) copy-start(bf16[3,1024,512]{2,1,0:T(8,128)(2,1)S(1)} %project_qkv.1.q_ref.k_ref.v_ref) | copy-start | bytes 9437188
  108.2 9.4 %copy-start.42 = (bf16[512,2048]{1,0:T(8,128)(2,1)S(1)}, bf16[512,2048]{1,0:T(8,128)(2,1)}, u32[]{:S(2)}) copy-start(bf16[512,2048]{1,0:T(8,128)(2,1)} %param.22) | copy-start | bytes 6291460
  321.2 110.6 %reduce-scatter.8.cloned.1.call-start = ((), (), s32[]{:S(2)}) async-start(), calls=%async_computation.7 | async-start | bytes 2621440 | tf_op jit(solution)/shard_map/reduce_scatter | solution.py:1103
  322.0 167.9 %reduce-scatter.10.cloned.1.call-start = ((), (), s32[]{:S(2)}) async-start(), calls=%async_computation.8 | async-start | bytes 2621440 | tf_op jit(solution)/shard_map/reduce_scatter | solution.py:1118
  431.9 167.2 %all-gather.5.cloned.1.call-start = ((), (), s32[]{:S(2)}) async-start(), calls=%async_computation.9 | async-start | bytes 5242880 | tf_op jit(solution)/shard_map/all_gather | solution.py:1128
  494.3 139.6 %reduce-scatter.12.cloned.1.call-start = ((), (), s32[]{:S(2)}) async-start(), calls=%async_computation.10 | async-start | bytes 2621440 | tf_op jit(solution)/shard_map/reduce_scatter | solution.py:1119
  494.9 215.8 %reduce-scatter.14.cloned.1.call-start = ((), (), s32[]{:S(2)}) async-start(), calls=%async_computation.11 | async-start | bytes 5242880 | tf_op jit(solution)/shard_map/reduce_scatter | solution.py:1140
  641.4 5.6 copy-start.26
  641.4 5.6 copy-start.24
  641.4 5.6 copy-start.30
  641.4 5.7 copy-start.39
  699.9 6.3 copy-start.22
  699.9 6.3 copy-start.23
  699.9 6.3 copy-start.34
  707.5 5.0 copy-start.16
  (26 other events, 58.0 us)
Sparse Core Ops, SparseCore 0:
  12.7 83.4 all-gather.2
  321.4 43.5 reduce-scatter.5
  367.4 43.1 reduce-scatter.7
  432.0 42.5 reduce-scatter.9
  494.4 79.3 all-gather.4
  576.1 42.3 reduce-scatter.11
  634.1 76.5 reduce-scatter.13

commit v8 on v7

--- a/solution.py
+++ b/solution.py
@@ -614,6 +614,32 @@
     )(lengths, qkv, qkv, qkv, d_mixed, cos_table, sin_table)
 
 
+def rows_times_body(dims, x_ref, w_ref, out_ref):
+    product = lax.dot_general(x_ref[...], w_ref[...], dims, preferred_element_type=jnp.float32)
+    out_ref[...] = product.astype(out_ref.dtype)
+
+
+def rows_times(x, w, dims, name):
+    slots, depth = x.shape
+    cols = w.shape[0] if dims == NT else w.shape[1]
+    rows = min(256, slots)
+    return pl.pallas_call(
+        functools.partial(rows_times_body, dims),
+        grid=(slots // rows,),
+        in_specs=[
+            pl.BlockSpec((rows, depth), lambda i: (i, 0)),
+            pl.BlockSpec(w.shape, lambda i: (0, 0), pipeline_mode=pl.Buffered(1)),
+        ],
+        out_specs=pl.BlockSpec((rows, cols), lambda i: (i, 0)),
+        out_shape=jax.ShapeDtypeStruct((slots, cols), jnp.bfloat16),
+        compiler_params=pltpu.CompilerParams(vmem_limit_bytes=32 * MIB),
+        cost_estimate=pl.CostEstimate(
+            flops=2 * slots * depth * cols, bytes_accessed=2 * (slots * depth + slots * cols + depth * cols), transcendentals=0
+        ),
+        name=name,
+    )(x, w)
+
+
 def qkv_back_body(d_ref, w_ref, x_ref, out_ref, np_ref):
     total = lax.dot_general(d_ref[0], w_ref[0], NT, preferred_element_type=jnp.float32)
     for j in range(1, 3):
@@ -1131,7 +1157,7 @@
         d_gate_up, [x_a, x_b], eff, 3, "expert_in_grads", 0, 2 * experts
     )
     d_one, in_grads_a = lax.optimization_barrier((d_one, in_grads_a))
-    d_mixed = lax.dot_general(d_one, out_weight, NT, preferred_element_type=jnp.float32).astype(bf)
+    d_mixed = rows_times(d_one, out_weight, NT, "mixed_back")
     d_qkv, d_qkv_t, bias_part = attend_back(lengths, qkv, d_mixed, cos_table, sin_table)
     grad_one, norm_one_part = qkv_back(d_qkv, qkv_w, normed_one)
     grad_one, d_qkv_t, mixed_t, two_b = lax.optimization_barrier(

time: 733 us -> 735 us (level)
    unnamed x89 -> x95, local copies, waits for them, and re-layouts: 49 us -> 53.8 us
  transfers between devices with their start and end apart: 7 -> 7, of which waited for: 2 -> 2; matrix products, arithmetic and copies ran while one was open for 10% -> 9% of each run, Pallas kernels for 47% -> 47%
where the time goes in v8:
time: 735 us; the launch traced here: 725 us
  Pallas kernels  558 us (76%)
  local copies, waits for them, and re-layouts  70.7 us (10%)
  waiting for transfers between devices  44.3 us (6%)
  other arithmetic  30.2 us (4%)
  between operations  15.6 us (2%)
    pallas_call x2, Pallas kernels, ffn(): pl.pallas_call(functools.partial(ffn_body, experts, chunks, scatter, own...  187 us
    pallas_call x2, Pallas kernels, weight_grad_scatter_kernel(): pl.pallas_call(functools.partial(rs_body, count, cut, len(a_list)), grid=...  155 us
    pallas_call x1, Pallas kernels, finish_branch(): pl.pallas_call(branch_body, in_specs=[pl.BlockSpec(memory_space=pltpu.SME...  120 us
    unnamed x95, local copies, waits for them, and re-layouts  53.8 us
    pallas_call x1, Pallas kernels, attention_grads(): pl.pallas_call(functools.partial(attention_grads_body, nc, cut, local_row...  46.5 us
    all_gather x1, waiting for transfers between devices, on_device(): lax.all_gather((unit_one * gain_one).astype(bf), 'tensor', axis=0, tiled=...  39.6 us
    pallas_call x1, Pallas kernels, attend_back(): pl.pallas_call(functools.partial(attend_back_body, rows), grid=(cols // w...  16.4 us
  transfers between devices with their start and end apart: 7, of which 2 were waited for; matrix products, arithmetic and copies ran while one was open for 9% of the time, Pallas kernels for 47%

profile of v8, /device:TPU:0, one launch (start us, length us, event | category | flops | bytes accessed | tf_op | source)
XLA Modules:
  0.0 724.5 jit_solution(12982565070851835452)
XLA Ops:
  10.1 2.5 fusion.3
  13.4 28.9 %copy.32 = bf16[2048,2,1408]{0,2,1:T(8,128)(2,1)} copy(bf16[2048,2,1408]{2,1,0:T(2,128)(2,1)} %param.27) | data formatting | bytes 23068672 | tf_op args[12]
  42.3 10.1 %copy.33 = bf16[4,2,352,2048]{3,2,1,0:T(8,128)(2,1)} copy(bf16[4,2,352,2048]{3,2,0,1:T(8,128)(2,1)} %bitcast.67) | data formatting | bytes 23068672 | tf_op jit(solution)/shard_map/transpose | solution.py:1094
  52.6 1.9 fusion.9
  56.6 39.6 %all-gather.3.cloned.1.call-done.x_ref.b_ref = bf16[1024,2048]{1,0:T(8,128)(2,1)} async-done(((bf16[256,2048]{1,0:T(8,128)(2,1)}), bf16[1024,2048]{1,0:T(8,128)(2,1)}) %all-gather.3.cloned.1.call-update) | async-done | bytes 4194320 | tf_op jit(solution)/shard_map/all_gather | solution.py:1087
  97.1 11.1 %project_qkv.1.q_ref.k_ref.v_ref = bf16[3,1024,512]{2,1,0:T(8,128)(2,1)S(1)} custom-call(bf16[1024,2048]{1,0:T(8,128)(2,1)} %all-gather.3.cloned.1.call-done.x_ref.b_ref, bf16[3,2048,512]{2,1,0:T(8,128)(2,1)} %bitcast.86, bf16[3,1,512]{2,1,0:T(2,128)(2,1)S(1)} %copy.34.bias_ref, f32[1024,128]{1,0:T(8,128)S(1)} %get-tuple-element.64.cos_ref, ...), custom_call_target="tpu_custom_call" | custom-call | flops 6442450944 | bytes 10485760 | tf_op jit(solution)/shard_map/project_qkv/pallas_call | solution.py:478
  108.2 9.4 %attend.1 = (bf16[1024,512]{1,0:T(8,128)(2,1)S(1)}, bf16[512,1024]{1,0:T(8,128)(2,1)S(1)}) custom-call(s32[1]{0:T(128)} %copy.45.length_ref, bf16[3,1024,512]{2,1,0:T(8,128)(2,1)S(1)} %project_qkv.1.q_ref.k_ref.v_ref, bf16[3,1024,512]{2,1,0:T(8,128)(2,1)S(1)} %project_qkv.1.q_ref.k_ref.v_ref, bf16[3,1024,512]{2,1,0:T(8,128)(2,1)S(1)} %project_qkv.1.q_ref.k_ref.v_ref), custom_call_target="tpu_custom_call" | custom-call | flops 2147483648 | bytes 5242880 | tf_op jit(solution)/shard_map/attend/pallas_call | solution.py:522
  117.7 4.4 convolution_convert_fusion
  122.0 119.8 %finish_branch.1 = (f32[256,2048]{1,0:T(8,128)S(1)}, bf16[128,2048]{1,0:T(8,128)(2,1)S(1)}, bf16[512,2048]{1,0:T(8,128)(2,1)}, bf16[512,2048]{1,0:T(8,128)(2,1)}) custom-call(s32[1]{0:T(128)} %copy.45.length_ref, bf16[4,256,2048]{2,1,0:T(8,128)(2,1)} %bitcast.71, bf16[256,2048]{1,0:T(8,128)(2,1)S(1)} %copy-done.3, ...), custom_call_target="tpu_custom_call" | custom-call | bytes 50331648 | tf_op jit(solution)/shard_map/finish_branch/pallas_call | solution.py:875
  244.0 77.2 %ffn.1 = (bf16[12,704,512]{2,1,0:T(8,128)(2,1)}, bf16[512,2048]{1,0:T(8,128)(2,1)}, bf16[512,2048]{1,0:T(8,128)(2,1)}, f32[16,2048]{1,0:T(8,128)}, f32[1,2048]{1...) custom-call(bf16[512,2048]{1,0:T(8,128)(2,1)} %get-tuple-element.69.x_ref.refs_2_, ...), custom_call_target="tpu_custom_call" | custom-call | flops 53150220288 | bytes 103284736 | tf_op jit(solution)/shard_map/ffn/pallas_call | solution.py:435
  322.4 109.6 %ffn_scatter.1 = (bf16[12,704,512]{2,1,0:T(8,128)(2,1)}, bf16[512,2048]{1,0:T(8,128)(2,1)}, bf16[512,2048]{1,0:T(8,128)(2,1)}, f32[16,2048]{1,0:T(8,128)}, f32[1...) custom-call(bf16[512,2048]{1,0:T(8,128)(2,1)} %get-tuple-element.76.x_ref.refs_3_, ...), custom_call_target="tpu_custom_call" | custom-call | flops 53150220288 | bytes 103284736 | tf_op jit(solution)/shard_map/ffn_scatter/pallas_call | solution.py:435
  435.9 54.2 %shared_in_grads.1 = (bf16[2816,256]{1,0:T(8,128)(2,1)S(1)}, bf16[352,256]{1,0:T(8,128)(2,1)}) custom-call(bf16[8448,512]{1,0:T(8,128)(2,1)} %bitcast.90, bf16[8448,512]{1,0:T(8,128)(2,1)} %bitcast.92, bf16[512,2048]{1,0:T(8,128)(2,1)S(1)} %copy-done.10, bf16[512,2048]{1,0:T(8,128)(2,1)S(1)} %copy-done.18), custom_call_target="tpu_custom_call" | custom-call | flops 11811160064 | bytes 12845056 | tf_op jit(solution)/shard_map/shared_in_grads/pallas_call | solution.py:204
  492.0 2.5 multiply_convert_fusion
  498.5 100.7 %expert_in_grads.1 = (bf16[5632,256]{1,0:T(8,128)(2,1)}, bf16[352,256]{1,0:T(8,128)(2,1)}) custom-call(bf16[8448,512]{1,0:T(8,128)(2,1)} %bitcast.91, bf16[8448,512]{1,0:T(8,128)(2,1)} %bitcast.93, bf16[512,2048]{1,0:T(8,128)(2,1)S(1)} %copy-done.11, bf16[512,2048]{1,0:T(8,128)(2,1)S(1)} %copy-done.19), custom_call_target="tpu_custom_call" | custom-call | flops 23622320128 | bytes 21495808 | tf_op jit(solution)/shard_map/expert_in_grads/pallas_call | solution.py:204
  599.3 2.2 copy-done.7
  603.1 3.0 mixed_back.1.dm_ref
  607.1 16.4 %attend_back.1 = (bf16[3,1024,512]{2,1,0:T(8,128)(2,1)}, bf16[3,512,1024]{2,1,0:T(8,128)(2,1)}, f32[3,1,512]{2,1,0:T(1,128)}) custom-call(s32[1]{0:T(128)} %copy.45.length_ref, bf16[3,1024,512]{2,1,0:T(8,128)(2,1)} %copy-done.2, bf16[3,1024,512]{2,1,0:T(8,128)(2,1)} %copy-done.2, bf16[3,1024,512]{2,1,0:T(8,128)(2,1)} %copy-done.2, ...), custom_call_target="tpu_custom_call" | custom-call | flops 5368709120 | bytes 10485760 | tf_op jit(solution)/shard_map/attend_back/pallas_call | solution.py:593
  625.4 10.4 %qkv_back.1 = (bf16[1024,2048]{1,0:T(8,128)(2,1)}, f32[1,2048]{1,0:T(1,128)S(1)}) custom-call(bf16[3,1024,512]{2,1,0:T(8,128)(2,1)S(1)} %copy-done.17, bf16[3,2048,512]{2,1,0:T(8,128)(2,1)} %bitcast.87, bf16[1024,2048]{1,0:T(8,128)(2,1)} %all-gather.3.cloned.1.call-done.x_ref.b_ref), custom_call_target="tpu_custom_call" | custom-call | flops 6442450944 | bytes 14680064 | tf_op jit(solution)/shard_map/qkv_back/pallas_call | solution.py:655
  635.9 2.4 convert_element_type.112
  643.3 5.6 copy.38
  652.1 46.5 %attention_grads.1 = (bf16[1536,256]{1,0:T(8,128)(2,1)S(1)}, bf16[512,256]{1,0:T(8,128)(2,1)S(1)}, f32[12,2048]{1,0:T(8,128)S(1)}) custom-call(bf16[1536,1024]{1,0:T(8,128)(2,1)S(1)} %bitcast.66, bf16[512,1024]{1,0:T(8,128)(2,1)S(1)} %copy-done.13, bf16[1024,2048]{1,0:T(8,128)(2,1)} %all-gather.3.cloned.1.call-done.x_ref.b_ref, ...), custom_call_target="tpu_custom_call" | custom-call | flops 8589934592 | bytes 12582912 | tf_op jit(solution)/shard_map/attention_grads/pallas_call | solution.py:1033
  701.5 5.1 convert_bitcast_fusion
  709.1 3.4 reduce-scatter.14.cloned.1.call-done
  714.3 3.1 fusion.7
  (149 shorter events, 38.9 us)
Async XLA Ops:
  7.2 6.1 copy-start.45
  7.2 6.2 copy-start.44
  7.2 6.2 copy-start.39
  7.2 6.2 copy-start.40
  7.2 89.0 %all-gather.3.cloned.1.call-start = ((), (), s32[]{:S(2)}) async-start(), calls=%async_computation.5 | async-start | bytes 5242880 | tf_op jit(solution)/shard_map/all_gather | solution.py:1087
  12.6 419.5 %reduce-scatter.6.cloned.1.call-start = ((), (), s32[]{:S(2)}) async-start(), calls=%async_computation.6 | async-start | bytes 2621440 | tf_op jit(solution)/shard_map/reduce_scatter | solution.py:1128
  52.5 439.5 %copy-start.37 = (f32[256]{0:T(256)}, f32[256]{0:T(256)S(1)}, u32[]{:S(2)}) copy-start(f32[256]{0:T(256)S(1)} %compare_convert_fusion) | copy-start | bytes 3076
  54.8 53.4 %copy-start.5 = (f32[1024,128]{1,0:T(8,128)}, f32[1024,128]{1,0:T(8,128)S(1)}, u32[]{:S(2)}) copy-start(f32[1024,128]{1,0:T(8,128)S(1)} %get-tuple-element.64.cos_ref) | copy-start | bytes 1572868
  54.9 53.4 %copy-start.6 = (f32[1024,128]{1,0:T(8,128)}, f32[1024,128]{1,0:T(8,128)S(1)}, u32[]{:S(2)}) copy-start(f32[1024,128]{1,0:T(8,128)S(1)} %get-tuple-element.65.sin_ref) | copy-start | bytes 1572868
  108.2 9.4 %copy-start.2 = (bf16[3,1024,512]{2,1,0:T(8,128)(2,1)}, bf16[3,1024,512]{2,1,0:T(8,128)(2,1)S(1)}, u32[]{:S(2)}) copy-start(bf16[3,1024,512]{2,1,0:T(8,128)(2,1)S(1)} %project_qkv.1.q_ref.k_ref.v_ref) | copy-start | bytes 9437188
  108.2 9.4 %copy-start.8 = (bf16[512,2048]{1,0:T(8,128)(2,1)S(1)}, bf16[512,2048]{1,0:T(8,128)(2,1)}, u32[]{:S(2)}) copy-start(bf16[512,2048]{1,0:T(8,128)(2,1)} %w_ref.1) | copy-start | bytes 6291460
  321.2 110.9 %reduce-scatter.8.cloned.1.call-start = ((), (), s32[]{:S(2)}) async-start(), calls=%async_computation.7 | async-start | bytes 2621440 | tf_op jit(solution)/shard_map/reduce_scatter | solution.py:1129
  322.0 168.2 %reduce-scatter.10.cloned.1.call-start = ((), (), s32[]{:S(2)}) async-start(), calls=%async_computation.8 | async-start | bytes 2621440 | tf_op jit(solution)/shard_map/reduce_scatter | solution.py:1144
  432.1 167.2 %all-gather.5.cloned.1.call-start = ((), (), s32[]{:S(2)}) async-start(), calls=%async_computation.9 | async-start | bytes 5242880 | tf_op jit(solution)/shard_map/all_gather | solution.py:1154
  494.5 141.3 %reduce-scatter.12.cloned.1.call-start = ((), (), s32[]{:S(2)}) async-start(), calls=%async_computation.10 | async-start | bytes 2621440 | tf_op jit(solution)/shard_map/reduce_scatter | solution.py:1145
  495.1 217.4 %reduce-scatter.14.cloned.1.call-start = ((), (), s32[]{:S(2)}) async-start(), calls=%async_computation.11 | async-start | bytes 5242880 | tf_op jit(solution)/shard_map/reduce_scatter | solution.py:1166
  643.3 5.6 copy-start.30
  643.3 5.6 copy-start.28
  643.3 5.6 copy-start.34
  643.3 5.7 copy-start.43
  701.5 6.3 copy-start.26
  701.5 6.3 copy-start.27
  701.5 6.3 copy-start.38
  709.1 5.2 copy-start.20
  (29 other events, 63.2 us)
Sparse Core Ops, SparseCore 0:
  12.7 83.4 all-gather.2
  321.4 43.6 reduce-scatter.5
  367.4 43.1 reduce-scatter.7
  432.3 42.5 reduce-scatter.9
  494.6 79.3 all-gather.4
  576.3 42.3 reduce-scatter.11
  636.0 76.5 reduce-scatter.13

commit v9 on v8

--- a/solution.py
+++ b/solution.py
@@ -632,7 +632,7 @@
         ],
         out_specs=pl.BlockSpec((rows, cols), lambda i: (i, 0)),
         out_shape=jax.ShapeDtypeStruct((slots, cols), jnp.bfloat16),
-        compiler_params=pltpu.CompilerParams(vmem_limit_bytes=32 * MIB),
+        compiler_params=pltpu.CompilerParams(vmem_limit_bytes=62 * MIB),
         cost_estimate=pl.CostEstimate(
             flops=2 * slots * depth * cols, bytes_accessed=2 * (slots * depth + slots * cols + depth * cols), transcendentals=0
         ),

time: 735 us -> 732 us (level)
    unnamed x95 -> x83, local copies, waits for them, and re-layouts: 53.8 us -> 46.9 us
  transfers between devices with their start and end apart: 7 -> 7, of which waited for: 2 -> 2; matrix products, arithmetic and copies ran while one was open for 9% -> 9% of each run, Pallas kernels for 47% -> 48%
where the time goes in v9:
time: 732 us; the launch traced here: 722 us
  Pallas kernels  562 us (77%)
  local copies, waits for them, and re-layouts  63.8 us (9%)
  waiting for transfers between devices  46.6 us (6%)
  other arithmetic  29 us (4%)
  between operations  15.6 us (2%)
    pallas_call x2, Pallas kernels, ffn(): pl.pallas_call(functools.partial(ffn_body, experts, chunks, scatter, own...  187 us
    pallas_call x2, Pallas kernels, weight_grad_scatter_kernel(): pl.pallas_call(functools.partial(rs_body, count, cut, len(a_list)), grid=...  155 us
    pallas_call x1, Pallas kernels, finish_branch(): pl.pallas_call(branch_body, in_specs=[pl.BlockSpec(memory_space=pltpu.SME...  120 us
    unnamed x83, local copies, waits for them, and re-layouts  46.9 us
    pallas_call x1, Pallas kernels, attention_grads(): pl.pallas_call(functools.partial(attention_grads_body, nc, cut, local_row...  46.8 us
    all_gather x1, waiting for transfers between devices, on_device(): lax.all_gather((unit_one * gain_one).astype(bf), 'tensor', axis=0, tiled=...  39.7 us
    pallas_call x1, Pallas kernels, attend_back(): pl.pallas_call(functools.partial(attend_back_body, rows), grid=(cols // w...  16.4 us
  transfers between devices with their start and end apart: 7, of which 2 were waited for; matrix products, arithmetic and copies ran while one was open for 9% of the time, Pallas kernels for 48%

profile of v9, /device:TPU:0, one launch (start us, length us, event | category | flops | bytes accessed | tf_op | source)
XLA Modules:
  0.0 722.4 jit_solution(4926725563253358487)
XLA Ops:
  10.1 2.5 fusion.3
  13.4 28.8 %copy.32 = bf16[2048,2,1408]{0,2,1:T(8,128)(2,1)} copy(bf16[2048,2,1408]{2,1,0:T(2,128)(2,1)} %param.27) | data formatting | bytes 23068672 | tf_op args[12]
  42.3 10.1 %copy.33 = bf16[4,2,352,2048]{3,2,1,0:T(8,128)(2,1)} copy(bf16[4,2,352,2048]{3,2,0,1:T(8,128)(2,1)} %bitcast.67) | data formatting | bytes 23068672 | tf_op jit(solution)/shard_map/transpose | solution.py:1094
  52.5 1.9 fusion.9
  56.6 39.7 %all-gather.3.cloned.1.call-done.x_ref.b_ref = bf16[1024,2048]{1,0:T(8,128)(2,1)} async-done(((bf16[256,2048]{1,0:T(8,128)(2,1)}), bf16[1024,2048]{1,0:T(8,128)(2,1)}) %all-gather.3.cloned.1.call-update) | async-done | bytes 4194320 | tf_op jit(solution)/shard_map/all_gather | solution.py:1087
  97.1 11.1 %project_qkv.1.q_ref.k_ref.v_ref = bf16[3,1024,512]{2,1,0:T(8,128)(2,1)S(1)} custom-call(bf16[1024,2048]{1,0:T(8,128)(2,1)} %all-gather.3.cloned.1.call-done.x_ref.b_ref, bf16[3,2048,512]{2,1,0:T(8,128)(2,1)} %bitcast.86, bf16[3,1,512]{2,1,0:T(2,128)(2,1)S(1)} %copy.34.bias_ref, f32[1024,128]{1,0:T(8,128)S(1)} %get-tuple-element.64.cos_ref, ...), custom_call_target="tpu_custom_call" | custom-call | flops 6442450944 | bytes 10485760 | tf_op jit(solution)/shard_map/project_qkv/pallas_call | solution.py:478
  108.2 9.4 %attend.1 = (bf16[1024,512]{1,0:T(8,128)(2,1)S(1)}, bf16[512,1024]{1,0:T(8,128)(2,1)S(1)}) custom-call(s32[1]{0:T(128)} %copy.45.length_ref, bf16[3,1024,512]{2,1,0:T(8,128)(2,1)S(1)} %project_qkv.1.q_ref.k_ref.v_ref, bf16[3,1024,512]{2,1,0:T(8,128)(2,1)S(1)} %project_qkv.1.q_ref.k_ref.v_ref, bf16[3,1024,512]{2,1,0:T(8,128)(2,1)S(1)} %project_qkv.1.q_ref.k_ref.v_ref), custom_call_target="tpu_custom_call" | custom-call | flops 2147483648 | bytes 5242880 | tf_op jit(solution)/shard_map/attend/pallas_call | solution.py:522
  117.7 4.4 convolution_convert_fusion
  122.0 119.9 %finish_branch.1 = (f32[256,2048]{1,0:T(8,128)S(1)}, bf16[128,2048]{1,0:T(8,128)(2,1)S(1)}, bf16[512,2048]{1,0:T(8,128)(2,1)}, bf16[512,2048]{1,0:T(8,128)(2,1)}) custom-call(s32[1]{0:T(128)} %copy.45.length_ref, bf16[4,256,2048]{2,1,0:T(8,128)(2,1)} %bitcast.71, bf16[256,2048]{1,0:T(8,128)(2,1)S(1)} %copy-done.4, ...), custom_call_target="tpu_custom_call" | custom-call | bytes 50331648 | tf_op jit(solution)/shard_map/finish_branch/pallas_call | solution.py:875
  244.0 77.3 %ffn.1 = (bf16[12,704,512]{2,1,0:T(8,128)(2,1)}, bf16[512,2048]{1,0:T(8,128)(2,1)}, bf16[512,2048]{1,0:T(8,128)(2,1)}, f32[16,2048]{1,0:T(8,128)}, f32[1,2048]{1...) custom-call(bf16[512,2048]{1,0:T(8,128)(2,1)} %get-tuple-element.69.x_ref.refs_2_, ...), custom_call_target="tpu_custom_call" | custom-call | flops 53150220288 | bytes 103284736 | tf_op jit(solution)/shard_map/ffn/pallas_call | solution.py:435
  322.6 109.6 %ffn_scatter.1 = (bf16[12,704,512]{2,1,0:T(8,128)(2,1)}, bf16[512,2048]{1,0:T(8,128)(2,1)}, bf16[512,2048]{1,0:T(8,128)(2,1)}, f32[16,2048]{1,0:T(8,128)}, f32[1...) custom-call(bf16[512,2048]{1,0:T(8,128)(2,1)} %get-tuple-element.76.x_ref.refs_3_, ...), custom_call_target="tpu_custom_call" | custom-call | flops 53150220288 | bytes 103284736 | tf_op jit(solution)/shard_map/ffn_scatter/pallas_call | solution.py:435
  436.0 54.2 %shared_in_grads.1 = (bf16[2816,256]{1,0:T(8,128)(2,1)S(1)}, bf16[352,256]{1,0:T(8,128)(2,1)}) custom-call(bf16[8448,512]{1,0:T(8,128)(2,1)} %bitcast.90, bf16[8448,512]{1,0:T(8,128)(2,1)} %bitcast.92, bf16[512,2048]{1,0:T(8,128)(2,1)S(1)} %copy-done.8, bf16[512,2048]{1,0:T(8,128)(2,1)S(1)} %copy-done.15), custom_call_target="tpu_custom_call" | custom-call | flops 11811160064 | bytes 12845056 | tf_op jit(solution)/shard_map/shared_in_grads/pallas_call | solution.py:204
  492.1 2.4 multiply_convert_fusion
  497.8 100.8 %expert_in_grads.1 = (bf16[5632,256]{1,0:T(8,128)(2,1)}, bf16[352,256]{1,0:T(8,128)(2,1)}) custom-call(bf16[8448,512]{1,0:T(8,128)(2,1)} %bitcast.91, bf16[8448,512]{1,0:T(8,128)(2,1)} %bitcast.93, bf16[512,2048]{1,0:T(8,128)(2,1)S(1)} %copy-done.9, bf16[512,2048]{1,0:T(8,128)(2,1)S(1)} %copy-done.16), custom_call_target="tpu_custom_call" | custom-call | flops 23622320128 | bytes 21495808 | tf_op jit(solution)/shard_map/expert_in_grads/pallas_call | solution.py:204
  598.6 6.3 mixed_back.1.dm_ref
  604.9 16.4 %attend_back.1 = (bf16[3,1024,512]{2,1,0:T(8,128)(2,1)}, bf16[3,512,1024]{2,1,0:T(8,128)(2,1)}, f32[3,1,512]{2,1,0:T(1,128)}) custom-call(s32[1]{0:T(128)} %copy.45.length_ref, bf16[3,1024,512]{2,1,0:T(8,128)(2,1)} %copy-done.3, bf16[3,1024,512]{2,1,0:T(8,128)(2,1)} %copy-done.3, bf16[3,1024,512]{2,1,0:T(8,128)(2,1)} %copy-done.3, ...), custom_call_target="tpu_custom_call" | custom-call | flops 5368709120 | bytes 10485760 | tf_op jit(solution)/shard_map/attend_back/pallas_call | solution.py:593
  621.3 1.9 copy-done.14
  623.2 10.4 %qkv_back.1 = (bf16[1024,2048]{1,0:T(8,128)(2,1)}, f32[1,2048]{1,0:T(1,128)S(1)}) custom-call(bf16[3,1024,512]{2,1,0:T(8,128)(2,1)S(1)} %copy-done.14, bf16[3,2048,512]{2,1,0:T(8,128)(2,1)} %bitcast.87, bf16[1024,2048]{1,0:T(8,128)(2,1)} %all-gather.3.cloned.1.call-done.x_ref.b_ref), custom_call_target="tpu_custom_call" | custom-call | flops 6442450944 | bytes 14680064 | tf_op jit(solution)/shard_map/qkv_back/pallas_call | solution.py:655
  633.7 2.4 convert_element_type.112
  639.9 5.6 copy.38
  647.5 46.8 %attention_grads.1 = (bf16[1536,256]{1,0:T(8,128)(2,1)S(1)}, bf16[512,256]{1,0:T(8,128)(2,1)S(1)}, f32[12,2048]{1,0:T(8,128)S(1)}) custom-call(bf16[1536,1024]{1,0:T(8,128)(2,1)S(1)} %bitcast.66, bf16[512,1024]{1,0:T(8,128)(2,1)S(1)} %copy-done.11, bf16[1024,2048]{1,0:T(8,128)(2,1)} %all-gather.3.cloned.1.call-done.x_ref.b_ref, ...), custom_call_target="tpu_custom_call" | custom-call | flops 8589934592 | bytes 12582912 | tf_op jit(solution)/shard_map/attention_grads/pallas_call | solution.py:1033
  697.2 5.1 convert_bitcast_fusion
  704.9 5.5 reduce-scatter.14.cloned.1.call-done
  712.2 3.1 fusion.7
  (137 shorter events, 31.0 us)
Async XLA Ops:
  7.2 6.1 copy-start.38
  7.2 6.2 copy-start.37
  7.2 6.2 copy-start.32
  7.2 6.2 copy-start.33
  7.2 89.0 %all-gather.3.cloned.1.call-start = ((), (), s32[]{:S(2)}) async-start(), calls=%async_computation.5 | async-start | bytes 5242880 | tf_op jit(solution)/shard_map/all_gather | solution.py:1087
  12.6 419.6 %reduce-scatter.6.cloned.1.call-start = ((), (), s32[]{:S(2)}) async-start(), calls=%async_computation.6 | async-start | bytes 2621440 | tf_op jit(solution)/shard_map/reduce_scatter | solution.py:1128
  54.8 53.4 %copy-start.6 = (f32[1024,128]{1,0:T(8,128)}, f32[1024,128]{1,0:T(8,128)S(1)}, u32[]{:S(2)}) copy-start(f32[1024,128]{1,0:T(8,128)S(1)} %get-tuple-element.64.cos_ref) | copy-start | bytes 1572868
  54.8 53.4 %copy-start.7 = (f32[1024,128]{1,0:T(8,128)}, f32[1024,128]{1,0:T(8,128)S(1)}, u32[]{:S(2)}) copy-start(f32[1024,128]{1,0:T(8,128)S(1)} %get-tuple-element.65.sin_ref) | copy-start | bytes 1572868
  108.2 9.4 %copy-start.3 = (bf16[3,1024,512]{2,1,0:T(8,128)(2,1)}, bf16[3,1024,512]{2,1,0:T(8,128)(2,1)S(1)}, u32[]{:S(2)}) copy-start(bf16[3,1024,512]{2,1,0:T(8,128)(2,1)S(1)} %project_qkv.1.q_ref.k_ref.v_ref) | copy-start | bytes 9437188
  108.2 9.4 %copy-start.39 = (bf16[512,2048]{1,0:T(8,128)(2,1)S(1)}, bf16[512,2048]{1,0:T(8,128)(2,1)}, u32[]{:S(2)}) copy-start(bf16[512,2048]{1,0:T(8,128)(2,1)} %w_ref.1) | copy-start | bytes 6291460
  321.4 110.9 %reduce-scatter.8.cloned.1.call-start = ((), (), s32[]{:S(2)}) async-start(), calls=%async_computation.7 | async-start | bytes 2621440 | tf_op jit(solution)/shard_map/reduce_scatter | solution.py:1129
  322.1 168.2 %reduce-scatter.10.cloned.1.call-start = ((), (), s32[]{:S(2)}) async-start(), calls=%async_computation.8 | async-start | bytes 2621440 | tf_op jit(solution)/shard_map/reduce_scatter | solution.py:1144
  432.3 166.3 %all-gather.5.cloned.1.call-start = ((), (), s32[]{:S(2)}) async-start(), calls=%async_computation.9 | async-start | bytes 5242880 | tf_op jit(solution)/shard_map/all_gather | solution.py:1154
  494.6 139.0 %reduce-scatter.12.cloned.1.call-start = ((), (), s32[]{:S(2)}) async-start(), calls=%async_computation.10 | async-start | bytes 2621440 | tf_op jit(solution)/shard_map/reduce_scatter | solution.py:1145
  495.2 215.2 %reduce-scatter.14.cloned.1.call-start = ((), (), s32[]{:S(2)}) async-start(), calls=%async_computation.11 | async-start | bytes 5242880 | tf_op jit(solution)/shard_map/reduce_scatter | solution.py:1166
  639.9 5.6 copy-start.26
  639.9 5.7 copy-start.36
  639.9 5.7 copy-start.11
  697.2 6.4 copy-start.2
  697.2 6.4 copy-start.23
  697.2 6.4 copy-start.24
  703.6 6.8 copy-start.5
  703.6 6.8 copy-start.31
  704.9 7.3 %copy-start.17 = (f32[256,2048]{1,0:T(8,128)S(1)}, f32[256,2048]{1,0:T(8,128)}, u32[]{:S(2)}) copy-start(f32[256,2048]{1,0:T(8,128)} %get-tuple-element.127) | copy-start | bytes 6291460
  (23 other events, 46.6 us)
Sparse Core Ops, SparseCore 0:
  12.7 83.4 all-gather.2
  321.5 43.7 reduce-scatter.5
  367.7 43.1 reduce-scatter.7
  432.4 42.6 reduce-scatter.9
  494.7 79.5 all-gather.4
  576.5 42.3 reduce-scatter.11
  633.8 76.6 reduce-scatter.13
